TPU v7x, 128 devices: a whole 4x4x4 slice. The times are simulated.
128 devices in a mesh: dp: 32 (over x_hi, y, z), pipe: 4 (over x_lo, core).
Axes of the slice: x: 4 (x_hi: 2, x_lo: 2; x = x_hi * 2 + x_lo), y: 4, z: 4, core: 2. Of those that a mesh axis runs over, the one named last changes fastest.
Arguments:
- inputs: bfloat16 [16, 256, 1024], P(None, 'dp'), may hold values from -6 to 6
- input_weight: bfloat16 [4, 1024, 4096], P('pipe'), may hold values from -0.1875 to 0.1875
- recurrent_weight: bfloat16 [4, 1024, 4096], P('pipe'), may hold values from -0.1875 to 0.1875
- gate_bias: float32 [4, 4096], P('pipe'), may hold values from -4 to 4
- lengths: int32 [256], P('dp'), may hold values from 1 to 16
- cotangent: bfloat16 [4, 16, 256, 1024], P('pipe', None, 'dp'), may hold values from -6 to 6
Outputs:
- grad_input: float32 [4, 1024, 4096], P('pipe', 'dp')
- grad_recurrent: float32 [4, 1024, 4096], P('pipe', 'dp')
- grad_bias: float32 [4, 4096], P('pipe', 'dp')
- final_hidden: bfloat16 [4, 256, 1024], P('pipe', 'dp')
- final_cell: float32 [4, 256, 1024], P('pipe', 'dp')
All inputs are finite; a program needn't handle non-finite values.
Results may differ from a plain program's by a relative error of at most 0.004.
Values may be sent and summed in bfloat16 or wider, within the bound.
No kernel may reach another device: no remote copies, remote signals or barrier semaphores. Data moves between devices by JAX's collectives and lax.ppermute only.
A program may use at most 128 MiB of HBM per device.

v0:
```python
from functools import partial

import jax
import jax.numpy as jnp
from jax import lax
from jax.experimental import pallas as pl
from jax.experimental.pallas import tpu as pltpu
from jax.sharding import Mesh, PartitionSpec as P

BLOCK = 4
LAG = 2
WIDE = 1024
COLS = 512
FORWARD_STEPS = 2
CHUNK = 256
PANEL = 256
SLOTS = 4
EXTRA = 16
DP = ("xh", "y", "z")
VMEM = pl.BlockSpec(memory_space=pltpu.VMEM)
SMEM = pl.BlockSpec(memory_space=pltpu.SMEM)
HBM = pl.BlockSpec(memory_space=pltpu.HBM)
LIMIT = 8 * 2**20


def squash(value):
    return 0.5 * jnp.tanh(0.5 * value) + 0.5


def dot(a, b):
    return jnp.dot(a, b, preferred_element_type=jnp.float32)


def shifted(at, by):
    return at + by if isinstance(at, int) else pl.multiple_of(at + by, CHUNK)


def over_columns(column, width, steps):
    run = width // steps

    def body(step, carry):
        for j in range(0, run, CHUNK):
            column(j if steps == 1 else pl.multiple_of(step * run + j, CHUNK))
        return carry

    if steps == 1:
        body(0, 0)
    else:
        lax.fori_loop(0, steps, body, 0)


def turn(share, shares, pairs, stage, sems):
    panels = pairs[0][1].shape[0] // PANEL
    groups = panels // SLOTS
    low = share * 2 * groups // shares
    high = (share + 1) * 2 * groups // shares

    for n, (source, target) in enumerate(pairs):

        def copy(at, slot, target=target):
            at = pl.multiple_of(at * PANEL, PANEL)
            return pltpu.make_async_copy(stage.at[slot], target.at[pl.ds(at, PANEL)], sems.at[slot])

        def body(group, carry, source=source, copy=copy):
            def move(slot, carry):
                at = group * SLOTS + slot
                stage[slot] = source[:, pl.ds(pl.multiple_of(at * PANEL, PANEL), PANEL)].T
                copy(at, slot).start()
                return carry

            def settle(slot, carry):
                copy(group * SLOTS + slot, slot).wait()
                return carry

            lax.fori_loop(0, SLOTS, move, 0)
            lax.fori_loop(0, SLOTS, settle, 0)
            return carry

        begin, end = (jnp.clip(v - n * groups, 0, groups) for v in (low, high))
        lax.fori_loop(begin, end, body, 0)


def forward_kernel(place, own, bias, lens, *rest, tick, stages):
    if tick == 0:
        (wi_in, wr_in), rest = rest[:2], rest[2:]
    else:
        arrived, rest = rest[0], rest[9:]
    emitted, wi, wr, xs, gates, cells, hs, wit_far, wrt_far = rest[:9]
    proj, staged, sems, load_sems = rest[-4:]
    span, rows, width = emitted.shape
    stage = place[0]
    blocks = own.shape[0] // span
    at = tick - LAG * stage
    active = (at >= 0) & (at < blocks)
    fs = at * span
    idle = LAG * (stages - 1)
    last = tick == blocks + idle - 1
    pairs = ((wr, wrt_far), (wi, wit_far))
    if tick == 0:
        load_wi = pltpu.make_async_copy(wi_in, wi, load_sems.at[0])
        load_wr = pltpu.make_async_copy(wr_in, wr, load_sems.at[1])
        load_wi.start()
        load_wr.start()
        load_wi.wait()

    @pl.when(active)
    def _():
        if tick == 0:
            xs[pl.ds(fs, span)] = own[pl.ds(fs, span)]
        else:

            @pl.when(stage == 0)
            def _():
                xs[pl.ds(fs, span)] = own[pl.ds(fs, span)]

            @pl.when(stage > 0)
            def _():
                xs[pl.ds(fs, span)] = arrived[...]

        x = xs[pl.ds(fs, span)].reshape(span * rows, width)

        def project(n, carry):
            cols = pl.ds(pl.multiple_of(n * WIDE, WIDE), WIDE)
            proj[:, :, cols] = (dot(x, wi[:, cols]) + bias[:, cols]).reshape(span, rows, WIDE)
            return carry

        lax.fori_loop(0, 4 * width // WIDE, project, 0)

    if tick == 0:
        load_wr.wait()

    turns = (0, 1, idle + blocks - 2, idle + blocks - 1)
    if tick in turns:
        late = turns.index(tick) // 2

        @pl.when((stage < stages // 2) == (late == 1))
        def _():
            turn(turns.index(tick) % 2, 2, pairs, staged, sems)

    if last:
        load = pltpu.make_async_copy(wrt_far, rest[9], load_sems.at[0])
        load.start()

    @pl.when(active)
    def _():
        @pl.when(fs == 0)
        def _():
            hs[0] = jnp.zeros((rows, width), jnp.bfloat16)
            cells[0] = jnp.zeros((rows, width), jnp.float32)

        def frame(t, carry):
            fr = fs + t
            h = hs[fr]

            def column(j):
                part = pl.ds(j, CHUNK)

                def pre(gate):
                    col = pl.ds(shifted(j, gate * width), CHUNK)
                    return proj[t, :, col] + dot(h, wr[:, col])

                alive = fr < lens[:, part]
                i, f, g, o = squash(pre(0)), squash(pre(1)), jnp.tanh(pre(2)), squash(pre(3))
                c = cells[fr, :, part]
                new_c = f * c + i * g
                new_h = (o * jnp.tanh(new_c)).astype(jnp.bfloat16)
                old_h = hs[fr, :, part]
                for gate, value in enumerate((i, f, g, o)):
                    gates[fr, :, pl.ds(shifted(j, gate * width), CHUNK)] = value
                cells[fr + 1, :, part] = jnp.where(alive, new_c, c)
                hs[fr + 1, :, part] = jnp.where(alive, new_h, old_h)
                emitted[t, :, part] = jnp.where(alive, new_h, jnp.zeros_like(new_h))

            over_columns(column, width, FORWARD_STEPS)
            return carry

        lax.fori_loop(0, span, frame, 0)

    if last:
        load.wait()


def block_at(tick, stage, stages, blocks):
    offset = tick - LAG * (stages - 1 - stage)
    return blocks - 1 - offset, (offset >= 0) & (offset < blocks)


def backward_kernel(place, cot, arrived, lens, *rest, tick, stages):
    if tick == 0:
        wit_far, gates_in, cells_in, wrt_in, lower, dy, dz, gates, cells, wit, wrt, dh, dc, sem = rest
        load = pltpu.make_async_copy(wit_far, wit, sem.at[0])
        load.start()
    else:
        lower, dy, dz, gates, cells, wit, wrt, dh, dc = rest[8:]
    span, rows, width = arrived.shape
    total = gates.shape[0]
    half = 2 * width
    stage = place[0]
    blocks = total // span
    at, active = block_at(tick, stage, stages, blocks)
    fs = at * span

    @pl.when(active)
    def _():
        @pl.when(fs + span == total)
        def _():
            dh[...] = jnp.zeros((rows, width), jnp.float32)
            dc[...] = jnp.zeros((rows, width), jnp.float32)

        def frame(n, carry):
            t = span - 1 - n
            fr = fs + t
            acc = None
            for j in range(0, width, CHUNK):
                part = pl.ds(j, CHUNK)
                alive = fr < lens[:, part]
                i = gates[fr, :, pl.ds(j, CHUNK)]
                f = gates[fr, :, pl.ds(width + j, CHUNK)]
                g = gates[fr, :, pl.ds(2 * width + j, CHUNK)]
                o = gates[fr, :, pl.ds(3 * width + j, CHUNK)]
                u = jnp.where(stage == stages - 1, 0.0, arrived[t, :, part].astype(jnp.float32))
                e = jnp.where(alive, dh[:, part] + u + cot[fr, :, part].astype(jnp.float32), 0.0)
                k = jnp.tanh(cells[fr + 1, :, part])
                old_dc = dc[:, part]
                dcell = jnp.where(alive, old_dc, 0.0) + e * o * (1.0 - k * k)
                parts = (
                    dcell * g * i * (1.0 - i),
                    dcell * cells[fr, :, part] * f * (1.0 - f),
                    dcell * i * (1.0 - g * g),
                    e * k * o * (1.0 - o),
                )
                dc[:, part] = jnp.where(alive, 0.0, old_dc) + dcell * f
                dh[:, part] = jnp.where(alive, 0.0, dh[:, part])
                for gate, value in enumerate(parts):
                    col = pl.ds(gate * width + j, CHUNK)
                    d = value.astype(jnp.bfloat16)
                    if gate < 2:
                        dy[fr, :, col] = d
                    else:
                        dz[fr, :, pl.ds(gate * width + j - half, CHUNK)] = d
                    term = dot(d, wrt[col, :])
                    acc = term if acc is None else acc + term
            dh[...] = dh[...] + acc
            return carry

        lax.fori_loop(0, span, frame, 0)

    if tick == 0:
        load.wait()
    if tick < blocks + LAG * (stages - 1) - 1:

        @pl.when(active & (stage > 0))
        def _():
            left, right = (v[pl.ds(fs, span)].reshape(span * rows, half) for v in (dy, dz))

            def descend(n, carry):
                cols = pl.ds(pl.multiple_of(n * CHUNK, CHUNK), CHUNK)
                u = dot(left, wit[pl.ds(0, half), cols]) + dot(right, wit[pl.ds(half, half), cols])
                lower[:, :, cols] = u.astype(jnp.bfloat16).reshape(span, rows, CHUNK)
                return carry

            lax.fori_loop(0, width // CHUNK, descend, 0)


def prepare_kernel(place, xs, hs, *rest):
    to_y, to_z, whole = rest[:4], rest[4:8], rest[8]
    total, rows, width = xs.shape
    y, z = place[1], place[2]
    for n, source in enumerate((xs, hs)):
        flat = source[pl.ds(0, total)].reshape(total * rows, width)
        whole[pl.ds(2 * n, 2)] = flat.T.reshape((2,) + whole.shape[1:])
    for d in range(4):
        for g in range(4):
            to_y[d][g] = whole[g, lax.rem(y + d, 4)]
            for i in range(4):
                to_z[d][g, i] = whole[g, i, lax.rem(z + d, 4)]


def as_rows(value):
    high = value.astype(jnp.bfloat16)
    rest = value - high.astype(jnp.float32)
    middle = rest.astype(jnp.bfloat16)
    low = (rest - middle.astype(jnp.float32)).astype(jnp.bfloat16)
    at = lax.broadcasted_iota(jnp.int32, (EXTRA, value.shape[1]), 0)
    out = jnp.zeros(at.shape, jnp.float32)
    for n, part in enumerate((high, middle, low)):
        out = jnp.where(at == n, part.astype(jnp.float32), out)
    return out.astype(jnp.bfloat16)


def from_rows(block):
    return jnp.sum(block.astype(jnp.float32), axis=0, keepdims=True)


def combine_kernel(place, *rest):
    lefts = (rest[:4], rest[4:8])
    dy, dz = rest[8:10]
    arrivals = (rest[10:13], rest[13:16])
    own_y, own_z, bias, *sends = rest[16:-2]
    left_all, right = rest[-2:]
    y, z = place[1], place[2]
    total, rows, half = dy.shape
    n = total * rows
    fine = left_all.shape[2]
    ones = jnp.ones((EXTRA, 4 * n), jnp.bfloat16)
    for side, (mine, other, own) in enumerate(((dy, z, own_y), (dz, y, own_z))):
        for d in range(4):
            block = mine if d == 0 else arrivals[side][d - 1]
            right[pl.ds(d * n, n)] = block[...].reshape(n, half)
            for g in range(4):
                left_all[g, :, :, pl.ds(d * n, n)] = lefts[side][d][g]

        def columns(step, carry, side=side, other=other, own=own):
            at = pl.multiple_of(step * COLS, COLS)
            cols = pl.ds(at, COLS)
            block = right[:, cols]
            sums = dot(ones, block)[:1]
            bias[:, pl.ds(pl.multiple_of(at + side * half, COLS), COLS)] = sums
            extra = as_rows(sums)
            for d in range(4):
                left = left_all[:, lax.rem(other + d, 4)].reshape(4 * fine, 4 * n)
                part = dot(left, block)
                if d == 0:
                    own[:, :, cols] = part.reshape(4, fine, COLS)
                else:
                    to = sends[3 * side + d - 1]
                    to[pl.ds(0, 4 * fine), cols] = part.astype(jnp.bfloat16)
                    to[pl.ds(4 * fine, EXTRA), cols] = extra
            return carry

        lax.fori_loop(0, half // COLS, columns, 0)


def finish_kernel(place, own_y, own_z, bias, *rest):
    arrivals, keep, kept_bias, give = rest[:6], rest[6], rest[7], rest[8]
    xh = place[3]
    fine, half = own_y.shape[1:]
    for side, own in enumerate((own_y, own_z)):
        cols = pl.ds(side * half, half)
        blocks = arrivals[3 * side : 3 * side + 3]
        for n in range(2):
            mine, other = 2 * n + xh, 2 * n + 1 - xh
            kept, given = own[mine], own[other]
            for block in blocks:
                kept += block[pl.ds(pl.multiple_of(mine * fine, fine), fine)].astype(jnp.float32)
                given += block[pl.ds(pl.multiple_of(other * fine, fine), fine)].astype(jnp.float32)
            keep[n, :, cols] = kept
            give[pl.ds(n * fine, fine), cols] = given.astype(jnp.bfloat16)
        total = bias[:, cols]
        for block in blocks:
            total += from_rows(block[pl.ds(4 * fine, EXTRA)])
        kept_bias[:, cols] = total
        give[pl.ds(2 * fine, EXTRA), cols] = as_rows(total)


def last_kernel(place, keep, bias, arrived, grad_i, grad_r, grad_b):
    fine = keep.shape[1]
    for n, out in enumerate((grad_i, grad_r)):
        out[...] = keep[n] + arrived[pl.ds(n * fine, fine)].astype(jnp.float32)
    width = grad_b.shape[1]
    cols = pl.ds(pl.multiple_of(((place[3] * 4 + place[1]) * 4 + place[2]) * width, width), width)
    grad_b[...] = bias[:, cols] + from_rows(arrived[pl.ds(2 * fine, EXTRA), cols])


def shape(dims, kind):
    return pltpu.VMEM(dims, kind)


def near(array):
    return pltpu.with_memory_space_constraint(array, pltpu.VMEM)


def local(inputs, input_weight, recurrent_weight, gate_bias, lengths, cotangent):
    total, rows, width = inputs.shape
    gated = 4 * width
    stages = lax.axis_size("pipe")
    stage = lax.axis_index("pipe")
    blocks = total // BLOCK
    ticks = blocks + LAG * (stages - 1)
    lens = near(jnp.broadcast_to(lengths[:, None], (rows, width)))
    cot, inputs, gate_bias = near(cotangent[0]), near(inputs), near(gate_bias)
    params = pltpu.CompilerParams(vmem_limit_bytes=LIMIT)
    bf16, f32 = jnp.bfloat16, jnp.float32

    flat, turned = shape((width, gated), bf16), shape((gated, width), bf16)
    kept_gates, kept_cells = shape((total, rows, gated), f32), shape((total + 1, rows, width), f32)
    one = shape((rows, width), f32)
    state = (flat, flat, shape((total, rows, width), bf16), kept_gates, kept_cells)
    fine, half = width // 32, gated // 2
    store = shape((total, rows, half), bf16)
    block = shape((BLOCK, rows, width), bf16)
    far = pltpu.HBM((gated, width), bf16)
    state += (shape((total + 1, rows, width), bf16), far, far)
    def forward(tick):
        first = tick == 0
        extra = (turned,) if tick == ticks - 1 else ()
        return pl.pallas_call(
            partial(forward_kernel, tick=tick, stages=stages),
            out_shape=(block,) + state + extra,
            in_specs=[SMEM] + [VMEM] * 3 + ([HBM] * 2 if first else [VMEM] * 7 + [HBM] * 2),
            out_specs=(VMEM,) * 7 + (HBM,) * 2 + (VMEM,) * len(extra),
            scratch_shapes=[
                pltpu.VMEM((BLOCK, rows, gated), f32),
                pltpu.VMEM((SLOTS, PANEL, width), bf16),
                pltpu.SemaphoreType.DMA((SLOTS,)),
                pltpu.SemaphoreType.DMA((2,)),
            ],
            input_output_aliases={} if first else {5 + n: 1 + n for n in range(8)},
            compiler_params=params,
            name="forward_tick",
        )

    place = jnp.stack([stage] + [lax.axis_index(a) for a in ("y", "z", "xh")]).astype(jnp.int32)
    landed = {}
    for tick in range(ticks):
        if tick == 0:
            got = [pltpu.with_memory_space_constraint(w[0], pltpu.HBM) for w in (input_weight, recurrent_weight)]
        else:
            got = [landed.get(tick, emitted), *held]
        emitted, *held = forward(tick)(place, inputs, gate_bias, lens, *got)
        on = [s for s in range(stages - 1) if 0 <= tick - LAG * s < blocks]
        if on:
            landed[tick + LAG] = near(lax.ppermute(emitted, "pipe", [(s, s + 1) for s in on]))

    _, _, xs, gates, cells, hs, wit_far, _, wrt = held

    def backward(tick):
        first = tick == 0
        aliases = {5: 3, 6: 4, 7: 6} if first else {4 + i: 1 + i for i in range(8)}
        return pl.pallas_call(
            partial(backward_kernel, tick=tick, stages=stages),
            out_shape=(block, store, store, kept_gates, kept_cells, turned, turned, one, one),
            in_specs=[SMEM] + [VMEM] * 3 + ([HBM] + [VMEM] * 3 if first else [VMEM] * 8),
            out_specs=(VMEM,) * 9,
            scratch_shapes=[pltpu.SemaphoreType.DMA((1,))] if first else [],
            input_output_aliases=aliases,
            compiler_params=params,
            name="backward_tick",
        )

    def simple(kernel, name, outs, count, scratch=()):
        return pl.pallas_call(
            kernel,
            out_shape=outs,
            in_specs=[SMEM] + [VMEM] * count,
            out_specs=jax.tree.map(lambda _: VMEM, outs),
            scratch_shapes=scratch,
            compiler_params=params,
            name=name,
        )

    final_hidden, final_cell = hs[total], cells[total]
    held = [pltpu.with_memory_space_constraint(wit_far, pltpu.HBM), gates, cells, wrt]
    routes = [[(i, (i + d) % 4) for i in range(4)] for d in range(1, 4)]

    def passed(made):
        return [near(lax.ppermute(made[n], "y" if n < 3 else "z", routes[n % 3])) for n in range(6)]

    group = shape((4, 4, fine, total * rows), bf16)
    lefts, landed, lower = [], {}, emitted
    for tick in range(ticks):
        lower, *held = backward(tick)(place, cot, landed.get(tick, lower), lens, *held)
        if tick == 0:
            xs, hs, lower = lax.optimization_barrier((xs, hs, lower))
            spread = simple(prepare_kernel, "prepare", (group,) * 8, 2, [pltpu.VMEM((4, 4, 4, fine, total * rows), bf16)])(
                place, near(xs), near(hs)
            )
        on = [s for s in range(1, stages) if 0 <= tick - LAG * (stages - 1 - s) < blocks]
        if on:
            landed[tick + LAG] = near(lax.ppermute(lower, "pipe", [(s, s - 1) for s in on]))
        if 1 <= tick <= 6:
            axis, d = ("y", tick) if tick < 4 else ("z", tick - 3)
            piece, _ = lax.optimization_barrier((spread[tick if tick < 4 else tick + 1], lower))
            piece = lax.ppermute(piece, axis, routes[d - 1])
            pair = lax.optimization_barrier((landed[tick + LAG], piece))
            landed[tick + LAG], piece = map(near, pair)
            lefts.append(piece)
    dy, dz = held[:2]
    part, whole = shape((4 * fine + EXTRA, half), bf16), shape((4, fine, half), f32)
    mine_y, mine_z, bias, *sends = simple(
        combine_kernel,
        "combine",
        (whole, whole, shape((1, gated), f32)) + (part,) * 6,
        16,
        [pltpu.VMEM((4, 4, fine, 4 * total * rows), bf16), pltpu.VMEM((4 * total * rows, half), bf16)],
    )(place, spread[0], *lefts[:3], spread[4], *lefts[3:], dy, dz, *passed([dy] * 3 + [dz] * 3))
    got = passed(sends[3:] + sends[:3])
    keep, bias, give = simple(
        finish_kernel,
        "finish",
        (shape((2, fine, gated), f32), shape((1, gated), f32), shape((2 * fine + EXTRA, gated), bf16)),
        9,
    )(place, mine_y, mine_z, bias, *got[3:], *got[:3])
    other = near(lax.ppermute(give, "xh", [(0, 1), (1, 0)]))
    made = jax.ShapeDtypeStruct
    grad_i, grad_r, grad_b = simple(
        last_kernel,
        "last",
        (made((fine, gated), f32), made((fine, gated), f32), made((1, gated // 32), f32)),
        3,
    )(place, keep, bias, other)
    return (grad_i[None], grad_r[None], grad_b, final_hidden[None], final_cell[None])


def solution(mesh):
    fine = Mesh(mesh.devices.reshape(2, 4, 4, 4), ("xh", "y", "z", "pipe"))
    return jax.shard_map(
        local,
        mesh=fine,
        in_specs=(
            P(None, DP, None),
            P("pipe", None, None),
            P("pipe", None, None),
            P("pipe", None),
            P(DP),
            P("pipe", None, DP, None),
        ),
        out_specs=(
            P("pipe", DP, None),
            P("pipe", DP, None),
            P("pipe", DP),
            P("pipe", DP, None),
            P("pipe", DP, None),
        ),
        check_vma=False,
    )
```

profile of v0, /device:TPU:0, one launch (start us, length us, event | category | flops | bytes accessed | tf_op | source)
XLA Modules:
  0.0 234.8 jit_solution(3459192300101431927)
XLA Ops:
  3.1 11.9 %forward_tick.10 = (bf16[4,8,1024]{2,1,0:T(8,128)(2,1)S(1)}, bf16[1024,4096]{1,0:T(8,128)(2,1)S(1)}, bf16[1024,4096]{1,0:T(8,128)(2,1)S(1)}, bf16[16,8,1024]{2,1...) custom-call(s32[4]{0:T(128)S(1)} %pad_add_fusion.place, ...), custom_call_target="tpu_custom_call" | custom-call | tf_op jit(solution)/shard_map/forward_tick/pallas_call | solution.py:420
  16.3 8.0 %forward_tick.11 = (bf16[4,8,1024]{2,1,0:T(8,128)(2,1)S(1)}, bf16[1024,4096]{1,0:T(8,128)(2,1)S(1)}, bf16[1024,4096]{1,0:T(8,128)(2,1)S(1)}, bf16[16,8,1024]{2,1...) custom-call(s32[4]{0:T(128)S(1)} %pad_add_fusion.place, ...), custom_call_target="tpu_custom_call", output_to_operand_aliasing={{1}: (5, {}), {2}: (6, {}), {3}: (7, {}), {4}: (8, {}), {5}... | custom-call | tf_op jit(solution)/shard_map/forward_tick/pallas_call | solution.py:420
  25.6 8.0 %forward_tick.12 = (bf16[4,8,1024]{2,1,0:T(8,128)(2,1)S(1)}, bf16[1024,4096]{1,0:T(8,128)(2,1)S(1)}, bf16[1024,4096]{1,0:T(8,128)(2,1)S(1)}, bf16[16,8,1024]{2,1...) custom-call(s32[4]{0:T(128)S(1)} %pad_add_fusion.place, ...), custom_call_target="tpu_custom_call", output_to_operand_aliasing={{1}: (5, {}), {2}: (6, {}), {3}: (7, {}), {4}: (8, {}), {5}... | custom-call | tf_op jit(solution)/shard_map/forward_tick/pallas_call | solution.py:420
  34.9 8.0 %forward_tick.13 = (bf16[4,8,1024]{2,1,0:T(8,128)(2,1)S(1)}, bf16[1024,4096]{1,0:T(8,128)(2,1)S(1)}, bf16[1024,4096]{1,0:T(8,128)(2,1)S(1)}, bf16[16,8,1024]{2,1...) custom-call(s32[4]{0:T(128)S(1)} %pad_add_fusion.place, ...), custom_call_target="tpu_custom_call", output_to_operand_aliasing={{1}: (5, {}), {2}: (6, {}), {3}: (7, {}), {4}: (8, {}), {5}... | custom-call | tf_op jit(solution)/shard_map/forward_tick/pallas_call | solution.py:420
  49.5 7.7 %forward_tick.18 = (bf16[4,8,1024]{2,1,0:T(8,128)(2,1)}, bf16[1024,4096]{1,0:T(8,128)(2,1)S(1)}, bf16[1024,4096]{1,0:T(8,128)(2,1)S(1)}, bf16[16,8,1024]{2,1,0:T...) custom-call(s32[4]{0:T(128)S(1)} %pad_add_fusion.place, ...), custom_call_target="tpu_custom_call", output_to_operand_aliasing={{1}: (5, {}), {2}: (6, {}), {3}: (7, {}), {4}: (8, {}), {5}... | custom-call | tf_op jit(solution)/shard_map/forward_tick/pallas_call | solution.py:420
  57.3 10.5 %forward_tick.19 = (bf16[4,8,1024]{2,1,0:T(8,128)(2,1)S(1)}, bf16[1024,4096]{1,0:T(8,128)(2,1)S(1)}, bf16[1024,4096]{1,0:T(8,128)(2,1)S(1)}, bf16[16,8,1024]{2,1...) custom-call(s32[4]{0:T(128)S(1)} %pad_add_fusion.place, ...), custom_call_target="tpu_custom_call", output_to_operand_aliasing={{1}: (5, {}), {2}: (6, {}), {3}: (7, {}), {4}: (8, {}), {5}... | custom-call | tf_op jit(solution)/shard_map/forward_tick/pallas_call | solution.py:420
  68.4 3.9 %backward_tick.10 = (bf16[4,8,1024]{2,1,0:T(8,128)(2,1)S(1)}, bf16[16,8,2048]{2,1,0:T(8,128)(2,1)S(1)}, bf16[16,8,2048]{2,1,0:T(8,128)(2,1)S(1)}, f32[16,8,4096]...) custom-call(s32[4]{0:T(128)S(1)} %pad_add_fusion.place, ...), custom_call_target="tpu_custom_call", output_to_operand_aliasing={{3}: (5, {}), {4}: (6, {}), {6}: (7, {})} | custom-call | tf_op jit(solution)/shard_map/backward_tick/pallas_call | solution.py:462
  77.6 3.0 %collective-permute-start.12 = (bf16[4,4,32,128]{3,2,1,0:T(8,128)(2,1)S(1)}, bf16[4,4,32,128]{3,2,1,0:T(8,128)(2,1)S(1)}, u32[]{:S(2)}, u32[]{:S(2)}) collective-permute-start(bf16[4,4,32,128]{3,2,1,0:T(8,128)(2,1)S(1)} %get-tuple-element.332), channel_id=1, source_target_pairs={{0,32},{16,48},{32,0},{48,16},{1,33},{17,49},{33,1},{49,17},{2,34}... | collective-permute-start | bytes 393224 | tf_op jit(solution)/shard_map/ppermute | solution.py:474
  88.6 3.7 %collective-permute-start.18 = (bf16[4,4,32,128]{3,2,1,0:T(8,128)(2,1)S(1)}, bf16[4,4,32,128]{3,2,1,0:T(8,128)(2,1)S(1)}, u32[]{:S(2)}, u32[]{:S(2)}) collective-permute-start(bf16[4,4,32,128]{3,2,1,0:T(8,128)(2,1)S(1)} %get-tuple-element.372), channel_id=1, source_target_pairs={{0,8},{4,12},{8,0},{12,4},{1,9},{5,13},{9,1},{13,5},{2,10},{6,14},... | collective-permute-start | bytes 393224 | tf_op jit(solution)/shard_map/ppermute | solution.py:474
  93.6 22.7 %collective-permute-done.15.arrived = bf16[4,8,1024]{2,1,0:T(8,128)(2,1)S(1)} collective-permute-done((bf16[4,8,1024]{2,1,0:T(8,128)(2,1)S(1)}, bf16[4,8,1024]{2,1,0:T(8,128)(2,1)S(1)}, u32[]{:S(2)}, u32[]{:S(2)}) %collective-permute-start.15) | collective-permute-done | bytes 65568 | tf_op jit(solution)/shard_map/ppermute | solution.py:470
  116.3 5.4 %backward_tick.16 = (bf16[4,8,1024]{2,1,0:T(8,128)(2,1)S(1)}, bf16[16,8,2048]{2,1,0:T(8,128)(2,1)S(1)}, bf16[16,8,2048]{2,1,0:T(8,128)(2,1)S(1)}, f32[16,8,4096]...) custom-call(s32[4]{0:T(128)S(1)} %pad_add_fusion.place, ...), custom_call_target="tpu_custom_call", output_to_operand_aliasing={{1}: (4, {}), {2}: (5, {}), {3}: (6, {}), {4}: (7, {}), {5}... | custom-call | tf_op jit(solution)/shard_map/backward_tick/pallas_call | solution.py:462
  125.4 3.5 %collective-permute-done.17.arrived = bf16[4,8,1024]{2,1,0:T(8,128)(2,1)S(1)} collective-permute-done((bf16[4,8,1024]{2,1,0:T(8,128)(2,1)S(1)}, bf16[4,8,1024]{2,1,0:T(8,128)(2,1)S(1)}, u32[]{:S(2)}, u32[]{:S(2)}) %collective-permute-start.17) | collective-permute-done | bytes 65568 | tf_op jit(solution)/shard_map/ppermute | solution.py:470
  128.9 5.4 %backward_tick.17 = (bf16[4,8,1024]{2,1,0:T(8,128)(2,1)S(1)}, bf16[16,8,2048]{2,1,0:T(8,128)(2,1)S(1)}, bf16[16,8,2048]{2,1,0:T(8,128)(2,1)S(1)}, f32[16,8,4096]...) custom-call(s32[4]{0:T(128)S(1)} %pad_add_fusion.place, ...), custom_call_target="tpu_custom_call", output_to_operand_aliasing={{1}: (4, {}), {2}: (5, {}), {3}: (6, {}), {4}: (7, {}), {5}... | custom-call | tf_op jit(solution)/shard_map/backward_tick/pallas_call | solution.py:462
  138.3 6.2 %backward_tick.18 = (bf16[4,8,1024]{2,1,0:T(8,128)(2,1)}, bf16[16,8,2048]{2,1,0:T(8,128)(2,1)S(1)}, bf16[16,8,2048]{2,1,0:T(8,128)(2,1)S(1)}, f32[16,8,4096]{2,1...) custom-call(s32[4]{0:T(128)S(1)} %pad_add_fusion.place, ...), custom_call_target="tpu_custom_call", output_to_operand_aliasing={{1}: (4, {}), {2}: (5, {}), {3}: (6, {}), {4}: (7, {}), {5}... | custom-call | tf_op jit(solution)/shard_map/backward_tick/pallas_call | solution.py:462
  144.4 2.7 %collective-permute-done.21.arrived = bf16[4,8,1024]{2,1,0:T(8,128)(2,1)S(1)} collective-permute-done((bf16[4,8,1024]{2,1,0:T(8,128)(2,1)S(1)}, bf16[4,8,1024]{2,1,0:T(8,128)(2,1)S(1)}, u32[]{:S(2)}, u32[]{:S(2)}) %collective-permute-start.21) | collective-permute-done | bytes 65568 | tf_op jit(solution)/shard_map/ppermute | solution.py:470
  147.2 6.0 %backward_tick.19 = (bf16[4,8,1024]{2,1,0:T(8,128)(2,1)}, bf16[16,8,2048]{2,1,0:T(8,128)(2,1)S(1)}, bf16[16,8,2048]{2,1,0:T(8,128)(2,1)S(1)}, f32[16,8,4096]{2,1...) custom-call(s32[4]{0:T(128)S(1)} %pad_add_fusion.place, ...), custom_call_target="tpu_custom_call", output_to_operand_aliasing={{1}: (4, {}), {2}: (5, {}), {3}: (6, {}), {4}: (7, {}), {5}... | custom-call | tf_op jit(solution)/shard_map/backward_tick/pallas_call | solution.py:462
  158.8 9.2 %collective-permute-done.24.rest_12_ = bf16[16,8,2048]{2,1,0:T(8,128)(2,1)S(1)} collective-permute-done((bf16[16,8,2048]{2,1,0:T(8,128)(2,1)S(1)}, bf16[16,8,2048]{2,1,0:T(8,128)(2,1)S(1)}, u32[]{:S(2)}, u32[]{:S(2)}) %collective-permute-start.24) | collective-permute-done | bytes 524320 | tf_op jit(solution)/shard_map/ppermute | solution.py:457
  170.5 5.8 %collective-permute-done.22.rest_10_ = bf16[16,8,2048]{2,1,0:T(8,128)(2,1)S(1)} collective-permute-done((bf16[16,8,2048]{2,1,0:T(8,128)(2,1)S(1)}, bf16[16,8,2048]{2,1,0:T(8,128)(2,1)S(1)}, u32[]{:S(2)}, u32[]{:S(2)}) %collective-permute-start.22) | collective-permute-done | bytes 524320 | tf_op jit(solution)/shard_map/ppermute | solution.py:457
  178.9 5.1 %combine.1 = (f32[4,32,2048]{2,1,0:T(8,128)S(1)}, f32[4,32,2048]{2,1,0:T(8,128)S(1)}, f32[1,4096]{1,0:T(1,128)S(1)}, bf16[144,2048]{1,0:T(8,128)(2,1)S(1)}, bf16...) custom-call(s32[4]{0:T(128)S(1)} %pad_add_fusion.place, ...), custom_call_target="tpu_custom_call" | custom-call | tf_op jit(solution)/shard_map/combine/pallas_call | solution.py:480
  189.7 2.9 %collective-permute-start.32 = (bf16[144,2048]{1,0:T(8,128)(2,1)S(1)}, bf16[144,2048]{1,0:T(8,128)(2,1)S(1)}, u32[]{:S(2)}, u32[]{:S(2)}) collective-permute-start(bf16[144,2048]{1,0:T(8,128)(2,1)S(1)} %get-tuple-element.423), channel_id=1, source_target_pairs={{0,32},{16,48},{32,0},{48,16},{1,33},{17,49},{33,1},{49,17},{2,34}... | collective-permute-start | bytes 1769480 | tf_op jit(solution)/shard_map/ppermute | solution.py:457
  192.6 17.3 %collective-permute-done.28.rest_0_ = bf16[144,2048]{1,0:T(8,128)(2,1)S(1)} collective-permute-done((bf16[144,2048]{1,0:T(8,128)(2,1)S(1)}, bf16[144,2048]{1,0:T(8,128)(2,1)S(1)}, u32[]{:S(2)}, u32[]{:S(2)}) %collective-permute-start.28) | collective-permute-done | bytes 589856 | tf_op jit(solution)/shard_map/ppermute | solution.py:457
  213.3 6.6 %collective-permute-done.33.rest_5_ = bf16[144,2048]{1,0:T(8,128)(2,1)S(1)} collective-permute-done((bf16[144,2048]{1,0:T(8,128)(2,1)S(1)}, bf16[144,2048]{1,0:T(8,128)(2,1)S(1)}, u32[]{:S(2)}, u32[]{:S(2)}) %collective-permute-start.33) | collective-permute-done | bytes 589856 | tf_op jit(solution)/shard_map/ppermute | solution.py:457
  221.0 2.8 %collective-permute-start.34 = (bf16[80,4096]{1,0:T(8,128)(2,1)S(1)}, bf16[80,4096]{1,0:T(8,128)(2,1)S(1)}, u32[]{:S(2)}, u32[]{:S(2)}) collective-permute-start(bf16[80,4096]{1,0:T(8,128)(2,1)S(1)} %get-tuple-element.427), channel_id=1, source_target_pairs={{0,64},{64,0},{1,65},{65,1},{2,66},{66,2},{3,67},{67,3},{4,68},{68... | collective-permute-start | bytes 1966088 | tf_op jit(solution)/shard_map/ppermute | solution.py:494
  224.5 8.7 %collective-permute-done.34.arrived = bf16[80,4096]{1,0:T(8,128)(2,1)S(1)} collective-permute-done((bf16[80,4096]{1,0:T(8,128)(2,1)S(1)}, bf16[80,4096]{1,0:T(8,128)(2,1)S(1)}, u32[]{:S(2)}, u32[]{:S(2)}) %collective-permute-start.34) | collective-permute-done | bytes 655392 | tf_op jit(solution)/shard_map/ppermute | solution.py:494
  (80 shorter events, 58.7 us)
Async XLA Ops:
  15.0 10.6 %collective-permute-start.1 = (bf16[4,8,1024]{2,1,0:T(8,128)(2,1)S(1)}, bf16[4,8,1024]{2,1,0:T(8,128)(2,1)S(1)}, u32[]{:S(2)}, u32[]{:S(2)}) collective-permute-start(bf16[4,8,1024]{2,1,0:T(8,128)(2,1)S(1)} %get-tuple-element.218.rest_0_), channel_id=1, source_target_pairs={{0,1},{4,5},{8,9},{12,13},{16,17},{20,21},{24,25},{28,29},{32,33},... | collective-permute-start | bytes 196616 | tf_op jit(solution)/shard_map/ppermute | solution.py:423
  24.3 10.6 %collective-permute-start = (bf16[4,8,1024]{2,1,0:T(8,128)(2,1)S(1)}, bf16[4,8,1024]{2,1,0:T(8,128)(2,1)S(1)}, u32[]{:S(2)}, u32[]{:S(2)}) collective-permute-start(bf16[4,8,1024]{2,1,0:T(8,128)(2,1)S(1)} %get-tuple-element.227), channel_id=1, source_target_pairs={{0,1},{4,5},{8,9},{12,13},{16,17},{20,21},{24,25},{28,29},{32,33},... | collective-permute-start | bytes 196616 | tf_op jit(solution)/shard_map/ppermute | solution.py:423
  33.6 10.6 %collective-permute-start.3 = (bf16[4,8,1024]{2,1,0:T(8,128)(2,1)S(1)}, bf16[4,8,1024]{2,1,0:T(8,128)(2,1)S(1)}, u32[]{:S(2)}, u32[]{:S(2)}) collective-permute-start(bf16[4,8,1024]{2,1,0:T(8,128)(2,1)S(1)} %get-tuple-element.245), channel_id=1, source_target_pairs={{0,1},{1,2},{4,5},{5,6},{8,9},{9,10},{12,13},{13,14},{16,17},{17,1... | collective-permute-start | bytes 196616 | tf_op jit(solution)/shard_map/ppermute | solution.py:423
  48.8 8.4 %collective-permute-start.6 = (bf16[4,8,1024]{2,1,0:T(8,128)(2,1)S(1)}, bf16[4,8,1024]{2,1,0:T(8,128)(2,1)S(1)}, u32[]{:S(2)}, u32[]{:S(2)}) collective-permute-start(bf16[4,8,1024]{2,1,0:T(8,128)(2,1)S(1)} %get-tuple-element.280), channel_id=1, source_target_pairs={{2,3},{6,7},{10,11},{14,15},{18,19},{22,23},{26,27},{30,31},{34,35... | collective-permute-start | bytes 196616 | tf_op jit(solution)/shard_map/ppermute | solution.py:423
  84.7 31.5 %collective-permute-start.16 = (bf16[4,4,32,128]{3,2,1,0:T(8,128)(2,1)S(1)}, bf16[4,4,32,128]{3,2,1,0:T(8,128)(2,1)S(1)}, u32[]{:S(2)}, u32[]{:S(2)}) collective-permute-start(bf16[4,4,32,128]{3,2,1,0:T(8,128)(2,1)S(1)} %get-tuple-element.359), channel_id=1, source_target_pairs={{0,4},{4,8},{8,12},{12,0},{1,5},{5,9},{9,13},{13,1},{2,6},{6,10},{... | collective-permute-start | bytes 393224 | tf_op jit(solution)/shard_map/ppermute | solution.py:474
  86.7 29.5 %collective-permute-start.15 = (bf16[4,8,1024]{2,1,0:T(8,128)(2,1)S(1)}, bf16[4,8,1024]{2,1,0:T(8,128)(2,1)S(1)}, u32[]{:S(2)}, u32[]{:S(2)}) collective-permute-start(bf16[4,8,1024]{2,1,0:T(8,128)(2,1)S(1)} %get-tuple-element.357), channel_id=1, source_target_pairs={{1,0},{2,1},{5,4},{6,5},{9,8},{10,9},{13,12},{14,13},{17,16},{18,1... | collective-permute-start | bytes 196616 | tf_op jit(solution)/shard_map/ppermute | solution.py:470
  88.6 40.2 %collective-permute-start.18 = (bf16[4,4,32,128]{3,2,1,0:T(8,128)(2,1)S(1)}, bf16[4,4,32,128]{3,2,1,0:T(8,128)(2,1)S(1)}, u32[]{:S(2)}, u32[]{:S(2)}) collective-permute-start(bf16[4,4,32,128]{3,2,1,0:T(8,128)(2,1)S(1)} %get-tuple-element.372), channel_id=1, source_target_pairs={{0,8},{4,12},{8,0},{12,4},{1,9},{5,13},{9,1},{13,5},{2,10},{6,14},... | collective-permute-start | bytes 393224 | tf_op jit(solution)/shard_map/ppermute | solution.py:474
  92.3 36.6 %collective-permute-start.17 = (bf16[4,8,1024]{2,1,0:T(8,128)(2,1)S(1)}, bf16[4,8,1024]{2,1,0:T(8,128)(2,1)S(1)}, u32[]{:S(2)}, u32[]{:S(2)}) collective-permute-start(bf16[4,8,1024]{2,1,0:T(8,128)(2,1)S(1)} %get-tuple-element.370), channel_id=1, source_target_pairs={{1,0},{2,1},{5,4},{6,5},{9,8},{10,9},{13,12},{14,13},{17,16},{18,1... | collective-permute-start | bytes 196616 | tf_op jit(solution)/shard_map/ppermute | solution.py:470
  121.6 16.6 %collective-permute-start.20 = (bf16[4,4,32,128]{3,2,1,0:T(8,128)(2,1)S(1)}, bf16[4,4,32,128]{3,2,1,0:T(8,128)(2,1)S(1)}, u32[]{:S(2)}, u32[]{:S(2)}) collective-permute-start(bf16[4,4,32,128]{3,2,1,0:T(8,128)(2,1)S(1)} %get-tuple-element.385), channel_id=1, source_target_pairs={{0,12},{4,0},{8,4},{12,8},{1,13},{5,1},{9,5},{13,9},{2,14},{6,2},{... | collective-permute-start | bytes 393224 | tf_op jit(solution)/shard_map/ppermute | solution.py:474
  124.1 14.2 %collective-permute-start.19 = (bf16[4,8,1024]{2,1,0:T(8,128)(2,1)S(1)}, bf16[4,8,1024]{2,1,0:T(8,128)(2,1)S(1)}, u32[]{:S(2)}, u32[]{:S(2)}) collective-permute-start(bf16[4,8,1024]{2,1,0:T(8,128)(2,1)S(1)} %get-tuple-element.383), channel_id=1, source_target_pairs={{1,0},{5,4},{9,8},{13,12},{17,16},{21,20},{25,24},{29,28},{33,32},... | collective-permute-start | bytes 196616 | tf_op jit(solution)/shard_map/ppermute | solution.py:470
  134.2 12.9 %collective-permute-start.21 = (bf16[4,8,1024]{2,1,0:T(8,128)(2,1)S(1)}, bf16[4,8,1024]{2,1,0:T(8,128)(2,1)S(1)}, u32[]{:S(2)}, u32[]{:S(2)}) collective-permute-start(bf16[4,8,1024]{2,1,0:T(8,128)(2,1)S(1)} %get-tuple-element.396), channel_id=1, source_target_pairs={{1,0},{5,4},{9,8},{13,12},{17,16},{21,20},{25,24},{29,28},{33,32},... | collective-permute-start | bytes 196616 | tf_op jit(solution)/shard_map/ppermute | solution.py:470
  153.2 14.9 %collective-permute-start.24 = (bf16[16,8,2048]{2,1,0:T(8,128)(2,1)S(1)}, bf16[16,8,2048]{2,1,0:T(8,128)(2,1)S(1)}, u32[]{:S(2)}, u32[]{:S(2)}) collective-permute-start(bf16[16,8,2048]{2,1,0:T(8,128)(2,1)S(1)} %get-tuple-element.414.rest_8_), channel_id=1, source_target_pairs={{0,48},{16,0},{32,16},{48,32},{1,49},{17,1},{33,17},{49,33},{2,50}... | collective-permute-start | bytes 1572872 | tf_op jit(solution)/shard_map/ppermute | solution.py:457
  154.1 16.4 %collective-permute-start.23 = (bf16[16,8,2048]{2,1,0:T(8,128)(2,1)S(1)}, bf16[16,8,2048]{2,1,0:T(8,128)(2,1)S(1)}, u32[]{:S(2)}, u32[]{:S(2)}) collective-permute-start(bf16[16,8,2048]{2,1,0:T(8,128)(2,1)S(1)} %get-tuple-element.414.rest_8_), channel_id=1, source_target_pairs={{0,32},{16,48},{32,0},{48,16},{1,33},{17,49},{33,1},{49,17},{2,34}... | collective-permute-start | bytes 1572872 | tf_op jit(solution)/shard_map/ppermute | solution.py:457
  156.2 20.1 %collective-permute-start.22 = (bf16[16,8,2048]{2,1,0:T(8,128)(2,1)S(1)}, bf16[16,8,2048]{2,1,0:T(8,128)(2,1)S(1)}, u32[]{:S(2)}, u32[]{:S(2)}) collective-permute-start(bf16[16,8,2048]{2,1,0:T(8,128)(2,1)S(1)} %get-tuple-element.414.rest_8_), channel_id=1, source_target_pairs={{0,16},{16,32},{32,48},{48,0},{1,17},{17,33},{33,49},{49,1},{2,18}... | collective-permute-start | bytes 1572872 | tf_op jit(solution)/shard_map/ppermute | solution.py:457
  156.3 20.0 %collective-permute-start.27 = (bf16[16,8,2048]{2,1,0:T(8,128)(2,1)S(1)}, bf16[16,8,2048]{2,1,0:T(8,128)(2,1)S(1)}, u32[]{:S(2)}, u32[]{:S(2)}) collective-permute-start(bf16[16,8,2048]{2,1,0:T(8,128)(2,1)S(1)} %get-tuple-element.415.rest_9_), channel_id=1, source_target_pairs={{0,12},{4,0},{8,4},{12,8},{1,13},{5,1},{9,5},{13,9},{2,14},{6,2},{... | collective-permute-start | bytes 1572872 | tf_op jit(solution)/shard_map/ppermute | solution.py:457
  157.3 19.0 %collective-permute-start.26 = (bf16[16,8,2048]{2,1,0:T(8,128)(2,1)S(1)}, bf16[16,8,2048]{2,1,0:T(8,128)(2,1)S(1)}, u32[]{:S(2)}, u32[]{:S(2)}) collective-permute-start(bf16[16,8,2048]{2,1,0:T(8,128)(2,1)S(1)} %get-tuple-element.415.rest_9_), channel_id=1, source_target_pairs={{0,8},{4,12},{8,0},{12,4},{1,9},{5,13},{9,1},{13,5},{2,10},{6,14},... | collective-permute-start | bytes 1572872 | tf_op jit(solution)/shard_map/ppermute | solution.py:457
  168.0 10.8 %collective-permute-start.25 = (bf16[16,8,2048]{2,1,0:T(8,128)(2,1)S(1)}, bf16[16,8,2048]{2,1,0:T(8,128)(2,1)S(1)}, u32[]{:S(2)}, u32[]{:S(2)}) collective-permute-start(bf16[16,8,2048]{2,1,0:T(8,128)(2,1)S(1)} %get-tuple-element.415.rest_9_), channel_id=1, source_target_pairs={{0,4},{4,8},{8,12},{12,0},{1,5},{5,9},{9,13},{13,1},{2,6},{6,10},{... | collective-permute-start | bytes 1572872 | tf_op jit(solution)/shard_map/ppermute | solution.py:457
  184.0 26.0 %collective-permute-start.28 = (bf16[144,2048]{1,0:T(8,128)(2,1)S(1)}, bf16[144,2048]{1,0:T(8,128)(2,1)S(1)}, u32[]{:S(2)}, u32[]{:S(2)}) collective-permute-start(bf16[144,2048]{1,0:T(8,128)(2,1)S(1)} %get-tuple-element.419), channel_id=1, source_target_pairs={{0,4},{4,8},{8,12},{12,0},{1,5},{5,9},{9,13},{13,1},{2,6},{6,10},{... | collective-permute-start | bytes 1769480 | tf_op jit(solution)/shard_map/ppermute | solution.py:457
  184.1 27.0 %collective-permute-start.29 = (bf16[144,2048]{1,0:T(8,128)(2,1)S(1)}, bf16[144,2048]{1,0:T(8,128)(2,1)S(1)}, u32[]{:S(2)}, u32[]{:S(2)}) collective-permute-start(bf16[144,2048]{1,0:T(8,128)(2,1)S(1)} %get-tuple-element.420), channel_id=1, source_target_pairs={{0,8},{4,12},{8,0},{12,4},{1,9},{5,13},{9,1},{13,5},{2,10},{6,14},... | collective-permute-start | bytes 1769480 | tf_op jit(solution)/shard_map/ppermute | solution.py:457
  186.1 25.0 %collective-permute-start.30 = (bf16[144,2048]{1,0:T(8,128)(2,1)S(1)}, bf16[144,2048]{1,0:T(8,128)(2,1)S(1)}, u32[]{:S(2)}, u32[]{:S(2)}) collective-permute-start(bf16[144,2048]{1,0:T(8,128)(2,1)S(1)} %get-tuple-element.421), channel_id=1, source_target_pairs={{0,12},{4,0},{8,4},{12,8},{1,13},{5,1},{9,5},{13,9},{2,14},{6,2},{... | collective-permute-start | bytes 1769480 | tf_op jit(solution)/shard_map/ppermute | solution.py:457
  188.2 22.9 %collective-permute-start.31 = (bf16[144,2048]{1,0:T(8,128)(2,1)S(1)}, bf16[144,2048]{1,0:T(8,128)(2,1)S(1)}, u32[]{:S(2)}, u32[]{:S(2)}) collective-permute-start(bf16[144,2048]{1,0:T(8,128)(2,1)S(1)} %get-tuple-element.422), channel_id=1, source_target_pairs={{0,16},{16,32},{32,48},{48,0},{1,17},{17,33},{33,49},{49,1},{2,18}... | collective-permute-start | bytes 1769480 | tf_op jit(solution)/shard_map/ppermute | solution.py:457
  189.7 23.5 %collective-permute-start.32 = (bf16[144,2048]{1,0:T(8,128)(2,1)S(1)}, bf16[144,2048]{1,0:T(8,128)(2,1)S(1)}, u32[]{:S(2)}, u32[]{:S(2)}) collective-permute-start(bf16[144,2048]{1,0:T(8,128)(2,1)S(1)} %get-tuple-element.423), channel_id=1, source_target_pairs={{0,32},{16,48},{32,0},{48,16},{1,33},{17,49},{33,1},{49,17},{2,34}... | collective-permute-start | bytes 1769480 | tf_op jit(solution)/shard_map/ppermute | solution.py:457
  210.0 9.9 %collective-permute-start.33 = (bf16[144,2048]{1,0:T(8,128)(2,1)S(1)}, bf16[144,2048]{1,0:T(8,128)(2,1)S(1)}, u32[]{:S(2)}, u32[]{:S(2)}) collective-permute-start(bf16[144,2048]{1,0:T(8,128)(2,1)S(1)} %get-tuple-element.424), channel_id=1, source_target_pairs={{0,48},{16,0},{32,16},{48,32},{1,49},{17,1},{33,17},{49,33},{2,50}... | collective-permute-start | bytes 1769480 | tf_op jit(solution)/shard_map/ppermute | solution.py:457
  221.0 12.2 %collective-permute-start.34 = (bf16[80,4096]{1,0:T(8,128)(2,1)S(1)}, bf16[80,4096]{1,0:T(8,128)(2,1)S(1)}, u32[]{:S(2)}, u32[]{:S(2)}) collective-permute-start(bf16[80,4096]{1,0:T(8,128)(2,1)S(1)} %get-tuple-element.427), channel_id=1, source_target_pairs={{0,64},{64,0},{1,65},{65,1},{2,66},{66,2},{3,67},{67,3},{4,68},{68... | collective-permute-start | bytes 1966088 | tf_op jit(solution)/shard_map/ppermute | solution.py:494
  (14 other events, 58.4 us)
where the time goes:
time: 235 us
  Pallas kernels  95.1 us (40%)
  waiting for transfers between devices  85.9 us (37%)
  starting transfers between devices  49.1 us (21%)
  local copies, waits for them, and re-layouts  3.62 us (2%)
    pallas_call x10, Pallas kernels, local(): emitted, *held = forward(tick)(place, inputs, gate_bias, lens, *got)  56.6 us
    ppermute x12, waiting for transfers between devices, passed(): lax.ppermute(made[n], 'y' if n < 3 else 'z', routes[n % 3])  45.3 us
    ppermute x8, waiting for transfers between devices, local(): lax.ppermute(lower, 'pipe', [(s, s - 1) for s in on])  31.6 us
    pallas_call x10, Pallas kernels, local(): backward(tick)(place, cot, landed.get(tick, lower), lens, *held)  29.7 us
    ppermute x12, starting transfers between devices, passed(): lax.ppermute(made[n], 'y' if n < 3 else 'z', routes[n % 3])  16.2 us
    ppermute x6, starting transfers between devices, local(): piece = lax.ppermute(piece, axis, routes[d - 1])  14.4 us
    ppermute x1, waiting for transfers between devices, local(): other = near(lax.ppermute(give, 'xh', [(0, 1), (1, 0)]))  8.75 us
    ppermute x8, starting transfers between devices, local(): lax.ppermute(lower, 'pipe', [(s, s - 1) for s in on])  7.94 us
  transfers between devices with their start and end apart: 35, of which 13 were waited for; matrix products, arithmetic and copies ran while one was open for 0% of the time, Pallas kernels for 23%

commit v1 on v0

--- a/solution.py
+++ b/solution.py
@@ -11,7 +11,7 @@
 LAG = 2
 WIDE = 1024
 COLS = 512
-FORWARD_STEPS = 2
+WHOLE = (2,)
 CHUNK = 256
 PANEL = 256
 SLOTS = 4
@@ -127,7 +127,10 @@
         lax.fori_loop(0, 4 * width // WIDE, project, 0)
 
     if tick == 0:
-        load_wr.wait()
+
+        @pl.when(jnp.logical_not(active))
+        def _():
+            load_wr.wait()
 
     turns = (0, 1, idle + blocks - 2, idle + blocks - 1)
     if tick in turns:
@@ -148,7 +151,7 @@
             hs[0] = jnp.zeros((rows, width), jnp.bfloat16)
             cells[0] = jnp.zeros((rows, width), jnp.float32)
 
-        def frame(t, carry):
+        def frame(t, carry, start=False):
             fr = fs + t
             h = hs[fr]
 
@@ -157,7 +160,7 @@
 
                 def pre(gate):
                     col = pl.ds(shifted(j, gate * width), CHUNK)
-                    return proj[t, :, col] + dot(h, wr[:, col])
+                    return proj[t, :, col] if start else proj[t, :, col] + dot(h, wr[:, col])
 
                 alive = fr < lens[:, part]
                 i, f, g, o = squash(pre(0)), squash(pre(1)), jnp.tanh(pre(2)), squash(pre(3))
@@ -171,10 +174,13 @@
                 hs[fr + 1, :, part] = jnp.where(alive, new_h, old_h)
                 emitted[t, :, part] = jnp.where(alive, new_h, jnp.zeros_like(new_h))
 
-            over_columns(column, width, FORWARD_STEPS)
+            over_columns(column, width, 1 if start or tick in WHOLE else 2)
             return carry
 
-        lax.fori_loop(0, span, frame, 0)
+        if tick == 0:
+            frame(0, 0, start=True)
+            load_wr.wait()
+        lax.fori_loop(1 if tick == 0 else 0, span, frame, 0)
 
     if last:
         load.wait()
@@ -207,7 +213,7 @@
             dh[...] = jnp.zeros((rows, width), jnp.float32)
             dc[...] = jnp.zeros((rows, width), jnp.float32)
 
-        def frame(n, carry):
+        def frame(n, carry, end=False):
             t = span - 1 - n
             fr = fs + t
             acc = None
@@ -238,12 +244,18 @@
                         dy[fr, :, col] = d
                     else:
                         dz[fr, :, pl.ds(gate * width + j - half, CHUNK)] = d
-                    term = dot(d, wrt[col, :])
-                    acc = term if acc is None else acc + term
-            dh[...] = dh[...] + acc
+                    if not end:
+                        term = dot(d, wrt[col, :])
+                        acc = term if acc is None else acc + term
+            if not end:
+                dh[...] = dh[...] + acc
             return carry
 
-        lax.fori_loop(0, span, frame, 0)
+        final = tick == blocks + LAG * (stages - 1) - 1
+        lax.fori_loop(0, span - 1 if final else span, frame, 0)
+        if final:
+            frame(span - 1, 0, end=True)
+
 
     if tick == 0:
         load.wait()
@@ -449,7 +461,6 @@
             name=name,
         )
 
-    final_hidden, final_cell = hs[total], cells[total]
     held = [pltpu.with_memory_space_constraint(wit_far, pltpu.HBM), gates, cells, wrt]
     routes = [[(i, (i + d) % 4) for i in range(4)] for d in range(1, 4)]
 
@@ -476,6 +487,7 @@
             landed[tick + LAG], piece = map(near, pair)
             lefts.append(piece)
     dy, dz = held[:2]
+    final_hidden, final_cell = hs[total], held[3][total]
     part, whole = shape((4 * fine + EXTRA, half), bf16), shape((4, fine, half), f32)
     mine_y, mine_z, bias, *sends = simple(
         combine_kernel,

time: 235 us -> 235 us (level)
  Pallas kernels: 95.1 us -> 91.9 us
  waiting for transfers between devices: 85.9 us -> 88.6 us
    ppermute x8, waiting for transfers between devices: 31.6 us -> 34 us  [local(): lax.ppermute(lower, 'pipe', [(s, s - 1) for s in on])]
  transfers between devices with their start and end apart: 35 -> 35, of which waited for: 13 -> 13; matrix products, arithmetic and copies ran while one was open for 0% -> 1% of each run, Pallas kernels for 23% -> 23%
where the time goes in v1:
time: 235 us
  Pallas kernels  91.9 us (39%)
  waiting for transfers between devices  88.6 us (38%)
  starting transfers between devices  49.5 us (21%)
  local copies, waits for them, and re-layouts  3.62 us (2%)
    pallas_call x10, Pallas kernels, local(): emitted, *held = forward(tick)(place, inputs, gate_bias, lens, *got)  54.7 us
    ppermute x12, waiting for transfers between devices, passed(): lax.ppermute(made[n], 'y' if n < 3 else 'z', routes[n % 3])  46.3 us
    ppermute x8, waiting for transfers between devices, local(): lax.ppermute(lower, 'pipe', [(s, s - 1) for s in on])  34 us
    pallas_call x10, Pallas kernels, local(): backward(tick)(place, cot, landed.get(tick, lower), lens, *held)  28.5 us
    ppermute x12, starting transfers between devices, passed(): lax.ppermute(made[n], 'y' if n < 3 else 'z', routes[n % 3])  16.7 us
    ppermute x6, starting transfers between devices, local(): piece = lax.ppermute(piece, axis, routes[d - 1])  14.4 us
    ppermute x1, waiting for transfers between devices, local(): other = near(lax.ppermute(give, 'xh', [(0, 1), (1, 0)]))  8.14 us
    ppermute x8, starting transfers between devices, local(): lax.ppermute(emitted, 'pipe', [(s, s + 1) for s in on])  7.83 us
  transfers between devices with their start and end apart: 35, of which 13 were waited for; matrix products, arithmetic and copies ran while one was open for 1% of the time, Pallas kernels for 23%

profile of v1, /device:TPU:0, one launch (start us, length us, event | category | flops | bytes accessed | tf_op | source)
XLA Modules:
  0.0 234.8 jit_solution(4305477298913947283)
XLA Ops:
  3.1 10.5 %forward_tick.10 = (bf16[4,8,1024]{2,1,0:T(8,128)(2,1)S(1)}, bf16[1024,4096]{1,0:T(8,128)(2,1)S(1)}, bf16[1024,4096]{1,0:T(8,128)(2,1)S(1)}, bf16[16,8,1024]{2,1...) custom-call(s32[4]{0:T(128)S(1)} %pad_add_fusion.place, ...), custom_call_target="tpu_custom_call" | custom-call | tf_op jit(solution)/shard_map/forward_tick/pallas_call | solution.py:432
  14.9 8.0 %forward_tick.11 = (bf16[4,8,1024]{2,1,0:T(8,128)(2,1)S(1)}, bf16[1024,4096]{1,0:T(8,128)(2,1)S(1)}, bf16[1024,4096]{1,0:T(8,128)(2,1)S(1)}, bf16[16,8,1024]{2,1...) custom-call(s32[4]{0:T(128)S(1)} %pad_add_fusion.place, ...), custom_call_target="tpu_custom_call", output_to_operand_aliasing={{1}: (5, {}), {2}: (6, {}), {3}: (7, {}), {4}: (8, {}), {5}... | custom-call | tf_op jit(solution)/shard_map/forward_tick/pallas_call | solution.py:432
  24.2 7.4 %forward_tick.12 = (bf16[4,8,1024]{2,1,0:T(8,128)(2,1)S(1)}, bf16[1024,4096]{1,0:T(8,128)(2,1)S(1)}, bf16[1024,4096]{1,0:T(8,128)(2,1)S(1)}, bf16[16,8,1024]{2,1...) custom-call(s32[4]{0:T(128)S(1)} %pad_add_fusion.place, ...), custom_call_target="tpu_custom_call", output_to_operand_aliasing={{1}: (5, {}), {2}: (6, {}), {3}: (7, {}), {4}: (8, {}), {5}... | custom-call | tf_op jit(solution)/shard_map/forward_tick/pallas_call | solution.py:432
  33.0 8.0 %forward_tick.13 = (bf16[4,8,1024]{2,1,0:T(8,128)(2,1)S(1)}, bf16[1024,4096]{1,0:T(8,128)(2,1)S(1)}, bf16[1024,4096]{1,0:T(8,128)(2,1)S(1)}, bf16[16,8,1024]{2,1...) custom-call(s32[4]{0:T(128)S(1)} %pad_add_fusion.place, ...), custom_call_target="tpu_custom_call", output_to_operand_aliasing={{1}: (5, {}), {2}: (6, {}), {3}: (7, {}), {4}: (8, {}), {5}... | custom-call | tf_op jit(solution)/shard_map/forward_tick/pallas_call | solution.py:432
  47.5 7.7 %forward_tick.18 = (bf16[4,8,1024]{2,1,0:T(8,128)(2,1)}, bf16[1024,4096]{1,0:T(8,128)(2,1)S(1)}, bf16[1024,4096]{1,0:T(8,128)(2,1)S(1)}, bf16[16,8,1024]{2,1,0:T...) custom-call(s32[4]{0:T(128)S(1)} %pad_add_fusion.place, ...), custom_call_target="tpu_custom_call", output_to_operand_aliasing={{1}: (5, {}), {2}: (6, {}), {3}: (7, {}), {4}: (8, {}), {5}... | custom-call | tf_op jit(solution)/shard_map/forward_tick/pallas_call | solution.py:432
  55.3 10.5 %forward_tick.19 = (bf16[4,8,1024]{2,1,0:T(8,128)(2,1)S(1)}, bf16[1024,4096]{1,0:T(8,128)(2,1)S(1)}, bf16[1024,4096]{1,0:T(8,128)(2,1)S(1)}, bf16[16,8,1024]{2,1...) custom-call(s32[4]{0:T(128)S(1)} %pad_add_fusion.place, ...), custom_call_target="tpu_custom_call", output_to_operand_aliasing={{1}: (5, {}), {2}: (6, {}), {3}: (7, {}), {4}: (8, {}), {5}... | custom-call | tf_op jit(solution)/shard_map/forward_tick/pallas_call | solution.py:432
  65.8 3.9 %backward_tick.10 = (bf16[4,8,1024]{2,1,0:T(8,128)(2,1)S(1)}, bf16[16,8,2048]{2,1,0:T(8,128)(2,1)S(1)}, bf16[16,8,2048]{2,1,0:T(8,128)(2,1)S(1)}, f32[16,8,4096]...) custom-call(s32[4]{0:T(128)S(1)} %pad_add_fusion.place, ...), custom_call_target="tpu_custom_call", output_to_operand_aliasing={{3}: (5, {}), {4}: (6, {}), {6}: (7, {})} | custom-call | tf_op jit(solution)/shard_map/backward_tick/pallas_call | solution.py:473
  74.9 3.0 %collective-permute-start.12 = (bf16[4,4,32,128]{3,2,1,0:T(8,128)(2,1)S(1)}, bf16[4,4,32,128]{3,2,1,0:T(8,128)(2,1)S(1)}, u32[]{:S(2)}, u32[]{:S(2)}) collective-permute-start(bf16[4,4,32,128]{3,2,1,0:T(8,128)(2,1)S(1)} %get-tuple-element.333), channel_id=1, source_target_pairs={{0,32},{16,48},{32,0},{48,16},{1,33},{17,49},{33,1},{49,17},{2,34}... | collective-permute-start | bytes 393224 | tf_op jit(solution)/shard_map/ppermute | solution.py:485
  85.9 3.7 %collective-permute-start.18 = (bf16[4,4,32,128]{3,2,1,0:T(8,128)(2,1)S(1)}, bf16[4,4,32,128]{3,2,1,0:T(8,128)(2,1)S(1)}, u32[]{:S(2)}, u32[]{:S(2)}) collective-permute-start(bf16[4,4,32,128]{3,2,1,0:T(8,128)(2,1)S(1)} %get-tuple-element.373), channel_id=1, source_target_pairs={{0,8},{4,12},{8,0},{12,4},{1,9},{5,13},{9,1},{13,5},{2,10},{6,14},... | collective-permute-start | bytes 393224 | tf_op jit(solution)/shard_map/ppermute | solution.py:485
  90.8 24.9 %collective-permute-done.15.arrived = bf16[4,8,1024]{2,1,0:T(8,128)(2,1)S(1)} collective-permute-done((bf16[4,8,1024]{2,1,0:T(8,128)(2,1)S(1)}, bf16[4,8,1024]{2,1,0:T(8,128)(2,1)S(1)}, u32[]{:S(2)}, u32[]{:S(2)}) %collective-permute-start.15) | collective-permute-done | bytes 65568 | tf_op jit(solution)/shard_map/ppermute | solution.py:481
  115.8 5.4 %backward_tick.16 = (bf16[4,8,1024]{2,1,0:T(8,128)(2,1)S(1)}, bf16[16,8,2048]{2,1,0:T(8,128)(2,1)S(1)}, bf16[16,8,2048]{2,1,0:T(8,128)(2,1)S(1)}, f32[16,8,4096]...) custom-call(s32[4]{0:T(128)S(1)} %pad_add_fusion.place, ...), custom_call_target="tpu_custom_call", output_to_operand_aliasing={{1}: (4, {}), {2}: (5, {}), {3}: (6, {}), {4}: (7, {}), {5}... | custom-call | tf_op jit(solution)/shard_map/backward_tick/pallas_call | solution.py:473
  124.9 3.5 %collective-permute-done.17.arrived = bf16[4,8,1024]{2,1,0:T(8,128)(2,1)S(1)} collective-permute-done((bf16[4,8,1024]{2,1,0:T(8,128)(2,1)S(1)}, bf16[4,8,1024]{2,1,0:T(8,128)(2,1)S(1)}, u32[]{:S(2)}, u32[]{:S(2)}) %collective-permute-start.17) | collective-permute-done | bytes 65568 | tf_op jit(solution)/shard_map/ppermute | solution.py:481
  128.4 5.5 %backward_tick.17 = (bf16[4,8,1024]{2,1,0:T(8,128)(2,1)S(1)}, bf16[16,8,2048]{2,1,0:T(8,128)(2,1)S(1)}, bf16[16,8,2048]{2,1,0:T(8,128)(2,1)S(1)}, f32[16,8,4096]...) custom-call(s32[4]{0:T(128)S(1)} %pad_add_fusion.place, ...), custom_call_target="tpu_custom_call", output_to_operand_aliasing={{1}: (4, {}), {2}: (5, {}), {3}: (6, {}), {4}: (7, {}), {5}... | custom-call | tf_op jit(solution)/shard_map/backward_tick/pallas_call | solution.py:473
  137.8 6.0 %backward_tick.18 = (bf16[4,8,1024]{2,1,0:T(8,128)(2,1)}, bf16[16,8,2048]{2,1,0:T(8,128)(2,1)S(1)}, bf16[16,8,2048]{2,1,0:T(8,128)(2,1)S(1)}, f32[16,8,4096]{2,1...) custom-call(s32[4]{0:T(128)S(1)} %pad_add_fusion.place, ...), custom_call_target="tpu_custom_call", output_to_operand_aliasing={{1}: (4, {}), {2}: (5, {}), {3}: (6, {}), {4}: (7, {}), {5}... | custom-call | tf_op jit(solution)/shard_map/backward_tick/pallas_call | solution.py:473
  143.8 3.0 %collective-permute-done.21.arrived = bf16[4,8,1024]{2,1,0:T(8,128)(2,1)S(1)} collective-permute-done((bf16[4,8,1024]{2,1,0:T(8,128)(2,1)S(1)}, bf16[4,8,1024]{2,1,0:T(8,128)(2,1)S(1)}, u32[]{:S(2)}, u32[]{:S(2)}) %collective-permute-start.21) | collective-permute-done | bytes 65568 | tf_op jit(solution)/shard_map/ppermute | solution.py:481
  146.8 4.8 %backward_tick.19 = (bf16[4,8,1024]{2,1,0:T(8,128)(2,1)}, bf16[16,8,2048]{2,1,0:T(8,128)(2,1)S(1)}, bf16[16,8,2048]{2,1,0:T(8,128)(2,1)S(1)}, f32[16,8,4096]{2,1...) custom-call(s32[4]{0:T(128)S(1)} %pad_add_fusion.place, ...), custom_call_target="tpu_custom_call", output_to_operand_aliasing={{1}: (4, {}), {2}: (5, {}), {3}: (6, {}), {4}: (7, {}), {5}... | custom-call | tf_op jit(solution)/shard_map/backward_tick/pallas_call | solution.py:473
  157.3 9.2 %collective-permute-done.24.rest_12_ = bf16[16,8,2048]{2,1,0:T(8,128)(2,1)S(1)} collective-permute-done((bf16[16,8,2048]{2,1,0:T(8,128)(2,1)S(1)}, bf16[16,8,2048]{2,1,0:T(8,128)(2,1)S(1)}, u32[]{:S(2)}, u32[]{:S(2)}) %collective-permute-start.24) | collective-permute-done | bytes 524320 | tf_op jit(solution)/shard_map/ppermute | solution.py:468
  168.8 6.8 %collective-permute-done.22.rest_10_ = bf16[16,8,2048]{2,1,0:T(8,128)(2,1)S(1)} collective-permute-done((bf16[16,8,2048]{2,1,0:T(8,128)(2,1)S(1)}, bf16[16,8,2048]{2,1,0:T(8,128)(2,1)S(1)}, u32[]{:S(2)}, u32[]{:S(2)}) %collective-permute-start.22) | collective-permute-done | bytes 524320 | tf_op jit(solution)/shard_map/ppermute | solution.py:468
  178.3 5.1 %combine.1 = (f32[4,32,2048]{2,1,0:T(8,128)S(1)}, f32[4,32,2048]{2,1,0:T(8,128)S(1)}, f32[1,4096]{1,0:T(1,128)S(1)}, bf16[144,2048]{1,0:T(8,128)(2,1)S(1)}, bf16...) custom-call(s32[4]{0:T(128)S(1)} %pad_add_fusion.place, ...), custom_call_target="tpu_custom_call" | custom-call | tf_op jit(solution)/shard_map/combine/pallas_call | solution.py:492
  189.1 2.9 %collective-permute-start.32 = (bf16[144,2048]{1,0:T(8,128)(2,1)S(1)}, bf16[144,2048]{1,0:T(8,128)(2,1)S(1)}, u32[]{:S(2)}, u32[]{:S(2)}) collective-permute-start(bf16[144,2048]{1,0:T(8,128)(2,1)S(1)} %get-tuple-element.424), channel_id=1, source_target_pairs={{0,32},{16,48},{32,0},{48,16},{1,33},{17,49},{33,1},{49,17},{2,34}... | collective-permute-start | bytes 1769480 | tf_op jit(solution)/shard_map/ppermute | solution.py:468
  192.1 17.9 %collective-permute-done.28.rest_0_ = bf16[144,2048]{1,0:T(8,128)(2,1)S(1)} collective-permute-done((bf16[144,2048]{1,0:T(8,128)(2,1)S(1)}, bf16[144,2048]{1,0:T(8,128)(2,1)S(1)}, u32[]{:S(2)}, u32[]{:S(2)}) %collective-permute-start.28) | collective-permute-done | bytes 589856 | tf_op jit(solution)/shard_map/ppermute | solution.py:468
  213.8 6.0 %collective-permute-done.33.rest_5_ = bf16[144,2048]{1,0:T(8,128)(2,1)S(1)} collective-permute-done((bf16[144,2048]{1,0:T(8,128)(2,1)S(1)}, bf16[144,2048]{1,0:T(8,128)(2,1)S(1)}, u32[]{:S(2)}, u32[]{:S(2)}) %collective-permute-start.33) | collective-permute-done | bytes 589856 | tf_op jit(solution)/shard_map/ppermute | solution.py:468
  221.0 2.8 %collective-permute-start.34 = (bf16[80,4096]{1,0:T(8,128)(2,1)S(1)}, bf16[80,4096]{1,0:T(8,128)(2,1)S(1)}, u32[]{:S(2)}, u32[]{:S(2)}) collective-permute-start(bf16[80,4096]{1,0:T(8,128)(2,1)S(1)} %get-tuple-element.428), channel_id=1, source_target_pairs={{0,64},{64,0},{1,65},{65,1},{2,66},{66,2},{3,67},{67,3},{4,68},{68... | collective-permute-start | bytes 1966088 | tf_op jit(solution)/shard_map/ppermute | solution.py:506
  225.0 8.1 %collective-permute-done.34.arrived = bf16[80,4096]{1,0:T(8,128)(2,1)S(1)} collective-permute-done((bf16[80,4096]{1,0:T(8,128)(2,1)S(1)}, bf16[80,4096]{1,0:T(8,128)(2,1)S(1)}, u32[]{:S(2)}, u32[]{:S(2)}) %collective-permute-start.34) | collective-permute-done | bytes 655392 | tf_op jit(solution)/shard_map/ppermute | solution.py:506
  (80 shorter events, 58.9 us)
Async XLA Ops:
  13.6 10.6 %collective-permute-start.1 = (bf16[4,8,1024]{2,1,0:T(8,128)(2,1)S(1)}, bf16[4,8,1024]{2,1,0:T(8,128)(2,1)S(1)}, u32[]{:S(2)}, u32[]{:S(2)}) collective-permute-start(bf16[4,8,1024]{2,1,0:T(8,128)(2,1)S(1)} %get-tuple-element.219.rest_0_), channel_id=1, source_target_pairs={{0,1},{4,5},{8,9},{12,13},{16,17},{20,21},{24,25},{28,29},{32,33},... | collective-permute-start | bytes 196616 | tf_op jit(solution)/shard_map/ppermute | solution.py:435
  22.9 10.1 %collective-permute-start = (bf16[4,8,1024]{2,1,0:T(8,128)(2,1)S(1)}, bf16[4,8,1024]{2,1,0:T(8,128)(2,1)S(1)}, u32[]{:S(2)}, u32[]{:S(2)}) collective-permute-start(bf16[4,8,1024]{2,1,0:T(8,128)(2,1)S(1)} %get-tuple-element.228), channel_id=1, source_target_pairs={{0,1},{4,5},{8,9},{12,13},{16,17},{20,21},{24,25},{28,29},{32,33},... | collective-permute-start | bytes 196616 | tf_op jit(solution)/shard_map/ppermute | solution.py:435
  31.7 10.6 %collective-permute-start.3 = (bf16[4,8,1024]{2,1,0:T(8,128)(2,1)S(1)}, bf16[4,8,1024]{2,1,0:T(8,128)(2,1)S(1)}, u32[]{:S(2)}, u32[]{:S(2)}) collective-permute-start(bf16[4,8,1024]{2,1,0:T(8,128)(2,1)S(1)} %get-tuple-element.246), channel_id=1, source_target_pairs={{0,1},{1,2},{4,5},{5,6},{8,9},{9,10},{12,13},{13,14},{16,17},{17,1... | collective-permute-start | bytes 196616 | tf_op jit(solution)/shard_map/ppermute | solution.py:435
  46.8 8.4 %collective-permute-start.6 = (bf16[4,8,1024]{2,1,0:T(8,128)(2,1)S(1)}, bf16[4,8,1024]{2,1,0:T(8,128)(2,1)S(1)}, u32[]{:S(2)}, u32[]{:S(2)}) collective-permute-start(bf16[4,8,1024]{2,1,0:T(8,128)(2,1)S(1)} %get-tuple-element.281), channel_id=1, source_target_pairs={{2,3},{6,7},{10,11},{14,15},{18,19},{22,23},{26,27},{30,31},{34,35... | collective-permute-start | bytes 196616 | tf_op jit(solution)/shard_map/ppermute | solution.py:435
  82.0 33.8 %collective-permute-start.16 = (bf16[4,4,32,128]{3,2,1,0:T(8,128)(2,1)S(1)}, bf16[4,4,32,128]{3,2,1,0:T(8,128)(2,1)S(1)}, u32[]{:S(2)}, u32[]{:S(2)}) collective-permute-start(bf16[4,4,32,128]{3,2,1,0:T(8,128)(2,1)S(1)} %get-tuple-element.360), channel_id=1, source_target_pairs={{0,4},{4,8},{8,12},{12,0},{1,5},{5,9},{9,13},{13,1},{2,6},{6,10},{... | collective-permute-start | bytes 393224 | tf_op jit(solution)/shard_map/ppermute | solution.py:485
  84.0 31.8 %collective-permute-start.15 = (bf16[4,8,1024]{2,1,0:T(8,128)(2,1)S(1)}, bf16[4,8,1024]{2,1,0:T(8,128)(2,1)S(1)}, u32[]{:S(2)}, u32[]{:S(2)}) collective-permute-start(bf16[4,8,1024]{2,1,0:T(8,128)(2,1)S(1)} %get-tuple-element.358), channel_id=1, source_target_pairs={{1,0},{2,1},{5,4},{6,5},{9,8},{10,9},{13,12},{14,13},{17,16},{18,1... | collective-permute-start | bytes 196616 | tf_op jit(solution)/shard_map/ppermute | solution.py:481
  85.9 42.5 %collective-permute-start.18 = (bf16[4,4,32,128]{3,2,1,0:T(8,128)(2,1)S(1)}, bf16[4,4,32,128]{3,2,1,0:T(8,128)(2,1)S(1)}, u32[]{:S(2)}, u32[]{:S(2)}) collective-permute-start(bf16[4,4,32,128]{3,2,1,0:T(8,128)(2,1)S(1)} %get-tuple-element.373), channel_id=1, source_target_pairs={{0,8},{4,12},{8,0},{12,4},{1,9},{5,13},{9,1},{13,5},{2,10},{6,14},... | collective-permute-start | bytes 393224 | tf_op jit(solution)/shard_map/ppermute | solution.py:485
  89.6 38.8 %collective-permute-start.17 = (bf16[4,8,1024]{2,1,0:T(8,128)(2,1)S(1)}, bf16[4,8,1024]{2,1,0:T(8,128)(2,1)S(1)}, u32[]{:S(2)}, u32[]{:S(2)}) collective-permute-start(bf16[4,8,1024]{2,1,0:T(8,128)(2,1)S(1)} %get-tuple-element.371), channel_id=1, source_target_pairs={{1,0},{2,1},{5,4},{6,5},{9,8},{10,9},{13,12},{14,13},{17,16},{18,1... | collective-permute-start | bytes 196616 | tf_op jit(solution)/shard_map/ppermute | solution.py:481
  121.1 16.6 %collective-permute-start.20 = (bf16[4,4,32,128]{3,2,1,0:T(8,128)(2,1)S(1)}, bf16[4,4,32,128]{3,2,1,0:T(8,128)(2,1)S(1)}, u32[]{:S(2)}, u32[]{:S(2)}) collective-permute-start(bf16[4,4,32,128]{3,2,1,0:T(8,128)(2,1)S(1)} %get-tuple-element.386), channel_id=1, source_target_pairs={{0,12},{4,0},{8,4},{12,8},{1,13},{5,1},{9,5},{13,9},{2,14},{6,2},{... | collective-permute-start | bytes 393224 | tf_op jit(solution)/shard_map/ppermute | solution.py:485
  123.6 14.2 %collective-permute-start.19 = (bf16[4,8,1024]{2,1,0:T(8,128)(2,1)S(1)}, bf16[4,8,1024]{2,1,0:T(8,128)(2,1)S(1)}, u32[]{:S(2)}, u32[]{:S(2)}) collective-permute-start(bf16[4,8,1024]{2,1,0:T(8,128)(2,1)S(1)} %get-tuple-element.384), channel_id=1, source_target_pairs={{1,0},{5,4},{9,8},{13,12},{17,16},{21,20},{25,24},{29,28},{33,32},... | collective-permute-start | bytes 196616 | tf_op jit(solution)/shard_map/ppermute | solution.py:481
  133.9 12.9 %collective-permute-start.21 = (bf16[4,8,1024]{2,1,0:T(8,128)(2,1)S(1)}, bf16[4,8,1024]{2,1,0:T(8,128)(2,1)S(1)}, u32[]{:S(2)}, u32[]{:S(2)}) collective-permute-start(bf16[4,8,1024]{2,1,0:T(8,128)(2,1)S(1)} %get-tuple-element.397), channel_id=1, source_target_pairs={{1,0},{5,4},{9,8},{13,12},{17,16},{21,20},{25,24},{29,28},{33,32},... | collective-permute-start | bytes 196616 | tf_op jit(solution)/shard_map/ppermute | solution.py:481
  151.7 14.9 %collective-permute-start.24 = (bf16[16,8,2048]{2,1,0:T(8,128)(2,1)S(1)}, bf16[16,8,2048]{2,1,0:T(8,128)(2,1)S(1)}, u32[]{:S(2)}, u32[]{:S(2)}) collective-permute-start(bf16[16,8,2048]{2,1,0:T(8,128)(2,1)S(1)} %get-tuple-element.415.rest_8_), channel_id=1, source_target_pairs={{0,48},{16,0},{32,16},{48,32},{1,49},{17,1},{33,17},{49,33},{2,50}... | collective-permute-start | bytes 1572872 | tf_op jit(solution)/shard_map/ppermute | solution.py:468
  152.4 16.4 %collective-permute-start.23 = (bf16[16,8,2048]{2,1,0:T(8,128)(2,1)S(1)}, bf16[16,8,2048]{2,1,0:T(8,128)(2,1)S(1)}, u32[]{:S(2)}, u32[]{:S(2)}) collective-permute-start(bf16[16,8,2048]{2,1,0:T(8,128)(2,1)S(1)} %get-tuple-element.415.rest_8_), channel_id=1, source_target_pairs={{0,32},{16,48},{32,0},{48,16},{1,33},{17,49},{33,1},{49,17},{2,34}... | collective-permute-start | bytes 1572872 | tf_op jit(solution)/shard_map/ppermute | solution.py:468
  154.7 20.9 %collective-permute-start.22 = (bf16[16,8,2048]{2,1,0:T(8,128)(2,1)S(1)}, bf16[16,8,2048]{2,1,0:T(8,128)(2,1)S(1)}, u32[]{:S(2)}, u32[]{:S(2)}) collective-permute-start(bf16[16,8,2048]{2,1,0:T(8,128)(2,1)S(1)} %get-tuple-element.415.rest_8_), channel_id=1, source_target_pairs={{0,16},{16,32},{32,48},{48,0},{1,17},{17,33},{33,49},{49,1},{2,18}... | collective-permute-start | bytes 1572872 | tf_op jit(solution)/shard_map/ppermute | solution.py:468
  154.8 20.8 %collective-permute-start.27 = (bf16[16,8,2048]{2,1,0:T(8,128)(2,1)S(1)}, bf16[16,8,2048]{2,1,0:T(8,128)(2,1)S(1)}, u32[]{:S(2)}, u32[]{:S(2)}) collective-permute-start(bf16[16,8,2048]{2,1,0:T(8,128)(2,1)S(1)} %get-tuple-element.416.rest_9_), channel_id=1, source_target_pairs={{0,12},{4,0},{8,4},{12,8},{1,13},{5,1},{9,5},{13,9},{2,14},{6,2},{... | collective-permute-start | bytes 1572872 | tf_op jit(solution)/shard_map/ppermute | solution.py:468
  155.8 19.8 %collective-permute-start.26 = (bf16[16,8,2048]{2,1,0:T(8,128)(2,1)S(1)}, bf16[16,8,2048]{2,1,0:T(8,128)(2,1)S(1)}, u32[]{:S(2)}, u32[]{:S(2)}) collective-permute-start(bf16[16,8,2048]{2,1,0:T(8,128)(2,1)S(1)} %get-tuple-element.416.rest_9_), channel_id=1, source_target_pairs={{0,8},{4,12},{8,0},{12,4},{1,9},{5,13},{9,1},{13,5},{2,10},{6,14},... | collective-permute-start | bytes 1572872 | tf_op jit(solution)/shard_map/ppermute | solution.py:468
  166.5 11.8 %collective-permute-start.25 = (bf16[16,8,2048]{2,1,0:T(8,128)(2,1)S(1)}, bf16[16,8,2048]{2,1,0:T(8,128)(2,1)S(1)}, u32[]{:S(2)}, u32[]{:S(2)}) collective-permute-start(bf16[16,8,2048]{2,1,0:T(8,128)(2,1)S(1)} %get-tuple-element.416.rest_9_), channel_id=1, source_target_pairs={{0,4},{4,8},{8,12},{12,0},{1,5},{5,9},{9,13},{13,1},{2,6},{6,10},{... | collective-permute-start | bytes 1572872 | tf_op jit(solution)/shard_map/ppermute | solution.py:468
  183.5 26.4 %collective-permute-start.28 = (bf16[144,2048]{1,0:T(8,128)(2,1)S(1)}, bf16[144,2048]{1,0:T(8,128)(2,1)S(1)}, u32[]{:S(2)}, u32[]{:S(2)}) collective-permute-start(bf16[144,2048]{1,0:T(8,128)(2,1)S(1)} %get-tuple-element.420), channel_id=1, source_target_pairs={{0,4},{4,8},{8,12},{12,0},{1,5},{5,9},{9,13},{13,1},{2,6},{6,10},{... | collective-permute-start | bytes 1769480 | tf_op jit(solution)/shard_map/ppermute | solution.py:468
  183.5 28.1 %collective-permute-start.29 = (bf16[144,2048]{1,0:T(8,128)(2,1)S(1)}, bf16[144,2048]{1,0:T(8,128)(2,1)S(1)}, u32[]{:S(2)}, u32[]{:S(2)}) collective-permute-start(bf16[144,2048]{1,0:T(8,128)(2,1)S(1)} %get-tuple-element.421), channel_id=1, source_target_pairs={{0,8},{4,12},{8,0},{12,4},{1,9},{5,13},{9,1},{13,5},{2,10},{6,14},... | collective-permute-start | bytes 1769480 | tf_op jit(solution)/shard_map/ppermute | solution.py:468
  185.5 26.1 %collective-permute-start.30 = (bf16[144,2048]{1,0:T(8,128)(2,1)S(1)}, bf16[144,2048]{1,0:T(8,128)(2,1)S(1)}, u32[]{:S(2)}, u32[]{:S(2)}) collective-permute-start(bf16[144,2048]{1,0:T(8,128)(2,1)S(1)} %get-tuple-element.422), channel_id=1, source_target_pairs={{0,12},{4,0},{8,4},{12,8},{1,13},{5,1},{9,5},{13,9},{2,14},{6,2},{... | collective-permute-start | bytes 1769480 | tf_op jit(solution)/shard_map/ppermute | solution.py:468
  187.6 24.0 %collective-permute-start.31 = (bf16[144,2048]{1,0:T(8,128)(2,1)S(1)}, bf16[144,2048]{1,0:T(8,128)(2,1)S(1)}, u32[]{:S(2)}, u32[]{:S(2)}) collective-permute-start(bf16[144,2048]{1,0:T(8,128)(2,1)S(1)} %get-tuple-element.423), channel_id=1, source_target_pairs={{0,16},{16,32},{32,48},{48,0},{1,17},{17,33},{33,49},{49,1},{2,18}... | collective-permute-start | bytes 1769480 | tf_op jit(solution)/shard_map/ppermute | solution.py:468
  189.1 24.6 %collective-permute-start.32 = (bf16[144,2048]{1,0:T(8,128)(2,1)S(1)}, bf16[144,2048]{1,0:T(8,128)(2,1)S(1)}, u32[]{:S(2)}, u32[]{:S(2)}) collective-permute-start(bf16[144,2048]{1,0:T(8,128)(2,1)S(1)} %get-tuple-element.424), channel_id=1, source_target_pairs={{0,32},{16,48},{32,0},{48,16},{1,33},{17,49},{33,1},{49,17},{2,34}... | collective-permute-start | bytes 1769480 | tf_op jit(solution)/shard_map/ppermute | solution.py:468
  209.9 9.9 %collective-permute-start.33 = (bf16[144,2048]{1,0:T(8,128)(2,1)S(1)}, bf16[144,2048]{1,0:T(8,128)(2,1)S(1)}, u32[]{:S(2)}, u32[]{:S(2)}) collective-permute-start(bf16[144,2048]{1,0:T(8,128)(2,1)S(1)} %get-tuple-element.425), channel_id=1, source_target_pairs={{0,48},{16,0},{32,16},{48,32},{1,49},{17,1},{33,17},{49,33},{2,50}... | collective-permute-start | bytes 1769480 | tf_op jit(solution)/shard_map/ppermute | solution.py:468
  221.0 12.2 %collective-permute-start.34 = (bf16[80,4096]{1,0:T(8,128)(2,1)S(1)}, bf16[80,4096]{1,0:T(8,128)(2,1)S(1)}, u32[]{:S(2)}, u32[]{:S(2)}) collective-permute-start(bf16[80,4096]{1,0:T(8,128)(2,1)S(1)} %get-tuple-element.428), channel_id=1, source_target_pairs={{0,64},{64,0},{1,65},{65,1},{2,66},{66,2},{3,67},{67,3},{4,68},{68... | collective-permute-start | bytes 1966088 | tf_op jit(solution)/shard_map/ppermute | solution.py:506
  (14 other events, 57.6 us)

commit v2 on v1

--- a/solution.py
+++ b/solution.py
@@ -10,8 +10,8 @@
 BLOCK = 4
 LAG = 2
 WIDE = 1024
-COLS = 512
-WHOLE = (2,)
+COLS = 256
+WHOLE = ()
 CHUNK = 256
 PANEL = 256
 SLOTS = 4
@@ -132,13 +132,19 @@
         def _():
             load_wr.wait()
 
-    turns = (0, 1, idle + blocks - 2, idle + blocks - 1)
+    top = stages - 1
+    turns = {
+        0: (stage >= top - 1, 0),
+        1: (stage == top, 1),
+        idle + blocks - 2: (stage < top, jnp.where(stage == top - 1, 1, 0)),
+        idle + blocks - 1: (stage < top - 1, 1),
+    }
     if tick in turns:
-        late = turns.index(tick) // 2
-
-        @pl.when((stage < stages // 2) == (late == 1))
+        here, share = turns[tick]
+
+        @pl.when(here)
         def _():
-            turn(turns.index(tick) % 2, 2, pairs, staged, sems)
+            turn(share, 2, pairs, staged, sems)
 
     if last:
         load = pltpu.make_async_copy(wrt_far, rest[9], load_sems.at[0])
@@ -308,7 +314,7 @@
     lefts = (rest[:4], rest[4:8])
     dy, dz = rest[8:10]
     arrivals = (rest[10:13], rest[13:16])
-    own_y, own_z, bias, *sends = rest[16:-2]
+    own_y, own_z, bias, *outs = rest[16:-2]
     left_all, right = rest[-2:]
     y, z = place[1], place[2]
     total, rows, half = dy.shape
@@ -328,28 +334,53 @@
             block = right[:, cols]
             sums = dot(ones, block)[:1]
             bias[:, pl.ds(pl.multiple_of(at + side * half, COLS), COLS)] = sums
-            extra = as_rows(sums)
+            up, down, first, second = outs[4 * side : 4 * side + 4]
             for d in range(4):
                 left = left_all[:, lax.rem(other + d, 4)].reshape(4 * fine, 4 * n)
                 part = dot(left, block)
                 if d == 0:
                     own[:, :, cols] = part.reshape(4, fine, COLS)
+                elif d == 2:
+                    first[:, cols] = part[: 2 * fine].astype(jnp.bfloat16)
+                    second[pl.ds(0, 2 * fine), cols] = part[2 * fine :].astype(jnp.bfloat16)
+                    second[pl.ds(2 * fine, EXTRA), cols] = as_rows(sums)
                 else:
-                    to = sends[3 * side + d - 1]
-                    to[pl.ds(0, 4 * fine), cols] = part.astype(jnp.bfloat16)
-                    to[pl.ds(4 * fine, EXTRA), cols] = extra
+                    to = up if d == 1 else down
+                    to[:, cols] = part
             return carry
 
         lax.fori_loop(0, half // COLS, columns, 0)
 
 
+def relay_kernel(place, bias, *rest):
+    outs = rest[8:]
+    for side in range(2):
+        up, down, first, second = rest[4 * side : 4 * side + 4]
+        ahead, behind = outs[2 * side : 2 * side + 2]
+        n, half = first.shape
+        def columns(step, carry, side=side, up=up, down=down, first=first, second=second, ahead=ahead, behind=behind):
+            start = pl.multiple_of(step * COLS, COLS)
+            cols = pl.ds(start, COLS)
+            sums = bias[:, pl.ds(pl.multiple_of(side * half + start, COLS), COLS)]
+            top, bottom = pl.ds(0, n), pl.ds(n, n)
+            ahead[top, cols] = (up[top, cols] + first[:, cols].astype(jnp.float32)).astype(jnp.bfloat16)
+            ahead[bottom, cols] = up[bottom, cols].astype(jnp.bfloat16)
+            ahead[pl.ds(2 * n, EXTRA), cols] = as_rows(sums)
+            behind[top, cols] = down[top, cols].astype(jnp.bfloat16)
+            behind[bottom, cols] = (down[bottom, cols] + second[top, cols].astype(jnp.float32)).astype(jnp.bfloat16)
+            behind[pl.ds(2 * n, EXTRA), cols] = as_rows(sums + from_rows(second[pl.ds(n, EXTRA), cols]))
+            return carry
+
+        lax.fori_loop(0, half // COLS, columns, 0)
+
+
 def finish_kernel(place, own_y, own_z, bias, *rest):
-    arrivals, keep, kept_bias, give = rest[:6], rest[6], rest[7], rest[8]
+    arrivals, keep, kept_bias, give = rest[:4], rest[4], rest[5], rest[6]
     xh = place[3]
     fine, half = own_y.shape[1:]
     for side, own in enumerate((own_y, own_z)):
         cols = pl.ds(side * half, half)
-        blocks = arrivals[3 * side : 3 * side + 3]
+        blocks = arrivals[2 * side : 2 * side + 2]
         for n in range(2):
             mine, other = 2 * n + xh, 2 * n + 1 - xh
             kept, given = own[mine], own[other]
@@ -488,21 +519,29 @@
             lefts.append(piece)
     dy, dz = held[:2]
     final_hidden, final_cell = hs[total], held[3][total]
-    part, whole = shape((4 * fine + EXTRA, half), bf16), shape((4, fine, half), f32)
-    mine_y, mine_z, bias, *sends = simple(
+    whole, far_part = shape((4, fine, half), f32), shape((4 * fine, half), f32)
+    pieces = (far_part, far_part, shape((2 * fine, half), bf16), shape((2 * fine + EXTRA, half), bf16))
+    mine_y, mine_z, bias, *made = simple(
         combine_kernel,
         "combine",
-        (whole, whole, shape((1, gated), f32)) + (part,) * 6,
+        (whole, whole, shape((1, gated), f32)) + pieces * 2,
         16,
         [pltpu.VMEM((4, 4, fine, 4 * total * rows), bf16), pltpu.VMEM((4 * total * rows, half), bf16)],
     )(place, spread[0], *lefts[:3], spread[4], *lefts[3:], dy, dz, *passed([dy] * 3 + [dz] * 3))
-    got = passed(sends[3:] + sends[:3])
+
+    def both_ways(ahead_z, behind_z, ahead_y, behind_y):
+        sent = ((ahead_z, "z", 0), (behind_z, "z", 2), (ahead_y, "y", 0), (behind_y, "y", 2))
+        return [near(lax.ppermute(v, axis, routes[d])) for v, axis, d in sent]
+
+    got = both_ways(made[2], made[3], made[6], made[7])
+    part = shape((4 * fine + EXTRA, half), bf16)
+    sends = simple(relay_kernel, "relay", (part,) * 4, 9)(place, bias, *made[:2], *got[:2], *made[4:6], *got[2:])
     keep, bias, give = simple(
         finish_kernel,
         "finish",
         (shape((2, fine, gated), f32), shape((1, gated), f32), shape((2 * fine + EXTRA, gated), bf16)),
-        9,
-    )(place, mine_y, mine_z, bias, *got[3:], *got[:3])
+        7,
+    )(place, mine_y, mine_z, bias, *both_ways(*sends))
     other = near(lax.ppermute(give, "xh", [(0, 1), (1, 0)]))
     made = jax.ShapeDtypeStruct
     grad_i, grad_r, grad_b = simple(

time: 235 us -> 233 us (level)
  waiting for transfers between devices: 88.6 us -> 77.1 us
  starting transfers between devices: 49.5 us -> 55.4 us
  Pallas kernels: 91.9 us -> 95.2 us
    ppermute x12 -> x6, waiting for transfers between devices: 46.3 us -> 21 us  [passed(): lax.ppermute(made[n], 'y' if n < 3 else 'z', routes[n % 3])]
    ppermute x0 -> x8, starting transfers between devices: none -> 16.1 us  [both_ways(): return [near(lax.ppermute(v, axis, routes[d])) for v, axis, d in sent]]
    ppermute x0 -> x8, waiting for transfers between devices: none -> 14.8 us  [both_ways(): return [near(lax.ppermute(v, axis, routes[d])) for v, axis, d in sent]]
    ppermute x12 -> x6, starting transfers between devices: 16.7 us -> 5.75 us  [passed(): lax.ppermute(made[n], 'y' if n < 3 else 'z', routes[n % 3])]
  transfers between devices with their start and end apart: 35 -> 37, of which waited for: 13 -> 15; matrix products, arithmetic and copies ran while one was open for 1% -> 1% of each run, Pallas kernels for 23% -> 24%
where the time goes in v2:
time: 233 us; the launch traced here: 232 us
  Pallas kernels  95.2 us (41%)
  waiting for transfers between devices  77.1 us (33%)
  starting transfers between devices  55.4 us (24%)
  local copies, waits for them, and re-layouts  3.62 us (2%)
    pallas_call x10, Pallas kernels, local(): emitted, *held = forward(tick)(place, inputs, gate_bias, lens, *got)  55.3 us
    ppermute x8, waiting for transfers between devices, local(): lax.ppermute(lower, 'pipe', [(s, s - 1) for s in on])  33.3 us
    pallas_call x10, Pallas kernels, local(): backward(tick)(place, cot, landed.get(tick, lower), lens, *held)  28.4 us
    ppermute x6, waiting for transfers between devices, passed(): lax.ppermute(made[n], 'y' if n < 3 else 'z', routes[n % 3])  21 us
    ppermute x8, starting transfers between devices, both_ways(): return [near(lax.ppermute(v, axis, routes[d])) for v, axis, d in sent]  16.1 us
    ppermute x8, waiting for transfers between devices, both_ways(): return [near(lax.ppermute(v, axis, routes[d])) for v, axis, d in sent]  14.8 us
    ppermute x6, starting transfers between devices, local(): piece = lax.ppermute(piece, axis, routes[d - 1])  14.4 us
    ppermute x8, starting transfers between devices, local(): lax.ppermute(lower, 'pipe', [(s, s - 1) for s in on])  8.16 us
  transfers between devices with their start and end apart: 37, of which 15 were waited for; matrix products, arithmetic and copies ran while one was open for 1% of the time, Pallas kernels for 24%

profile of v2, /device:TPU:0, one launch (start us, length us, event | category | flops | bytes accessed | tf_op | source)
XLA Modules:
  0.0 232.4 jit_solution(5529691556352259481)
XLA Ops:
  3.1 10.5 %forward_tick.10 = (bf16[4,8,1024]{2,1,0:T(8,128)(2,1)S(1)}, bf16[1024,4096]{1,0:T(8,128)(2,1)S(1)}, bf16[1024,4096]{1,0:T(8,128)(2,1)S(1)}, bf16[16,8,1024]{2,1...) custom-call(s32[4]{0:T(128)S(1)} %pad_add_fusion.place, ...), custom_call_target="tpu_custom_call" | custom-call | tf_op jit(solution)/shard_map/forward_tick/pallas_call | solution.py:463
  14.9 8.0 %forward_tick.11 = (bf16[4,8,1024]{2,1,0:T(8,128)(2,1)S(1)}, bf16[1024,4096]{1,0:T(8,128)(2,1)S(1)}, bf16[1024,4096]{1,0:T(8,128)(2,1)S(1)}, bf16[16,8,1024]{2,1...) custom-call(s32[4]{0:T(128)S(1)} %pad_add_fusion.place, ...), custom_call_target="tpu_custom_call", output_to_operand_aliasing={{1}: (5, {}), {2}: (6, {}), {3}: (7, {}), {4}: (8, {}), {5}... | custom-call | tf_op jit(solution)/shard_map/forward_tick/pallas_call | solution.py:463
  24.2 8.0 %forward_tick.12 = (bf16[4,8,1024]{2,1,0:T(8,128)(2,1)S(1)}, bf16[1024,4096]{1,0:T(8,128)(2,1)S(1)}, bf16[1024,4096]{1,0:T(8,128)(2,1)S(1)}, bf16[16,8,1024]{2,1...) custom-call(s32[4]{0:T(128)S(1)} %pad_add_fusion.place, ...), custom_call_target="tpu_custom_call", output_to_operand_aliasing={{1}: (5, {}), {2}: (6, {}), {3}: (7, {}), {4}: (8, {}), {5}... | custom-call | tf_op jit(solution)/shard_map/forward_tick/pallas_call | solution.py:463
  33.6 8.0 %forward_tick.13 = (bf16[4,8,1024]{2,1,0:T(8,128)(2,1)S(1)}, bf16[1024,4096]{1,0:T(8,128)(2,1)S(1)}, bf16[1024,4096]{1,0:T(8,128)(2,1)S(1)}, bf16[16,8,1024]{2,1...) custom-call(s32[4]{0:T(128)S(1)} %pad_add_fusion.place, ...), custom_call_target="tpu_custom_call", output_to_operand_aliasing={{1}: (5, {}), {2}: (6, {}), {3}: (7, {}), {4}: (8, {}), {5}... | custom-call | tf_op jit(solution)/shard_map/forward_tick/pallas_call | solution.py:463
  48.1 7.8 %forward_tick.18 = (bf16[4,8,1024]{2,1,0:T(8,128)(2,1)}, bf16[1024,4096]{1,0:T(8,128)(2,1)S(1)}, bf16[1024,4096]{1,0:T(8,128)(2,1)S(1)}, bf16[16,8,1024]{2,1,0:T...) custom-call(s32[4]{0:T(128)S(1)} %pad_add_fusion.place, ...), custom_call_target="tpu_custom_call", output_to_operand_aliasing={{1}: (5, {}), {2}: (6, {}), {3}: (7, {}), {4}: (8, {}), {5}... | custom-call | tf_op jit(solution)/shard_map/forward_tick/pallas_call | solution.py:463
  55.9 10.5 %forward_tick.19 = (bf16[4,8,1024]{2,1,0:T(8,128)(2,1)S(1)}, bf16[1024,4096]{1,0:T(8,128)(2,1)S(1)}, bf16[1024,4096]{1,0:T(8,128)(2,1)S(1)}, bf16[16,8,1024]{2,1...) custom-call(s32[4]{0:T(128)S(1)} %pad_add_fusion.place, ...), custom_call_target="tpu_custom_call", output_to_operand_aliasing={{1}: (5, {}), {2}: (6, {}), {3}: (7, {}), {4}: (8, {}), {5}... | custom-call | tf_op jit(solution)/shard_map/forward_tick/pallas_call | solution.py:463
  66.5 3.9 %backward_tick.10 = (bf16[4,8,1024]{2,1,0:T(8,128)(2,1)S(1)}, bf16[16,8,2048]{2,1,0:T(8,128)(2,1)S(1)}, bf16[16,8,2048]{2,1,0:T(8,128)(2,1)S(1)}, f32[16,8,4096]...) custom-call(s32[4]{0:T(128)S(1)} %pad_add_fusion.place, ...), custom_call_target="tpu_custom_call", output_to_operand_aliasing={{3}: (5, {}), {4}: (6, {}), {6}: (7, {})} | custom-call | tf_op jit(solution)/shard_map/backward_tick/pallas_call | solution.py:504
  86.7 3.7 %collective-permute-start.18 = (bf16[4,4,32,128]{3,2,1,0:T(8,128)(2,1)S(1)}, bf16[4,4,32,128]{3,2,1,0:T(8,128)(2,1)S(1)}, u32[]{:S(2)}, u32[]{:S(2)}) collective-permute-start(bf16[4,4,32,128]{3,2,1,0:T(8,128)(2,1)S(1)} %get-tuple-element.379), channel_id=1, source_target_pairs={{0,8},{4,12},{8,0},{12,4},{1,9},{5,13},{9,1},{13,5},{2,10},{6,14},... | collective-permute-start | bytes 393224 | tf_op jit(solution)/shard_map/ppermute | solution.py:516
  91.6 24.2 %collective-permute-done.15.arrived = bf16[4,8,1024]{2,1,0:T(8,128)(2,1)S(1)} collective-permute-done((bf16[4,8,1024]{2,1,0:T(8,128)(2,1)S(1)}, bf16[4,8,1024]{2,1,0:T(8,128)(2,1)S(1)}, u32[]{:S(2)}, u32[]{:S(2)}) %collective-permute-start.15) | collective-permute-done | bytes 65568 | tf_op jit(solution)/shard_map/ppermute | solution.py:512
  115.8 5.4 %backward_tick.16 = (bf16[4,8,1024]{2,1,0:T(8,128)(2,1)S(1)}, bf16[16,8,2048]{2,1,0:T(8,128)(2,1)S(1)}, bf16[16,8,2048]{2,1,0:T(8,128)(2,1)S(1)}, f32[16,8,4096]...) custom-call(s32[4]{0:T(128)S(1)} %pad_add_fusion.place, ...), custom_call_target="tpu_custom_call", output_to_operand_aliasing={{1}: (4, {}), {2}: (5, {}), {3}: (6, {}), {4}: (7, {}), {5}... | custom-call | tf_op jit(solution)/shard_map/backward_tick/pallas_call | solution.py:504
  124.9 3.5 %collective-permute-done.17.arrived = bf16[4,8,1024]{2,1,0:T(8,128)(2,1)S(1)} collective-permute-done((bf16[4,8,1024]{2,1,0:T(8,128)(2,1)S(1)}, bf16[4,8,1024]{2,1,0:T(8,128)(2,1)S(1)}, u32[]{:S(2)}, u32[]{:S(2)}) %collective-permute-start.17) | collective-permute-done | bytes 65568 | tf_op jit(solution)/shard_map/ppermute | solution.py:512
  128.4 5.4 %backward_tick.17 = (bf16[4,8,1024]{2,1,0:T(8,128)(2,1)S(1)}, bf16[16,8,2048]{2,1,0:T(8,128)(2,1)S(1)}, bf16[16,8,2048]{2,1,0:T(8,128)(2,1)S(1)}, f32[16,8,4096]...) custom-call(s32[4]{0:T(128)S(1)} %pad_add_fusion.place, ...), custom_call_target="tpu_custom_call", output_to_operand_aliasing={{1}: (4, {}), {2}: (5, {}), {3}: (6, {}), {4}: (7, {}), {5}... | custom-call | tf_op jit(solution)/shard_map/backward_tick/pallas_call | solution.py:504
  137.8 6.0 %backward_tick.18 = (bf16[4,8,1024]{2,1,0:T(8,128)(2,1)}, bf16[16,8,2048]{2,1,0:T(8,128)(2,1)S(1)}, bf16[16,8,2048]{2,1,0:T(8,128)(2,1)S(1)}, f32[16,8,4096]{2,1...) custom-call(s32[4]{0:T(128)S(1)} %pad_add_fusion.place, ...), custom_call_target="tpu_custom_call", output_to_operand_aliasing={{1}: (4, {}), {2}: (5, {}), {3}: (6, {}), {4}: (7, {}), {5}... | custom-call | tf_op jit(solution)/shard_map/backward_tick/pallas_call | solution.py:504
  143.8 3.2 %collective-permute-done.21.arrived = bf16[4,8,1024]{2,1,0:T(8,128)(2,1)S(1)} collective-permute-done((bf16[4,8,1024]{2,1,0:T(8,128)(2,1)S(1)}, bf16[4,8,1024]{2,1,0:T(8,128)(2,1)S(1)}, u32[]{:S(2)}, u32[]{:S(2)}) %collective-permute-start.21) | collective-permute-done | bytes 65568 | tf_op jit(solution)/shard_map/ppermute | solution.py:512
  147.0 4.8 %backward_tick.19 = (bf16[4,8,1024]{2,1,0:T(8,128)(2,1)}, bf16[16,8,2048]{2,1,0:T(8,128)(2,1)S(1)}, bf16[16,8,2048]{2,1,0:T(8,128)(2,1)S(1)}, f32[16,8,4096]{2,1...) custom-call(s32[4]{0:T(128)S(1)} %pad_add_fusion.place, ...), custom_call_target="tpu_custom_call", output_to_operand_aliasing={{1}: (4, {}), {2}: (5, {}), {3}: (6, {}), {4}: (7, {}), {5}... | custom-call | tf_op jit(solution)/shard_map/backward_tick/pallas_call | solution.py:504
  157.1 9.6 %collective-permute-done.24.rest_12_ = bf16[16,8,2048]{2,1,0:T(8,128)(2,1)S(1)} collective-permute-done((bf16[16,8,2048]{2,1,0:T(8,128)(2,1)S(1)}, bf16[16,8,2048]{2,1,0:T(8,128)(2,1)S(1)}, u32[]{:S(2)}, u32[]{:S(2)}) %collective-permute-start.24) | collective-permute-done | bytes 524320 | tf_op jit(solution)/shard_map/ppermute | solution.py:499
  169.0 7.0 %collective-permute-done.22.rest_10_ = bf16[16,8,2048]{2,1,0:T(8,128)(2,1)S(1)} collective-permute-done((bf16[16,8,2048]{2,1,0:T(8,128)(2,1)S(1)}, bf16[16,8,2048]{2,1,0:T(8,128)(2,1)S(1)}, u32[]{:S(2)}, u32[]{:S(2)}) %collective-permute-start.22) | collective-permute-done | bytes 524320 | tf_op jit(solution)/shard_map/ppermute | solution.py:499
  178.6 6.5 %combine.1 = (f32[4,32,2048]{2,1,0:T(8,128)S(1)}, f32[4,32,2048]{2,1,0:T(8,128)S(1)}, f32[1,4096]{1,0:T(1,128)S(1)}, f32[128,2048]{1,0:T(8,128)S(1)}, f32[128,20...) custom-call(s32[4]{0:T(128)S(1)} %pad_add_fusion.place, ...), custom_call_target="tpu_custom_call" | custom-call | tf_op jit(solution)/shard_map/combine/pallas_call | solution.py:524
  189.9 3.7 %collective-permute-start.30 = (bf16[64,2048]{1,0:T(8,128)(2,1)S(1)}, bf16[64,2048]{1,0:T(8,128)(2,1)S(1)}, u32[]{:S(2)}, u32[]{:S(2)}) collective-permute-start(bf16[64,2048]{1,0:T(8,128)(2,1)S(1)} %get-tuple-element.432), channel_id=1, source_target_pairs={{0,16},{16,32},{32,48},{48,0},{1,17},{17,33},{33,49},{49,1},{2,18}... | collective-permute-start | bytes 786440 | tf_op jit(solution)/shard_map/ppermute | solution.py:534
  203.4 3.8 %collective-permute-start.34 = (bf16[144,2048]{1,0:T(8,128)(2,1)S(1)}, bf16[144,2048]{1,0:T(8,128)(2,1)S(1)}, u32[]{:S(2)}, u32[]{:S(2)}) collective-permute-start(bf16[144,2048]{1,0:T(8,128)(2,1)S(1)} %get-tuple-element.436), channel_id=1, source_target_pairs={{0,16},{16,32},{32,48},{48,0},{1,17},{17,33},{33,49},{49,1},{2,18}... | collective-permute-start | bytes 1769480 | tf_op jit(solution)/shard_map/ppermute | solution.py:534
  207.7 3.6 %collective-permute-done.32.rest_0_ = bf16[144,2048]{1,0:T(8,128)(2,1)S(1)} collective-permute-done((bf16[144,2048]{1,0:T(8,128)(2,1)S(1)}, bf16[144,2048]{1,0:T(8,128)(2,1)S(1)}, u32[]{:S(2)}, u32[]{:S(2)}) %collective-permute-start.32) | collective-permute-done | bytes 589856 | tf_op jit(solution)/shard_map/ppermute | solution.py:534
  211.3 4.2 %collective-permute-done.34.rest_2_ = bf16[144,2048]{1,0:T(8,128)(2,1)S(1)} collective-permute-done((bf16[144,2048]{1,0:T(8,128)(2,1)S(1)}, bf16[144,2048]{1,0:T(8,128)(2,1)S(1)}, u32[]{:S(2)}, u32[]{:S(2)}) %collective-permute-start.34) | collective-permute-done | bytes 589856 | tf_op jit(solution)/shard_map/ppermute | solution.py:534
  218.6 3.1 %collective-permute-start.36 = (bf16[80,4096]{1,0:T(8,128)(2,1)S(1)}, bf16[80,4096]{1,0:T(8,128)(2,1)S(1)}, u32[]{:S(2)}, u32[]{:S(2)}) collective-permute-start(bf16[80,4096]{1,0:T(8,128)(2,1)S(1)} %get-tuple-element.440), channel_id=1, source_target_pairs={{0,64},{64,0},{1,65},{65,1},{2,66},{66,2},{3,67},{67,3},{4,68},{68... | collective-permute-start | bytes 1966088 | tf_op jit(solution)/shard_map/ppermute | solution.py:545
  222.9 7.8 %collective-permute-done.36.arrived = bf16[80,4096]{1,0:T(8,128)(2,1)S(1)} collective-permute-done((bf16[80,4096]{1,0:T(8,128)(2,1)S(1)}, bf16[80,4096]{1,0:T(8,128)(2,1)S(1)}, u32[]{:S(2)}, u32[]{:S(2)}) %collective-permute-start.36) | collective-permute-done | bytes 655392 | tf_op jit(solution)/shard_map/ppermute | solution.py:545
  (85 shorter events, 69.1 us)
Async XLA Ops:
  13.6 10.6 %collective-permute-start.1 = (bf16[4,8,1024]{2,1,0:T(8,128)(2,1)S(1)}, bf16[4,8,1024]{2,1,0:T(8,128)(2,1)S(1)}, u32[]{:S(2)}, u32[]{:S(2)}) collective-permute-start(bf16[4,8,1024]{2,1,0:T(8,128)(2,1)S(1)} %get-tuple-element.225.rest_0_), channel_id=1, source_target_pairs={{0,1},{4,5},{8,9},{12,13},{16,17},{20,21},{24,25},{28,29},{32,33},... | collective-permute-start | bytes 196616 | tf_op jit(solution)/shard_map/ppermute | solution.py:466
  22.9 10.6 %collective-permute-start = (bf16[4,8,1024]{2,1,0:T(8,128)(2,1)S(1)}, bf16[4,8,1024]{2,1,0:T(8,128)(2,1)S(1)}, u32[]{:S(2)}, u32[]{:S(2)}) collective-permute-start(bf16[4,8,1024]{2,1,0:T(8,128)(2,1)S(1)} %get-tuple-element.234), channel_id=1, source_target_pairs={{0,1},{4,5},{8,9},{12,13},{16,17},{20,21},{24,25},{28,29},{32,33},... | collective-permute-start | bytes 196616 | tf_op jit(solution)/shard_map/ppermute | solution.py:466
  32.2 10.6 %collective-permute-start.3 = (bf16[4,8,1024]{2,1,0:T(8,128)(2,1)S(1)}, bf16[4,8,1024]{2,1,0:T(8,128)(2,1)S(1)}, u32[]{:S(2)}, u32[]{:S(2)}) collective-permute-start(bf16[4,8,1024]{2,1,0:T(8,128)(2,1)S(1)} %get-tuple-element.252), channel_id=1, source_target_pairs={{0,1},{1,2},{4,5},{5,6},{8,9},{9,10},{12,13},{13,14},{16,17},{17,1... | collective-permute-start | bytes 196616 | tf_op jit(solution)/shard_map/ppermute | solution.py:466
  82.8 33.0 %collective-permute-start.16 = (bf16[4,4,32,128]{3,2,1,0:T(8,128)(2,1)S(1)}, bf16[4,4,32,128]{3,2,1,0:T(8,128)(2,1)S(1)}, u32[]{:S(2)}, u32[]{:S(2)}) collective-permute-start(bf16[4,4,32,128]{3,2,1,0:T(8,128)(2,1)S(1)} %get-tuple-element.366), channel_id=1, source_target_pairs={{0,4},{4,8},{8,12},{12,0},{1,5},{5,9},{9,13},{13,1},{2,6},{6,10},{... | collective-permute-start | bytes 393224 | tf_op jit(solution)/shard_map/ppermute | solution.py:516
  84.8 31.0 %collective-permute-start.15 = (bf16[4,8,1024]{2,1,0:T(8,128)(2,1)S(1)}, bf16[4,8,1024]{2,1,0:T(8,128)(2,1)S(1)}, u32[]{:S(2)}, u32[]{:S(2)}) collective-permute-start(bf16[4,8,1024]{2,1,0:T(8,128)(2,1)S(1)} %get-tuple-element.364), channel_id=1, source_target_pairs={{1,0},{2,1},{5,4},{6,5},{9,8},{10,9},{13,12},{14,13},{17,16},{18,1... | collective-permute-start | bytes 196616 | tf_op jit(solution)/shard_map/ppermute | solution.py:512
  86.7 41.8 %collective-permute-start.18 = (bf16[4,4,32,128]{3,2,1,0:T(8,128)(2,1)S(1)}, bf16[4,4,32,128]{3,2,1,0:T(8,128)(2,1)S(1)}, u32[]{:S(2)}, u32[]{:S(2)}) collective-permute-start(bf16[4,4,32,128]{3,2,1,0:T(8,128)(2,1)S(1)} %get-tuple-element.379), channel_id=1, source_target_pairs={{0,8},{4,12},{8,0},{12,4},{1,9},{5,13},{9,1},{13,5},{2,10},{6,14},... | collective-permute-start | bytes 393224 | tf_op jit(solution)/shard_map/ppermute | solution.py:516
  90.3 38.1 %collective-permute-start.17 = (bf16[4,8,1024]{2,1,0:T(8,128)(2,1)S(1)}, bf16[4,8,1024]{2,1,0:T(8,128)(2,1)S(1)}, u32[]{:S(2)}, u32[]{:S(2)}) collective-permute-start(bf16[4,8,1024]{2,1,0:T(8,128)(2,1)S(1)} %get-tuple-element.377), channel_id=1, source_target_pairs={{1,0},{2,1},{5,4},{6,5},{9,8},{10,9},{13,12},{14,13},{17,16},{18,1... | collective-permute-start | bytes 196616 | tf_op jit(solution)/shard_map/ppermute | solution.py:512
  121.2 16.6 %collective-permute-start.20 = (bf16[4,4,32,128]{3,2,1,0:T(8,128)(2,1)S(1)}, bf16[4,4,32,128]{3,2,1,0:T(8,128)(2,1)S(1)}, u32[]{:S(2)}, u32[]{:S(2)}) collective-permute-start(bf16[4,4,32,128]{3,2,1,0:T(8,128)(2,1)S(1)} %get-tuple-element.392), channel_id=1, source_target_pairs={{0,12},{4,0},{8,4},{12,8},{1,13},{5,1},{9,5},{13,9},{2,14},{6,2},{... | collective-permute-start | bytes 393224 | tf_op jit(solution)/shard_map/ppermute | solution.py:516
  123.6 14.2 %collective-permute-start.19 = (bf16[4,8,1024]{2,1,0:T(8,128)(2,1)S(1)}, bf16[4,8,1024]{2,1,0:T(8,128)(2,1)S(1)}, u32[]{:S(2)}, u32[]{:S(2)}) collective-permute-start(bf16[4,8,1024]{2,1,0:T(8,128)(2,1)S(1)} %get-tuple-element.390), channel_id=1, source_target_pairs={{1,0},{5,4},{9,8},{13,12},{17,16},{21,20},{25,24},{29,28},{33,32},... | collective-permute-start | bytes 196616 | tf_op jit(solution)/shard_map/ppermute | solution.py:512
  133.8 13.2 %collective-permute-start.21 = (bf16[4,8,1024]{2,1,0:T(8,128)(2,1)S(1)}, bf16[4,8,1024]{2,1,0:T(8,128)(2,1)S(1)}, u32[]{:S(2)}, u32[]{:S(2)}) collective-permute-start(bf16[4,8,1024]{2,1,0:T(8,128)(2,1)S(1)} %get-tuple-element.403), channel_id=1, source_target_pairs={{1,0},{5,4},{9,8},{13,12},{17,16},{21,20},{25,24},{29,28},{33,32},... | collective-permute-start | bytes 196616 | tf_op jit(solution)/shard_map/ppermute | solution.py:512
  151.8 14.9 %collective-permute-start.24 = (bf16[16,8,2048]{2,1,0:T(8,128)(2,1)S(1)}, bf16[16,8,2048]{2,1,0:T(8,128)(2,1)S(1)}, u32[]{:S(2)}, u32[]{:S(2)}) collective-permute-start(bf16[16,8,2048]{2,1,0:T(8,128)(2,1)S(1)} %get-tuple-element.421.rest_8_), channel_id=1, source_target_pairs={{0,48},{16,0},{32,16},{48,32},{1,49},{17,1},{33,17},{49,33},{2,50}... | collective-permute-start | bytes 1572872 | tf_op jit(solution)/shard_map/ppermute | solution.py:499
  152.6 16.4 %collective-permute-start.23 = (bf16[16,8,2048]{2,1,0:T(8,128)(2,1)S(1)}, bf16[16,8,2048]{2,1,0:T(8,128)(2,1)S(1)}, u32[]{:S(2)}, u32[]{:S(2)}) collective-permute-start(bf16[16,8,2048]{2,1,0:T(8,128)(2,1)S(1)} %get-tuple-element.421.rest_8_), channel_id=1, source_target_pairs={{0,32},{16,48},{32,0},{48,16},{1,33},{17,49},{33,1},{49,17},{2,34}... | collective-permute-start | bytes 1572872 | tf_op jit(solution)/shard_map/ppermute | solution.py:499
  154.6 21.4 %collective-permute-start.22 = (bf16[16,8,2048]{2,1,0:T(8,128)(2,1)S(1)}, bf16[16,8,2048]{2,1,0:T(8,128)(2,1)S(1)}, u32[]{:S(2)}, u32[]{:S(2)}) collective-permute-start(bf16[16,8,2048]{2,1,0:T(8,128)(2,1)S(1)} %get-tuple-element.421.rest_8_), channel_id=1, source_target_pairs={{0,16},{16,32},{32,48},{48,0},{1,17},{17,33},{33,49},{49,1},{2,18}... | collective-permute-start | bytes 1572872 | tf_op jit(solution)/shard_map/ppermute | solution.py:499
  154.6 21.4 %collective-permute-start.27 = (bf16[16,8,2048]{2,1,0:T(8,128)(2,1)S(1)}, bf16[16,8,2048]{2,1,0:T(8,128)(2,1)S(1)}, u32[]{:S(2)}, u32[]{:S(2)}) collective-permute-start(bf16[16,8,2048]{2,1,0:T(8,128)(2,1)S(1)} %get-tuple-element.422.rest_9_), channel_id=1, source_target_pairs={{0,12},{4,0},{8,4},{12,8},{1,13},{5,1},{9,5},{13,9},{2,14},{6,2},{... | collective-permute-start | bytes 1572872 | tf_op jit(solution)/shard_map/ppermute | solution.py:499
  155.6 20.4 %collective-permute-start.26 = (bf16[16,8,2048]{2,1,0:T(8,128)(2,1)S(1)}, bf16[16,8,2048]{2,1,0:T(8,128)(2,1)S(1)}, u32[]{:S(2)}, u32[]{:S(2)}) collective-permute-start(bf16[16,8,2048]{2,1,0:T(8,128)(2,1)S(1)} %get-tuple-element.422.rest_9_), channel_id=1, source_target_pairs={{0,8},{4,12},{8,0},{12,4},{1,9},{5,13},{9,1},{13,5},{2,10},{6,14},... | collective-permute-start | bytes 1572872 | tf_op jit(solution)/shard_map/ppermute | solution.py:499
  166.7 11.9 %collective-permute-start.25 = (bf16[16,8,2048]{2,1,0:T(8,128)(2,1)S(1)}, bf16[16,8,2048]{2,1,0:T(8,128)(2,1)S(1)}, u32[]{:S(2)}, u32[]{:S(2)}) collective-permute-start(bf16[16,8,2048]{2,1,0:T(8,128)(2,1)S(1)} %get-tuple-element.422.rest_9_), channel_id=1, source_target_pairs={{0,4},{4,8},{8,12},{12,0},{1,5},{5,9},{9,13},{13,1},{2,6},{6,10},{... | collective-permute-start | bytes 1572872 | tf_op jit(solution)/shard_map/ppermute | solution.py:499
  185.0 13.5 %collective-permute-start.29 = (bf16[80,2048]{1,0:T(8,128)(2,1)S(1)}, bf16[80,2048]{1,0:T(8,128)(2,1)S(1)}, u32[]{:S(2)}, u32[]{:S(2)}) collective-permute-start(bf16[80,2048]{1,0:T(8,128)(2,1)S(1)} %get-tuple-element.429), channel_id=1, source_target_pairs={{0,12},{4,0},{8,4},{12,8},{1,13},{5,1},{9,5},{13,9},{2,14},{6,2},{... | collective-permute-start | bytes 983048 | tf_op jit(solution)/shard_map/ppermute | solution.py:534
  185.5 13.0 %collective-permute-start.31 = (bf16[80,2048]{1,0:T(8,128)(2,1)S(1)}, bf16[80,2048]{1,0:T(8,128)(2,1)S(1)}, u32[]{:S(2)}, u32[]{:S(2)}) collective-permute-start(bf16[80,2048]{1,0:T(8,128)(2,1)S(1)} %get-tuple-element.433), channel_id=1, source_target_pairs={{0,48},{16,0},{32,16},{48,32},{1,49},{17,1},{33,17},{49,33},{2,50}... | collective-permute-start | bytes 983048 | tf_op jit(solution)/shard_map/ppermute | solution.py:534
  189.9 8.6 %collective-permute-start.30 = (bf16[64,2048]{1,0:T(8,128)(2,1)S(1)}, bf16[64,2048]{1,0:T(8,128)(2,1)S(1)}, u32[]{:S(2)}, u32[]{:S(2)}) collective-permute-start(bf16[64,2048]{1,0:T(8,128)(2,1)S(1)} %get-tuple-element.432), channel_id=1, source_target_pairs={{0,16},{16,32},{32,48},{48,0},{1,17},{17,33},{33,49},{49,1},{2,18}... | collective-permute-start | bytes 786440 | tf_op jit(solution)/shard_map/ppermute | solution.py:534
  200.1 11.2 %collective-permute-start.32 = (bf16[144,2048]{1,0:T(8,128)(2,1)S(1)}, bf16[144,2048]{1,0:T(8,128)(2,1)S(1)}, u32[]{:S(2)}, u32[]{:S(2)}) collective-permute-start(bf16[144,2048]{1,0:T(8,128)(2,1)S(1)} %get-tuple-element.434), channel_id=1, source_target_pairs={{0,4},{4,8},{8,12},{12,0},{1,5},{5,9},{9,13},{13,1},{2,6},{6,10},{... | collective-permute-start | bytes 1769480 | tf_op jit(solution)/shard_map/ppermute | solution.py:534
  201.1 10.2 %collective-permute-start.33 = (bf16[144,2048]{1,0:T(8,128)(2,1)S(1)}, bf16[144,2048]{1,0:T(8,128)(2,1)S(1)}, u32[]{:S(2)}, u32[]{:S(2)}) collective-permute-start(bf16[144,2048]{1,0:T(8,128)(2,1)S(1)} %get-tuple-element.435), channel_id=1, source_target_pairs={{0,12},{4,0},{8,4},{12,8},{1,13},{5,1},{9,5},{13,9},{2,14},{6,2},{... | collective-permute-start | bytes 1769480 | tf_op jit(solution)/shard_map/ppermute | solution.py:534
  203.4 12.1 %collective-permute-start.34 = (bf16[144,2048]{1,0:T(8,128)(2,1)S(1)}, bf16[144,2048]{1,0:T(8,128)(2,1)S(1)}, u32[]{:S(2)}, u32[]{:S(2)}) collective-permute-start(bf16[144,2048]{1,0:T(8,128)(2,1)S(1)} %get-tuple-element.436), channel_id=1, source_target_pairs={{0,16},{16,32},{32,48},{48,0},{1,17},{17,33},{33,49},{49,1},{2,18}... | collective-permute-start | bytes 1769480 | tf_op jit(solution)/shard_map/ppermute | solution.py:534
  207.2 10.3 %collective-permute-start.35 = (bf16[144,2048]{1,0:T(8,128)(2,1)S(1)}, bf16[144,2048]{1,0:T(8,128)(2,1)S(1)}, u32[]{:S(2)}, u32[]{:S(2)}) collective-permute-start(bf16[144,2048]{1,0:T(8,128)(2,1)S(1)} %get-tuple-element.437), channel_id=1, source_target_pairs={{0,48},{16,0},{32,16},{48,32},{1,49},{17,1},{33,17},{49,33},{2,50}... | collective-permute-start | bytes 1769480 | tf_op jit(solution)/shard_map/ppermute | solution.py:534
  218.6 12.2 %collective-permute-start.36 = (bf16[80,4096]{1,0:T(8,128)(2,1)S(1)}, bf16[80,4096]{1,0:T(8,128)(2,1)S(1)}, u32[]{:S(2)}, u32[]{:S(2)}) collective-permute-start(bf16[80,4096]{1,0:T(8,128)(2,1)S(1)} %get-tuple-element.440), channel_id=1, source_target_pairs={{0,64},{64,0},{1,65},{65,1},{2,66},{66,2},{3,67},{67,3},{4,68},{68... | collective-permute-start | bytes 1966088 | tf_op jit(solution)/shard_map/ppermute | solution.py:545
  (16 other events, 73.8 us)

commit v3 on v2

--- a/solution.py
+++ b/solution.py
@@ -80,16 +80,17 @@
         lax.fori_loop(begin, end, body, 0)
 
 
-def forward_kernel(place, own, bias, lens, *rest, tick, stages):
+def forward_kernel(place, *rest, tick, stages):
     if tick == 0:
-        (wi_in, wr_in), rest = rest[:2], rest[2:]
+        (lengths, own, bias_in, wi_in, wr_in), rest = rest[:5], rest[5:]
+        bias, lens = rest[9:11]
     else:
-        arrived, rest = rest[0], rest[9:]
+        (bias, lens, arrived), rest = rest[:3], rest[11:]
     emitted, wi, wr, xs, gates, cells, hs, wit_far, wrt_far = rest[:9]
     proj, staged, sems, load_sems = rest[-4:]
     span, rows, width = emitted.shape
     stage = place[0]
-    blocks = own.shape[0] // span
+    blocks = xs.shape[0] // span
     at = tick - LAG * stage
     active = (at >= 0) & (at < blocks)
     fs = at * span
@@ -99,19 +100,21 @@
     if tick == 0:
         load_wi = pltpu.make_async_copy(wi_in, wi, load_sems.at[0])
         load_wr = pltpu.make_async_copy(wr_in, wr, load_sems.at[1])
-        load_wi.start()
-        load_wr.start()
-        load_wi.wait()
+        load_own = pltpu.make_async_copy(own, xs, load_sems.at[2])
+        load_bias = pltpu.make_async_copy(bias_in, bias, load_sems.at[3])
+        for load in (load_own, load_bias, load_wi, load_wr):
+            load.start()
+        at_row = lax.broadcasted_iota(jnp.int32, lens.shape, 0)
+        known = jnp.zeros(lens.shape, jnp.int32)
+        for n in range(rows):
+            known = jnp.where(at_row == n, lengths[n], known)
+        lens[...] = known
+        for load in (load_own, load_bias, load_wi):
+            load.wait()
 
     @pl.when(active)
     def _():
-        if tick == 0:
-            xs[pl.ds(fs, span)] = own[pl.ds(fs, span)]
-        else:
-
-            @pl.when(stage == 0)
-            def _():
-                xs[pl.ds(fs, span)] = own[pl.ds(fs, span)]
+        if tick > 0:
 
             @pl.when(stage > 0)
             def _():
@@ -374,35 +377,39 @@
         lax.fori_loop(0, half // COLS, columns, 0)
 
 
-def finish_kernel(place, own_y, own_z, bias, *rest):
-    arrivals, keep, kept_bias, give = rest[:4], rest[4], rest[5], rest[6]
+def finish_kernel(place, own, bias, ahead, behind, keep, kept_bias, give, *, side):
+    blocks = (ahead, behind)
     xh = place[3]
-    fine, half = own_y.shape[1:]
-    for side, own in enumerate((own_y, own_z)):
-        cols = pl.ds(side * half, half)
-        blocks = arrivals[2 * side : 2 * side + 2]
-        for n in range(2):
-            mine, other = 2 * n + xh, 2 * n + 1 - xh
-            kept, given = own[mine], own[other]
-            for block in blocks:
-                kept += block[pl.ds(pl.multiple_of(mine * fine, fine), fine)].astype(jnp.float32)
-                given += block[pl.ds(pl.multiple_of(other * fine, fine), fine)].astype(jnp.float32)
-            keep[n, :, cols] = kept
-            give[pl.ds(n * fine, fine), cols] = given.astype(jnp.bfloat16)
-        total = bias[:, cols]
+    fine, half = own.shape[1:]
+    for n in range(2):
+        mine, other = 2 * n + xh, 2 * n + 1 - xh
+        kept, given = own[mine], own[other]
         for block in blocks:
-            total += from_rows(block[pl.ds(4 * fine, EXTRA)])
-        kept_bias[:, cols] = total
-        give[pl.ds(2 * fine, EXTRA), cols] = as_rows(total)
-
-
-def last_kernel(place, keep, bias, arrived, grad_i, grad_r, grad_b):
-    fine = keep.shape[1]
-    for n, out in enumerate((grad_i, grad_r)):
-        out[...] = keep[n] + arrived[pl.ds(n * fine, fine)].astype(jnp.float32)
-    width = grad_b.shape[1]
-    cols = pl.ds(pl.multiple_of(((place[3] * 4 + place[1]) * 4 + place[2]) * width, width), width)
-    grad_b[...] = bias[:, cols] + from_rows(arrived[pl.ds(2 * fine, EXTRA), cols])
+            kept += block[pl.ds(pl.multiple_of(mine * fine, fine), fine)].astype(jnp.float32)
+            given += block[pl.ds(pl.multiple_of(other * fine, fine), fine)].astype(jnp.float32)
+        keep[n] = kept
+        give[pl.ds(n * fine, fine)] = given.astype(jnp.bfloat16)
+    total = bias[:, pl.ds(side * half, half)]
+    for block in blocks:
+        total += from_rows(block[pl.ds(4 * fine, EXTRA)])
+    kept_bias[...] = total
+    give[pl.ds(2 * fine, EXTRA)] = as_rows(total)
+
+
+def last_kernel(place, *rest):
+    sides = (rest[:3], rest[3:6])
+    grad_i, grad_r, grad_b = rest[6:]
+    xh = place[3]
+    for side, (keep, bias, arrived) in enumerate(sides):
+        fine, half = keep.shape[1:]
+        for n, out in enumerate((grad_i, grad_r)):
+            out[:, pl.ds(side * half, half)] = keep[n] + arrived[pl.ds(n * fine, fine)].astype(jnp.float32)
+
+        @pl.when(xh == side)
+        def _():
+            width = grad_b.shape[1]
+            cols = pl.ds(pl.multiple_of((place[1] * 4 + place[2]) * width, width), width)
+            grad_b[...] = bias[:, cols] + from_rows(arrived[pl.ds(2 * fine, EXTRA), cols])
 
 
 def shape(dims, kind):
@@ -420,8 +427,7 @@
     stage = lax.axis_index("pipe")
     blocks = total // BLOCK
     ticks = blocks + LAG * (stages - 1)
-    lens = near(jnp.broadcast_to(lengths[:, None], (rows, width)))
-    cot, inputs, gate_bias = near(cotangent[0]), near(inputs), near(gate_bias)
+    cot = near(cotangent[0])
     params = pltpu.CompilerParams(vmem_limit_bytes=LIMIT)
     bf16, f32 = jnp.bfloat16, jnp.float32
 
@@ -437,18 +443,20 @@
     def forward(tick):
         first = tick == 0
         extra = (turned,) if tick == ticks - 1 else ()
+        if first:
+            extra = (shape((1, gated), f32), shape((rows, width), jnp.int32))
         return pl.pallas_call(
             partial(forward_kernel, tick=tick, stages=stages),
             out_shape=(block,) + state + extra,
-            in_specs=[SMEM] + [VMEM] * 3 + ([HBM] * 2 if first else [VMEM] * 7 + [HBM] * 2),
+            in_specs=[SMEM] * 2 + [HBM] * 4 if first else [SMEM] + [VMEM] * 9 + [HBM] * 2,
             out_specs=(VMEM,) * 7 + (HBM,) * 2 + (VMEM,) * len(extra),
             scratch_shapes=[
                 pltpu.VMEM((BLOCK, rows, gated), f32),
                 pltpu.VMEM((SLOTS, PANEL, width), bf16),
                 pltpu.SemaphoreType.DMA((SLOTS,)),
-                pltpu.SemaphoreType.DMA((2,)),
+                pltpu.SemaphoreType.DMA((4,)),
             ],
-            input_output_aliases={} if first else {5 + n: 1 + n for n in range(8)},
+            input_output_aliases={} if first else {4 + n: 1 + n for n in range(8)},
             compiler_params=params,
             name="forward_tick",
         )
@@ -457,10 +465,13 @@
     landed = {}
     for tick in range(ticks):
         if tick == 0:
-            got = [pltpu.with_memory_space_constraint(w[0], pltpu.HBM) for w in (input_weight, recurrent_weight)]
+            far_args = (inputs, gate_bias, input_weight[0], recurrent_weight[0])
+            got = [lengths, *(pltpu.with_memory_space_constraint(v, pltpu.HBM) for v in far_args)]
         else:
-            got = [landed.get(tick, emitted), *held]
-        emitted, *held = forward(tick)(place, inputs, gate_bias, lens, *got)
+            got = [bias, lens, landed.get(tick, emitted), *held]
+        emitted, *held = forward(tick)(place, *got)
+        if tick == 0:
+            held, (bias, lens) = held[:8], held[8:]
         on = [s for s in range(stages - 1) if 0 <= tick - LAG * s < blocks]
         if on:
             landed[tick + LAG] = near(lax.ppermute(emitted, "pipe", [(s, s + 1) for s in on]))
@@ -536,20 +547,23 @@
     got = both_ways(made[2], made[3], made[6], made[7])
     part = shape((4 * fine + EXTRA, half), bf16)
     sends = simple(relay_kernel, "relay", (part,) * 4, 9)(place, bias, *made[:2], *got[:2], *made[4:6], *got[2:])
-    keep, bias, give = simple(
-        finish_kernel,
-        "finish",
-        (shape((2, fine, gated), f32), shape((1, gated), f32), shape((2 * fine + EXTRA, gated), bf16)),
-        7,
-    )(place, mine_y, mine_z, bias, *both_ways(*sends))
-    other = near(lax.ppermute(give, "xh", [(0, 1), (1, 0)]))
+    got = both_ways(*sends)
+    done = []
+    for side, mine in enumerate((mine_y, mine_z)):
+        keep, total_bias, give = simple(
+            partial(finish_kernel, side=side),
+            "finish",
+            (shape((2, fine, half), f32), shape((1, half), f32), shape((2 * fine + EXTRA, half), bf16)),
+            4,
+        )(place, mine, bias, *got[2 * side : 2 * side + 2])
+        done += [keep, total_bias, near(lax.ppermute(give, "xh", [(0, 1), (1, 0)]))]
     made = jax.ShapeDtypeStruct
     grad_i, grad_r, grad_b = simple(
         last_kernel,
         "last",
         (made((fine, gated), f32), made((fine, gated), f32), made((1, gated // 32), f32)),
-        3,
-    )(place, keep, bias, other)
+        6,
+    )(place, *done)
     return (grad_i[None], grad_r[None], grad_b, final_hidden[None], final_cell[None])
 
 

time: 233 us -> 228 us (0.979)
  waiting for transfers between devices: 77.1 us -> 69.8 us
  starting transfers between devices: 55.4 us -> 58.2 us
    ppermute x8, waiting for transfers between devices: 14.8 us -> 10.9 us  [both_ways(): return [near(lax.ppermute(v, axis, routes[d])) for v, axis, d in sent]]
    ppermute x1 -> x2, waiting for transfers between devices: 7.84 us -> 4.34 us  [local(): done += [keep, total_bias, near(lax.ppermute(give, 'xh', [(0, 1), (1, 0)]))]]
    ppermute x1 -> x2, starting transfers between devices: 3.11 us -> 6.19 us  [local(): done += [keep, total_bias, near(lax.ppermute(give, 'xh', [(0, 1), (1, 0)]))]]
    pallas_call x11 -> x12, Pallas kernels: 56.3 us -> 57.1 us  [the longest x10 55.4 us: local(): emitted, *held = forward(tick)(place, *got)]
  transfers between devices with their start and end apart: 37 -> 38, of which waited for: 15 -> 15; matrix products, arithmetic and copies ran while one was open for 1% -> 1% of each run, Pallas kernels for 24% -> 25%
where the time goes in v3:
time: 228 us; the launch traced here: 227 us
  Pallas kernels  96.1 us (42%)
  waiting for transfers between devices  69.8 us (31%)
  starting transfers between devices  58.2 us (26%)
    pallas_call x10, Pallas kernels, local(): emitted, *held = forward(tick)(place, *got)  55.4 us
    ppermute x8, waiting for transfers between devices, local(): lax.ppermute(lower, 'pipe', [(s, s - 1) for s in on])  33.4 us
    pallas_call x10, Pallas kernels, local(): backward(tick)(place, cot, landed.get(tick, lower), lens, *held)  28.5 us
    ppermute x6, waiting for transfers between devices, passed(): lax.ppermute(made[n], 'y' if n < 3 else 'z', routes[n % 3])  21 us
    ppermute x8, starting transfers between devices, both_ways(): return [near(lax.ppermute(v, axis, routes[d])) for v, axis, d in sent]  16.2 us
    ppermute x6, starting transfers between devices, local(): piece = lax.ppermute(piece, axis, routes[d - 1])  14.4 us
    ppermute x8, waiting for transfers between devices, both_ways(): return [near(lax.ppermute(v, axis, routes[d])) for v, axis, d in sent]  10.9 us
    ppermute x8, starting transfers between devices, local(): lax.ppermute(lower, 'pipe', [(s, s - 1) for s in on])  7.94 us
  transfers between devices with their start and end apart: 38, of which 15 were waited for; matrix products, arithmetic and copies ran while one was open for 1% of the time, Pallas kernels for 25%

profile of v3, /device:TPU:0, one launch (start us, length us, event | category | flops | bytes accessed | tf_op | source)
XLA Modules:
  0.0 227.2 jit_solution(8646717782231922123)
XLA Ops:
  1.4 10.6 %forward_tick.10 = (bf16[4,8,1024]{2,1,0:T(8,128)(2,1)S(1)}, bf16[1024,4096]{1,0:T(8,128)(2,1)S(1)}, bf16[1024,4096]{1,0:T(8,128)(2,1)S(1)}, bf16[16,8,1024]{2,1...) custom-call(s32[4]{0:T(128)S(1)} %pad_add_fusion.place, ...), custom_call_target="tpu_custom_call" | custom-call | tf_op jit(solution)/shard_map/forward_tick/pallas_call | solution.py:472
  13.3 8.0 %forward_tick.11 = (bf16[4,8,1024]{2,1,0:T(8,128)(2,1)S(1)}, bf16[1024,4096]{1,0:T(8,128)(2,1)S(1)}, bf16[1024,4096]{1,0:T(8,128)(2,1)S(1)}, bf16[16,8,1024]{2,1...) custom-call(s32[4]{0:T(128)S(1)} %pad_add_fusion.place, ...), custom_call_target="tpu_custom_call", output_to_operand_aliasing={{1}: (4, {}), {2}: (5, {}), {3}: (6, {}), {4}: (7, {}), {5}... | custom-call | tf_op jit(solution)/shard_map/forward_tick/pallas_call | solution.py:472
  22.6 8.0 %forward_tick.12 = (bf16[4,8,1024]{2,1,0:T(8,128)(2,1)S(1)}, bf16[1024,4096]{1,0:T(8,128)(2,1)S(1)}, bf16[1024,4096]{1,0:T(8,128)(2,1)S(1)}, bf16[16,8,1024]{2,1...) custom-call(s32[4]{0:T(128)S(1)} %pad_add_fusion.place, ...), custom_call_target="tpu_custom_call", output_to_operand_aliasing={{1}: (4, {}), {2}: (5, {}), {3}: (6, {}), {4}: (7, {}), {5}... | custom-call | tf_op jit(solution)/shard_map/forward_tick/pallas_call | solution.py:472
  32.0 8.0 %forward_tick.13 = (bf16[4,8,1024]{2,1,0:T(8,128)(2,1)S(1)}, bf16[1024,4096]{1,0:T(8,128)(2,1)S(1)}, bf16[1024,4096]{1,0:T(8,128)(2,1)S(1)}, bf16[16,8,1024]{2,1...) custom-call(s32[4]{0:T(128)S(1)} %pad_add_fusion.place, ...), custom_call_target="tpu_custom_call", output_to_operand_aliasing={{1}: (4, {}), {2}: (5, {}), {3}: (6, {}), {4}: (7, {}), {5}... | custom-call | tf_op jit(solution)/shard_map/forward_tick/pallas_call | solution.py:472
  46.6 7.7 %forward_tick.18 = (bf16[4,8,1024]{2,1,0:T(8,128)(2,1)}, bf16[1024,4096]{1,0:T(8,128)(2,1)S(1)}, bf16[1024,4096]{1,0:T(8,128)(2,1)S(1)}, bf16[16,8,1024]{2,1,0:T...) custom-call(s32[4]{0:T(128)S(1)} %pad_add_fusion.place, ...), custom_call_target="tpu_custom_call", output_to_operand_aliasing={{1}: (4, {}), {2}: (5, {}), {3}: (6, {}), {4}: (7, {}), {5}... | custom-call | tf_op jit(solution)/shard_map/forward_tick/pallas_call | solution.py:472
  54.4 10.5 %forward_tick.19 = (bf16[4,8,1024]{2,1,0:T(8,128)(2,1)S(1)}, bf16[1024,4096]{1,0:T(8,128)(2,1)S(1)}, bf16[1024,4096]{1,0:T(8,128)(2,1)S(1)}, bf16[16,8,1024]{2,1...) custom-call(s32[4]{0:T(128)S(1)} %pad_add_fusion.place, ...), custom_call_target="tpu_custom_call", output_to_operand_aliasing={{1}: (4, {}), {2}: (5, {}), {3}: (6, {}), {4}: (7, {}), {5}... | custom-call | tf_op jit(solution)/shard_map/forward_tick/pallas_call | solution.py:472
  64.9 3.9 %backward_tick.10 = (bf16[4,8,1024]{2,1,0:T(8,128)(2,1)S(1)}, bf16[16,8,2048]{2,1,0:T(8,128)(2,1)S(1)}, bf16[16,8,2048]{2,1,0:T(8,128)(2,1)S(1)}, f32[16,8,4096]...) custom-call(s32[4]{0:T(128)S(1)} %pad_add_fusion.place, ...), custom_call_target="tpu_custom_call", output_to_operand_aliasing={{3}: (5, {}), {4}: (6, {}), {6}: (7, {})} | custom-call | tf_op jit(solution)/shard_map/backward_tick/pallas_call | solution.py:515
  85.1 3.7 %collective-permute-start.18 = (bf16[4,4,32,128]{3,2,1,0:T(8,128)(2,1)S(1)}, bf16[4,4,32,128]{3,2,1,0:T(8,128)(2,1)S(1)}, u32[]{:S(2)}, u32[]{:S(2)}) collective-permute-start(bf16[4,4,32,128]{3,2,1,0:T(8,128)(2,1)S(1)} %get-tuple-element.386), channel_id=1, source_target_pairs={{0,8},{4,12},{8,0},{12,4},{1,9},{5,13},{9,1},{13,5},{2,10},{6,14},... | collective-permute-start | bytes 393224 | tf_op jit(solution)/shard_map/ppermute | solution.py:527
  90.1 24.2 %collective-permute-done.15.arrived = bf16[4,8,1024]{2,1,0:T(8,128)(2,1)S(1)} collective-permute-done((bf16[4,8,1024]{2,1,0:T(8,128)(2,1)S(1)}, bf16[4,8,1024]{2,1,0:T(8,128)(2,1)S(1)}, u32[]{:S(2)}, u32[]{:S(2)}) %collective-permute-start.15) | collective-permute-done | bytes 65568 | tf_op jit(solution)/shard_map/ppermute | solution.py:523
  114.3 5.4 %backward_tick.16 = (bf16[4,8,1024]{2,1,0:T(8,128)(2,1)S(1)}, bf16[16,8,2048]{2,1,0:T(8,128)(2,1)S(1)}, bf16[16,8,2048]{2,1,0:T(8,128)(2,1)S(1)}, f32[16,8,4096]...) custom-call(s32[4]{0:T(128)S(1)} %pad_add_fusion.place, ...), custom_call_target="tpu_custom_call", output_to_operand_aliasing={{1}: (4, {}), {2}: (5, {}), {3}: (6, {}), {4}: (7, {}), {5}... | custom-call | tf_op jit(solution)/shard_map/backward_tick/pallas_call | solution.py:515
  123.4 3.5 %collective-permute-done.17.arrived = bf16[4,8,1024]{2,1,0:T(8,128)(2,1)S(1)} collective-permute-done((bf16[4,8,1024]{2,1,0:T(8,128)(2,1)S(1)}, bf16[4,8,1024]{2,1,0:T(8,128)(2,1)S(1)}, u32[]{:S(2)}, u32[]{:S(2)}) %collective-permute-start.17) | collective-permute-done | bytes 65568 | tf_op jit(solution)/shard_map/ppermute | solution.py:523
  126.9 5.4 %backward_tick.17 = (bf16[4,8,1024]{2,1,0:T(8,128)(2,1)S(1)}, bf16[16,8,2048]{2,1,0:T(8,128)(2,1)S(1)}, bf16[16,8,2048]{2,1,0:T(8,128)(2,1)S(1)}, f32[16,8,4096]...) custom-call(s32[4]{0:T(128)S(1)} %pad_add_fusion.place, ...), custom_call_target="tpu_custom_call", output_to_operand_aliasing={{1}: (4, {}), {2}: (5, {}), {3}: (6, {}), {4}: (7, {}), {5}... | custom-call | tf_op jit(solution)/shard_map/backward_tick/pallas_call | solution.py:515
  136.2 6.2 %backward_tick.18 = (bf16[4,8,1024]{2,1,0:T(8,128)(2,1)}, bf16[16,8,2048]{2,1,0:T(8,128)(2,1)S(1)}, bf16[16,8,2048]{2,1,0:T(8,128)(2,1)S(1)}, f32[16,8,4096]{2,1...) custom-call(s32[4]{0:T(128)S(1)} %pad_add_fusion.place, ...), custom_call_target="tpu_custom_call", output_to_operand_aliasing={{1}: (4, {}), {2}: (5, {}), {3}: (6, {}), {4}: (7, {}), {5}... | custom-call | tf_op jit(solution)/shard_map/backward_tick/pallas_call | solution.py:515
  142.4 3.0 %collective-permute-done.21.arrived = bf16[4,8,1024]{2,1,0:T(8,128)(2,1)S(1)} collective-permute-done((bf16[4,8,1024]{2,1,0:T(8,128)(2,1)S(1)}, bf16[4,8,1024]{2,1,0:T(8,128)(2,1)S(1)}, u32[]{:S(2)}, u32[]{:S(2)}) %collective-permute-start.21) | collective-permute-done | bytes 65568 | tf_op jit(solution)/shard_map/ppermute | solution.py:523
  145.4 4.8 %backward_tick.19 = (bf16[4,8,1024]{2,1,0:T(8,128)(2,1)}, bf16[16,8,2048]{2,1,0:T(8,128)(2,1)S(1)}, bf16[16,8,2048]{2,1,0:T(8,128)(2,1)S(1)}, f32[16,8,4096]{2,1...) custom-call(s32[4]{0:T(128)S(1)} %pad_add_fusion.place, ...), custom_call_target="tpu_custom_call", output_to_operand_aliasing={{1}: (4, {}), {2}: (5, {}), {3}: (6, {}), {4}: (7, {}), {5}... | custom-call | tf_op jit(solution)/shard_map/backward_tick/pallas_call | solution.py:515
  155.6 9.6 %collective-permute-done.24.rest_12_ = bf16[16,8,2048]{2,1,0:T(8,128)(2,1)S(1)} collective-permute-done((bf16[16,8,2048]{2,1,0:T(8,128)(2,1)S(1)}, bf16[16,8,2048]{2,1,0:T(8,128)(2,1)S(1)}, u32[]{:S(2)}, u32[]{:S(2)}) %collective-permute-start.24) | collective-permute-done | bytes 524320 | tf_op jit(solution)/shard_map/ppermute | solution.py:510
  167.4 7.0 %collective-permute-done.22.rest_10_ = bf16[16,8,2048]{2,1,0:T(8,128)(2,1)S(1)} collective-permute-done((bf16[16,8,2048]{2,1,0:T(8,128)(2,1)S(1)}, bf16[16,8,2048]{2,1,0:T(8,128)(2,1)S(1)}, u32[]{:S(2)}, u32[]{:S(2)}) %collective-permute-start.22) | collective-permute-done | bytes 524320 | tf_op jit(solution)/shard_map/ppermute | solution.py:510
  177.0 6.5 %combine.1 = (f32[4,32,2048]{2,1,0:T(8,128)S(1)}, f32[4,32,2048]{2,1,0:T(8,128)S(1)}, f32[1,4096]{1,0:T(1,128)S(1)}, f32[128,2048]{1,0:T(8,128)S(1)}, f32[128,20...) custom-call(s32[4]{0:T(128)S(1)} %pad_add_fusion.place, ...), custom_call_target="tpu_custom_call" | custom-call | tf_op jit(solution)/shard_map/combine/pallas_call | solution.py:535
  188.4 3.7 %collective-permute-start.30 = (bf16[64,2048]{1,0:T(8,128)(2,1)S(1)}, bf16[64,2048]{1,0:T(8,128)(2,1)S(1)}, u32[]{:S(2)}, u32[]{:S(2)}) collective-permute-start(bf16[64,2048]{1,0:T(8,128)(2,1)S(1)} %get-tuple-element.438), channel_id=1, source_target_pairs={{0,16},{16,32},{32,48},{48,0},{1,17},{17,33},{33,49},{49,1},{2,18}... | collective-permute-start | bytes 786440 | tf_op jit(solution)/shard_map/ppermute | solution.py:545
  201.9 3.8 %collective-permute-start.35 = (bf16[144,2048]{1,0:T(8,128)(2,1)S(1)}, bf16[144,2048]{1,0:T(8,128)(2,1)S(1)}, u32[]{:S(2)}, u32[]{:S(2)}) collective-permute-start(bf16[144,2048]{1,0:T(8,128)(2,1)S(1)} %get-tuple-element.446), channel_id=1, source_target_pairs={{0,16},{16,32},{32,48},{48,0},{1,17},{17,33},{33,49},{49,1},{2,18}... | collective-permute-start | bytes 1769480 | tf_op jit(solution)/shard_map/ppermute | solution.py:545
  206.2 3.6 %collective-permute-done.32.ahead = bf16[144,2048]{1,0:T(8,128)(2,1)S(1)} collective-permute-done((bf16[144,2048]{1,0:T(8,128)(2,1)S(1)}, bf16[144,2048]{1,0:T(8,128)(2,1)S(1)}, u32[]{:S(2)}, u32[]{:S(2)}) %collective-permute-start.32) | collective-permute-done | bytes 589856 | tf_op jit(solution)/shard_map/ppermute | solution.py:545
  210.6 3.1 %collective-permute-start.34 = (bf16[80,2048]{1,0:T(8,128)(2,1)S(1)}, bf16[80,2048]{1,0:T(8,128)(2,1)S(1)}, u32[]{:S(2)}, u32[]{:S(2)}) collective-permute-start(bf16[80,2048]{1,0:T(8,128)(2,1)S(1)} %get-tuple-element.444), channel_id=1, source_target_pairs={{0,64},{64,0},{1,65},{65,1},{2,66},{66,2},{3,67},{67,3},{4,68},{68... | collective-permute-start | bytes 983048 | tf_op jit(solution)/shard_map/ppermute | solution.py:559
  216.8 3.1 %collective-permute-start.37 = (bf16[80,2048]{1,0:T(8,128)(2,1)S(1)}, bf16[80,2048]{1,0:T(8,128)(2,1)S(1)}, u32[]{:S(2)}, u32[]{:S(2)}) collective-permute-start(bf16[80,2048]{1,0:T(8,128)(2,1)S(1)} %get-tuple-element.450), channel_id=1, source_target_pairs={{0,64},{64,0},{1,65},{65,1},{2,66},{66,2},{3,67},{67,3},{4,68},{68... | collective-permute-start | bytes 983048 | tf_op jit(solution)/shard_map/ppermute | solution.py:559
  221.2 4.3 %collective-permute-done.37.rest_5_ = bf16[80,2048]{1,0:T(8,128)(2,1)S(1)} collective-permute-done((bf16[80,2048]{1,0:T(8,128)(2,1)S(1)}, bf16[80,2048]{1,0:T(8,128)(2,1)S(1)}, u32[]{:S(2)}, u32[]{:S(2)}) %collective-permute-start.37) | collective-permute-done | bytes 327712 | tf_op jit(solution)/shard_map/ppermute | solution.py:559
  (85 shorter events, 68.5 us)
Async XLA Ops:
  12.0 10.6 %collective-permute-start.1 = (bf16[4,8,1024]{2,1,0:T(8,128)(2,1)S(1)}, bf16[4,8,1024]{2,1,0:T(8,128)(2,1)S(1)}, u32[]{:S(2)}, u32[]{:S(2)}) collective-permute-start(bf16[4,8,1024]{2,1,0:T(8,128)(2,1)S(1)} %get-tuple-element.232.rest_2_), channel_id=1, source_target_pairs={{0,1},{4,5},{8,9},{12,13},{16,17},{20,21},{24,25},{28,29},{32,33},... | collective-permute-start | bytes 196616 | tf_op jit(solution)/shard_map/ppermute | solution.py:477
  21.3 10.6 %collective-permute-start = (bf16[4,8,1024]{2,1,0:T(8,128)(2,1)S(1)}, bf16[4,8,1024]{2,1,0:T(8,128)(2,1)S(1)}, u32[]{:S(2)}, u32[]{:S(2)}) collective-permute-start(bf16[4,8,1024]{2,1,0:T(8,128)(2,1)S(1)} %get-tuple-element.241), channel_id=1, source_target_pairs={{0,1},{4,5},{8,9},{12,13},{16,17},{20,21},{24,25},{28,29},{32,33},... | collective-permute-start | bytes 196616 | tf_op jit(solution)/shard_map/ppermute | solution.py:477
  30.7 10.6 %collective-permute-start.3 = (bf16[4,8,1024]{2,1,0:T(8,128)(2,1)S(1)}, bf16[4,8,1024]{2,1,0:T(8,128)(2,1)S(1)}, u32[]{:S(2)}, u32[]{:S(2)}) collective-permute-start(bf16[4,8,1024]{2,1,0:T(8,128)(2,1)S(1)} %get-tuple-element.259), channel_id=1, source_target_pairs={{0,1},{1,2},{4,5},{5,6},{8,9},{9,10},{12,13},{13,14},{16,17},{17,1... | collective-permute-start | bytes 196616 | tf_op jit(solution)/shard_map/ppermute | solution.py:477
  81.2 33.0 %collective-permute-start.16 = (bf16[4,4,32,128]{3,2,1,0:T(8,128)(2,1)S(1)}, bf16[4,4,32,128]{3,2,1,0:T(8,128)(2,1)S(1)}, u32[]{:S(2)}, u32[]{:S(2)}) collective-permute-start(bf16[4,4,32,128]{3,2,1,0:T(8,128)(2,1)S(1)} %get-tuple-element.373), channel_id=1, source_target_pairs={{0,4},{4,8},{8,12},{12,0},{1,5},{5,9},{9,13},{13,1},{2,6},{6,10},{... | collective-permute-start | bytes 393224 | tf_op jit(solution)/shard_map/ppermute | solution.py:527
  83.2 31.0 %collective-permute-start.15 = (bf16[4,8,1024]{2,1,0:T(8,128)(2,1)S(1)}, bf16[4,8,1024]{2,1,0:T(8,128)(2,1)S(1)}, u32[]{:S(2)}, u32[]{:S(2)}) collective-permute-start(bf16[4,8,1024]{2,1,0:T(8,128)(2,1)S(1)} %get-tuple-element.371), channel_id=1, source_target_pairs={{1,0},{2,1},{5,4},{6,5},{9,8},{10,9},{13,12},{14,13},{17,16},{18,1... | collective-permute-start | bytes 196616 | tf_op jit(solution)/shard_map/ppermute | solution.py:523
  85.1 41.8 %collective-permute-start.18 = (bf16[4,4,32,128]{3,2,1,0:T(8,128)(2,1)S(1)}, bf16[4,4,32,128]{3,2,1,0:T(8,128)(2,1)S(1)}, u32[]{:S(2)}, u32[]{:S(2)}) collective-permute-start(bf16[4,4,32,128]{3,2,1,0:T(8,128)(2,1)S(1)} %get-tuple-element.386), channel_id=1, source_target_pairs={{0,8},{4,12},{8,0},{12,4},{1,9},{5,13},{9,1},{13,5},{2,10},{6,14},... | collective-permute-start | bytes 393224 | tf_op jit(solution)/shard_map/ppermute | solution.py:527
  88.8 38.1 %collective-permute-start.17 = (bf16[4,8,1024]{2,1,0:T(8,128)(2,1)S(1)}, bf16[4,8,1024]{2,1,0:T(8,128)(2,1)S(1)}, u32[]{:S(2)}, u32[]{:S(2)}) collective-permute-start(bf16[4,8,1024]{2,1,0:T(8,128)(2,1)S(1)} %get-tuple-element.384), channel_id=1, source_target_pairs={{1,0},{2,1},{5,4},{6,5},{9,8},{10,9},{13,12},{14,13},{17,16},{18,1... | collective-permute-start | bytes 196616 | tf_op jit(solution)/shard_map/ppermute | solution.py:523
  119.6 16.6 %collective-permute-start.20 = (bf16[4,4,32,128]{3,2,1,0:T(8,128)(2,1)S(1)}, bf16[4,4,32,128]{3,2,1,0:T(8,128)(2,1)S(1)}, u32[]{:S(2)}, u32[]{:S(2)}) collective-permute-start(bf16[4,4,32,128]{3,2,1,0:T(8,128)(2,1)S(1)} %get-tuple-element.399), channel_id=1, source_target_pairs={{0,12},{4,0},{8,4},{12,8},{1,13},{5,1},{9,5},{13,9},{2,14},{6,2},{... | collective-permute-start | bytes 393224 | tf_op jit(solution)/shard_map/ppermute | solution.py:527
  122.1 14.2 %collective-permute-start.19 = (bf16[4,8,1024]{2,1,0:T(8,128)(2,1)S(1)}, bf16[4,8,1024]{2,1,0:T(8,128)(2,1)S(1)}, u32[]{:S(2)}, u32[]{:S(2)}) collective-permute-start(bf16[4,8,1024]{2,1,0:T(8,128)(2,1)S(1)} %get-tuple-element.397), channel_id=1, source_target_pairs={{1,0},{5,4},{9,8},{13,12},{17,16},{21,20},{25,24},{29,28},{33,32},... | collective-permute-start | bytes 196616 | tf_op jit(solution)/shard_map/ppermute | solution.py:523
  132.2 13.2 %collective-permute-start.21 = (bf16[4,8,1024]{2,1,0:T(8,128)(2,1)S(1)}, bf16[4,8,1024]{2,1,0:T(8,128)(2,1)S(1)}, u32[]{:S(2)}, u32[]{:S(2)}) collective-permute-start(bf16[4,8,1024]{2,1,0:T(8,128)(2,1)S(1)} %get-tuple-element.410), channel_id=1, source_target_pairs={{1,0},{5,4},{9,8},{13,12},{17,16},{21,20},{25,24},{29,28},{33,32},... | collective-permute-start | bytes 196616 | tf_op jit(solution)/shard_map/ppermute | solution.py:523
  150.3 14.9 %collective-permute-start.24 = (bf16[16,8,2048]{2,1,0:T(8,128)(2,1)S(1)}, bf16[16,8,2048]{2,1,0:T(8,128)(2,1)S(1)}, u32[]{:S(2)}, u32[]{:S(2)}) collective-permute-start(bf16[16,8,2048]{2,1,0:T(8,128)(2,1)S(1)} %get-tuple-element.428.rest_8_), channel_id=1, source_target_pairs={{0,48},{16,0},{32,16},{48,32},{1,49},{17,1},{33,17},{49,33},{2,50}... | collective-permute-start | bytes 1572872 | tf_op jit(solution)/shard_map/ppermute | solution.py:510
  151.1 16.4 %collective-permute-start.23 = (bf16[16,8,2048]{2,1,0:T(8,128)(2,1)S(1)}, bf16[16,8,2048]{2,1,0:T(8,128)(2,1)S(1)}, u32[]{:S(2)}, u32[]{:S(2)}) collective-permute-start(bf16[16,8,2048]{2,1,0:T(8,128)(2,1)S(1)} %get-tuple-element.428.rest_8_), channel_id=1, source_target_pairs={{0,32},{16,48},{32,0},{48,16},{1,33},{17,49},{33,1},{49,17},{2,34}... | collective-permute-start | bytes 1572872 | tf_op jit(solution)/shard_map/ppermute | solution.py:510
  153.0 21.4 %collective-permute-start.22 = (bf16[16,8,2048]{2,1,0:T(8,128)(2,1)S(1)}, bf16[16,8,2048]{2,1,0:T(8,128)(2,1)S(1)}, u32[]{:S(2)}, u32[]{:S(2)}) collective-permute-start(bf16[16,8,2048]{2,1,0:T(8,128)(2,1)S(1)} %get-tuple-element.428.rest_8_), channel_id=1, source_target_pairs={{0,16},{16,32},{32,48},{48,0},{1,17},{17,33},{33,49},{49,1},{2,18}... | collective-permute-start | bytes 1572872 | tf_op jit(solution)/shard_map/ppermute | solution.py:510
  153.0 21.4 %collective-permute-start.27 = (bf16[16,8,2048]{2,1,0:T(8,128)(2,1)S(1)}, bf16[16,8,2048]{2,1,0:T(8,128)(2,1)S(1)}, u32[]{:S(2)}, u32[]{:S(2)}) collective-permute-start(bf16[16,8,2048]{2,1,0:T(8,128)(2,1)S(1)} %get-tuple-element.429.rest_9_), channel_id=1, source_target_pairs={{0,12},{4,0},{8,4},{12,8},{1,13},{5,1},{9,5},{13,9},{2,14},{6,2},{... | collective-permute-start | bytes 1572872 | tf_op jit(solution)/shard_map/ppermute | solution.py:510
  154.0 20.4 %collective-permute-start.26 = (bf16[16,8,2048]{2,1,0:T(8,128)(2,1)S(1)}, bf16[16,8,2048]{2,1,0:T(8,128)(2,1)S(1)}, u32[]{:S(2)}, u32[]{:S(2)}) collective-permute-start(bf16[16,8,2048]{2,1,0:T(8,128)(2,1)S(1)} %get-tuple-element.429.rest_9_), channel_id=1, source_target_pairs={{0,8},{4,12},{8,0},{12,4},{1,9},{5,13},{9,1},{13,5},{2,10},{6,14},... | collective-permute-start | bytes 1572872 | tf_op jit(solution)/shard_map/ppermute | solution.py:510
  165.2 11.9 %collective-permute-start.25 = (bf16[16,8,2048]{2,1,0:T(8,128)(2,1)S(1)}, bf16[16,8,2048]{2,1,0:T(8,128)(2,1)S(1)}, u32[]{:S(2)}, u32[]{:S(2)}) collective-permute-start(bf16[16,8,2048]{2,1,0:T(8,128)(2,1)S(1)} %get-tuple-element.429.rest_9_), channel_id=1, source_target_pairs={{0,4},{4,8},{8,12},{12,0},{1,5},{5,9},{9,13},{13,1},{2,6},{6,10},{... | collective-permute-start | bytes 1572872 | tf_op jit(solution)/shard_map/ppermute | solution.py:510
  183.5 13.5 %collective-permute-start.29 = (bf16[80,2048]{1,0:T(8,128)(2,1)S(1)}, bf16[80,2048]{1,0:T(8,128)(2,1)S(1)}, u32[]{:S(2)}, u32[]{:S(2)}) collective-permute-start(bf16[80,2048]{1,0:T(8,128)(2,1)S(1)} %get-tuple-element.435), channel_id=1, source_target_pairs={{0,12},{4,0},{8,4},{12,8},{1,13},{5,1},{9,5},{13,9},{2,14},{6,2},{... | collective-permute-start | bytes 983048 | tf_op jit(solution)/shard_map/ppermute | solution.py:545
  184.0 13.1 %collective-permute-start.31 = (bf16[80,2048]{1,0:T(8,128)(2,1)S(1)}, bf16[80,2048]{1,0:T(8,128)(2,1)S(1)}, u32[]{:S(2)}, u32[]{:S(2)}) collective-permute-start(bf16[80,2048]{1,0:T(8,128)(2,1)S(1)} %get-tuple-element.439), channel_id=1, source_target_pairs={{0,48},{16,0},{32,16},{48,32},{1,49},{17,1},{33,17},{49,33},{2,50}... | collective-permute-start | bytes 983048 | tf_op jit(solution)/shard_map/ppermute | solution.py:545
  198.6 11.2 %collective-permute-start.32 = (bf16[144,2048]{1,0:T(8,128)(2,1)S(1)}, bf16[144,2048]{1,0:T(8,128)(2,1)S(1)}, u32[]{:S(2)}, u32[]{:S(2)}) collective-permute-start(bf16[144,2048]{1,0:T(8,128)(2,1)S(1)} %get-tuple-element.440), channel_id=1, source_target_pairs={{0,4},{4,8},{8,12},{12,0},{1,5},{5,9},{9,13},{13,1},{2,6},{6,10},{... | collective-permute-start | bytes 1769480 | tf_op jit(solution)/shard_map/ppermute | solution.py:545
  199.6 10.1 %collective-permute-start.33 = (bf16[144,2048]{1,0:T(8,128)(2,1)S(1)}, bf16[144,2048]{1,0:T(8,128)(2,1)S(1)}, u32[]{:S(2)}, u32[]{:S(2)}) collective-permute-start(bf16[144,2048]{1,0:T(8,128)(2,1)S(1)} %get-tuple-element.441), channel_id=1, source_target_pairs={{0,12},{4,0},{8,4},{12,8},{1,13},{5,1},{9,5},{13,9},{2,14},{6,2},{... | collective-permute-start | bytes 1769480 | tf_op jit(solution)/shard_map/ppermute | solution.py:545
  201.9 12.1 %collective-permute-start.35 = (bf16[144,2048]{1,0:T(8,128)(2,1)S(1)}, bf16[144,2048]{1,0:T(8,128)(2,1)S(1)}, u32[]{:S(2)}, u32[]{:S(2)}) collective-permute-start(bf16[144,2048]{1,0:T(8,128)(2,1)S(1)} %get-tuple-element.446), channel_id=1, source_target_pairs={{0,16},{16,32},{32,48},{48,0},{1,17},{17,33},{33,49},{49,1},{2,18}... | collective-permute-start | bytes 1769480 | tf_op jit(solution)/shard_map/ppermute | solution.py:545
  205.7 10.3 %collective-permute-start.36 = (bf16[144,2048]{1,0:T(8,128)(2,1)S(1)}, bf16[144,2048]{1,0:T(8,128)(2,1)S(1)}, u32[]{:S(2)}, u32[]{:S(2)}) collective-permute-start(bf16[144,2048]{1,0:T(8,128)(2,1)S(1)} %get-tuple-element.447), channel_id=1, source_target_pairs={{0,48},{16,0},{32,16},{48,32},{1,49},{17,1},{33,17},{49,33},{2,50}... | collective-permute-start | bytes 1769480 | tf_op jit(solution)/shard_map/ppermute | solution.py:545
  210.6 10.6 %collective-permute-start.34 = (bf16[80,2048]{1,0:T(8,128)(2,1)S(1)}, bf16[80,2048]{1,0:T(8,128)(2,1)S(1)}, u32[]{:S(2)}, u32[]{:S(2)}) collective-permute-start(bf16[80,2048]{1,0:T(8,128)(2,1)S(1)} %get-tuple-element.444), channel_id=1, source_target_pairs={{0,64},{64,0},{1,65},{65,1},{2,66},{66,2},{3,67},{67,3},{4,68},{68... | collective-permute-start | bytes 983048 | tf_op jit(solution)/shard_map/ppermute | solution.py:559
  216.8 8.7 %collective-permute-start.37 = (bf16[80,2048]{1,0:T(8,128)(2,1)S(1)}, bf16[80,2048]{1,0:T(8,128)(2,1)S(1)}, u32[]{:S(2)}, u32[]{:S(2)}) collective-permute-start(bf16[80,2048]{1,0:T(8,128)(2,1)S(1)} %get-tuple-element.450), channel_id=1, source_target_pairs={{0,64},{64,0},{1,65},{65,1},{2,66},{66,2},{3,67},{67,3},{4,68},{68... | collective-permute-start | bytes 983048 | tf_op jit(solution)/shard_map/ppermute | solution.py:559
  (16 other events, 81.5 us)

commit v4 on v3

--- a/solution.py
+++ b/solution.py
@@ -313,74 +313,64 @@
     return jnp.sum(block.astype(jnp.float32), axis=0, keepdims=True)
 
 
-def combine_kernel(place, *rest):
-    lefts = (rest[:4], rest[4:8])
-    dy, dz = rest[8:10]
-    arrivals = (rest[10:13], rest[13:16])
-    own_y, own_z, bias, *outs = rest[16:-2]
-    left_all, right = rest[-2:]
-    y, z = place[1], place[2]
-    total, rows, half = dy.shape
+def combine_kernel(place, *rest, side):
+    lefts, mine, arrivals = rest[:4], rest[4], rest[5:8]
+    own, bias, up, down, first, second, left_all, right = rest[8:]
+    other = place[2 - side]
+    total, rows, half = mine.shape
     n = total * rows
     fine = left_all.shape[2]
     ones = jnp.ones((EXTRA, 4 * n), jnp.bfloat16)
-    for side, (mine, other, own) in enumerate(((dy, z, own_y), (dz, y, own_z))):
+    for d in range(4):
+        block = mine if d == 0 else arrivals[d - 1]
+        right[pl.ds(d * n, n)] = block[...].reshape(n, half)
+        for g in range(4):
+            left_all[g, :, :, pl.ds(d * n, n)] = lefts[d][g]
+
+    def columns(step, carry):
+        cols = pl.ds(pl.multiple_of(step * COLS, COLS), COLS)
+        block = right[:, cols]
+        sums = dot(ones, block)[:1]
+        bias[:, cols] = sums
         for d in range(4):
-            block = mine if d == 0 else arrivals[side][d - 1]
-            right[pl.ds(d * n, n)] = block[...].reshape(n, half)
-            for g in range(4):
-                left_all[g, :, :, pl.ds(d * n, n)] = lefts[side][d][g]
-
-        def columns(step, carry, side=side, other=other, own=own):
-            at = pl.multiple_of(step * COLS, COLS)
-            cols = pl.ds(at, COLS)
-            block = right[:, cols]
-            sums = dot(ones, block)[:1]
-            bias[:, pl.ds(pl.multiple_of(at + side * half, COLS), COLS)] = sums
-            up, down, first, second = outs[4 * side : 4 * side + 4]
-            for d in range(4):
-                left = left_all[:, lax.rem(other + d, 4)].reshape(4 * fine, 4 * n)
-                part = dot(left, block)
-                if d == 0:
-                    own[:, :, cols] = part.reshape(4, fine, COLS)
-                elif d == 2:
-                    first[:, cols] = part[: 2 * fine].astype(jnp.bfloat16)
-                    second[pl.ds(0, 2 * fine), cols] = part[2 * fine :].astype(jnp.bfloat16)
-                    second[pl.ds(2 * fine, EXTRA), cols] = as_rows(sums)
-                else:
-                    to = up if d == 1 else down
-                    to[:, cols] = part
-            return carry
-
-        lax.fori_loop(0, half // COLS, columns, 0)
-
-
-def relay_kernel(place, bias, *rest):
-    outs = rest[8:]
-    for side in range(2):
-        up, down, first, second = rest[4 * side : 4 * side + 4]
-        ahead, behind = outs[2 * side : 2 * side + 2]
-        n, half = first.shape
-        def columns(step, carry, side=side, up=up, down=down, first=first, second=second, ahead=ahead, behind=behind):
-            start = pl.multiple_of(step * COLS, COLS)
-            cols = pl.ds(start, COLS)
-            sums = bias[:, pl.ds(pl.multiple_of(side * half + start, COLS), COLS)]
-            top, bottom = pl.ds(0, n), pl.ds(n, n)
-            ahead[top, cols] = (up[top, cols] + first[:, cols].astype(jnp.float32)).astype(jnp.bfloat16)
-            ahead[bottom, cols] = up[bottom, cols].astype(jnp.bfloat16)
-            ahead[pl.ds(2 * n, EXTRA), cols] = as_rows(sums)
-            behind[top, cols] = down[top, cols].astype(jnp.bfloat16)
-            behind[bottom, cols] = (down[bottom, cols] + second[top, cols].astype(jnp.float32)).astype(jnp.bfloat16)
-            behind[pl.ds(2 * n, EXTRA), cols] = as_rows(sums + from_rows(second[pl.ds(n, EXTRA), cols]))
-            return carry
-
-        lax.fori_loop(0, half // COLS, columns, 0)
-
-
-def finish_kernel(place, own, bias, ahead, behind, keep, kept_bias, give, *, side):
+            left = left_all[:, lax.rem(other + d, 4)].reshape(4 * fine, 4 * n)
+            part = dot(left, block)
+            if d == 0:
+                own[:, :, cols] = part.reshape(4, fine, COLS)
+            elif d == 2:
+                first[:, cols] = part[: 2 * fine].astype(jnp.bfloat16)
+                second[pl.ds(0, 2 * fine), cols] = part[2 * fine :].astype(jnp.bfloat16)
+                second[pl.ds(2 * fine, EXTRA), cols] = as_rows(sums)
+            else:
+                to = up if d == 1 else down
+                to[:, cols] = part
+        return carry
+
+    lax.fori_loop(0, half // COLS, columns, 0)
+
+
+def relay_kernel(place, bias, up, down, first, second, ahead, behind):
+    n, half = first.shape
+    top, bottom = pl.ds(0, n), pl.ds(n, n)
+
+    def columns(step, carry):
+        cols = pl.ds(pl.multiple_of(step * COLS, COLS), COLS)
+        sums = bias[:, cols]
+        ahead[top, cols] = (up[top, cols] + first[:, cols].astype(jnp.float32)).astype(jnp.bfloat16)
+        ahead[bottom, cols] = up[bottom, cols].astype(jnp.bfloat16)
+        ahead[pl.ds(2 * n, EXTRA), cols] = as_rows(sums)
+        behind[top, cols] = down[top, cols].astype(jnp.bfloat16)
+        behind[bottom, cols] = (down[bottom, cols] + second[top, cols].astype(jnp.float32)).astype(jnp.bfloat16)
+        behind[pl.ds(2 * n, EXTRA), cols] = as_rows(sums + from_rows(second[pl.ds(n, EXTRA), cols]))
+        return carry
+
+    lax.fori_loop(0, half // COLS, columns, 0)
+
+
+def finish_kernel(place, own, bias, ahead, behind, keep, kept_bias, give):
     blocks = (ahead, behind)
     xh = place[3]
-    fine, half = own.shape[1:]
+    fine = own.shape[1]
     for n in range(2):
         mine, other = 2 * n + xh, 2 * n + 1 - xh
         kept, given = own[mine], own[other]
@@ -389,7 +379,7 @@
             given += block[pl.ds(pl.multiple_of(other * fine, fine), fine)].astype(jnp.float32)
         keep[n] = kept
         give[pl.ds(n * fine, fine)] = given.astype(jnp.bfloat16)
-    total = bias[:, pl.ds(side * half, half)]
+    total = bias[...]
     for block in blocks:
         total += from_rows(block[pl.ds(4 * fine, EXTRA)])
     kept_bias[...] = total
@@ -532,31 +522,22 @@
     final_hidden, final_cell = hs[total], held[3][total]
     whole, far_part = shape((4, fine, half), f32), shape((4 * fine, half), f32)
     pieces = (far_part, far_part, shape((2 * fine, half), bf16), shape((2 * fine + EXTRA, half), bf16))
-    mine_y, mine_z, bias, *made = simple(
-        combine_kernel,
-        "combine",
-        (whole, whole, shape((1, gated), f32)) + pieces * 2,
-        16,
-        [pltpu.VMEM((4, 4, fine, 4 * total * rows), bf16), pltpu.VMEM((4 * total * rows, half), bf16)],
-    )(place, spread[0], *lefts[:3], spread[4], *lefts[3:], dy, dz, *passed([dy] * 3 + [dz] * 3))
-
-    def both_ways(ahead_z, behind_z, ahead_y, behind_y):
-        sent = ((ahead_z, "z", 0), (behind_z, "z", 2), (ahead_y, "y", 0), (behind_y, "y", 2))
-        return [near(lax.ppermute(v, axis, routes[d])) for v, axis, d in sent]
-
-    got = both_ways(made[2], made[3], made[6], made[7])
-    part = shape((4 * fine + EXTRA, half), bf16)
-    sends = simple(relay_kernel, "relay", (part,) * 4, 9)(place, bias, *made[:2], *got[:2], *made[4:6], *got[2:])
-    got = both_ways(*sends)
-    done = []
-    for side, mine in enumerate((mine_y, mine_z)):
-        keep, total_bias, give = simple(
-            partial(finish_kernel, side=side),
-            "finish",
-            (shape((2, fine, half), f32), shape((1, half), f32), shape((2 * fine + EXTRA, half), bf16)),
-            4,
-        )(place, mine, bias, *got[2 * side : 2 * side + 2])
-        done += [keep, total_bias, near(lax.ppermute(give, "xh", [(0, 1), (1, 0)]))]
+    part, bias_row = shape((4 * fine + EXTRA, half), bf16), shape((1, half), f32)
+    room = [pltpu.VMEM((4, 4, fine, 4 * total * rows), bf16), pltpu.VMEM((4 * total * rows, half), bf16)]
+
+    def ring(axis, ahead, behind):
+        return [near(lax.ppermute(v, axis, routes[d])) for v, d in ((ahead, 0), (behind, 2))]
+
+    arrivals, done = passed([dy] * 3 + [dz] * 3), []
+    for side, (mine, axis) in enumerate(((dy, "z"), (dz, "y"))):
+        three = slice(3 * side, 3 * side + 3)
+        own, bias, up, down, *pair = simple(partial(combine_kernel, side=side), "combine", (whole, bias_row) + pieces, 8, room)(
+            place, spread[4 * side], *lefts[three], mine, *arrivals[three]
+        )
+        pair = simple(relay_kernel, "relay", (part,) * 2, 5)(place, bias, up, down, *ring(axis, *pair))
+        outs = (shape((2, fine, half), f32), bias_row, shape((2 * fine + EXTRA, half), bf16))
+        keep, bias, give = simple(finish_kernel, "finish", outs, 4)(place, own, bias, *ring(axis, *pair))
+        done += [keep, bias, near(lax.ppermute(give, "xh", [(0, 1), (1, 0)]))]
     made = jax.ShapeDtypeStruct
     grad_i, grad_r, grad_b = simple(
         last_kernel,

time: 228 us -> 225 us (0.987)
  starting transfers between devices: 58.2 us -> 53.4 us
    ppermute x10, starting transfers between devices: 22.3 us -> 16.9 us  [the longest x8 10.8 us: ring(): lax.ppermute(v, axis, routes[d])]
    ppermute x10, waiting for transfers between devices: 15.2 us -> 18.9 us  [the longest x8 12.2 us: ring(): lax.ppermute(v, axis, routes[d])]
    ppermute x6, waiting for transfers between devices: 21 us -> 18 us  [passed(): lax.ppermute(made[n], 'y' if n < 3 else 'z', routes[n % 3])]
    pallas_call x4 -> x6, Pallas kernels: 9.69 us -> 10.8 us  [the longest x2 7.05 us: local(): simple(partial(combine_kernel, side=side), 'combine', (whole, bias_row) +...]
  transfers between devices with their start and end apart: 38 -> 38, of which waited for: 15 -> 13; matrix products, arithmetic and copies ran while one was open for 1% -> 1% of each run, Pallas kernels for 25% -> 29%
where the time goes in v4:
time: 225 us; the launch traced here: 224 us
  Pallas kernels  97.3 us (43%)
  waiting for transfers between devices  70.5 us (31%)
  starting transfers between devices  53.4 us (24%)
    pallas_call x10, Pallas kernels, local(): emitted, *held = forward(tick)(place, *got)  55.5 us
    ppermute x8, waiting for transfers between devices, local(): lax.ppermute(lower, 'pipe', [(s, s - 1) for s in on])  33.4 us
    pallas_call x10, Pallas kernels, local(): backward(tick)(place, cot, landed.get(tick, lower), lens, *held)  28.5 us
    ppermute x6, waiting for transfers between devices, passed(): lax.ppermute(made[n], 'y' if n < 3 else 'z', routes[n % 3])  18 us
    ppermute x6, starting transfers between devices, local(): piece = lax.ppermute(piece, axis, routes[d - 1])  14.4 us
    ppermute x8, waiting for transfers between devices, ring(): lax.ppermute(v, axis, routes[d])  12.2 us
    ppermute x8, starting transfers between devices, ring(): lax.ppermute(v, axis, routes[d])  10.8 us
    ppermute x8, starting transfers between devices, local(): lax.ppermute(lower, 'pipe', [(s, s - 1) for s in on])  7.94 us
  transfers between devices with their start and end apart: 38, of which 13 were waited for; matrix products, arithmetic and copies ran while one was open for 1% of the time, Pallas kernels for 29%

profile of v4, /device:TPU:0, one launch (start us, length us, event | category | flops | bytes accessed | tf_op | source)
XLA Modules:
  0.0 224.2 jit_solution(15153025660022353142)
XLA Ops:
  1.4 10.6 %forward_tick.10 = (bf16[4,8,1024]{2,1,0:T(8,128)(2,1)S(1)}, bf16[1024,4096]{1,0:T(8,128)(2,1)S(1)}, bf16[1024,4096]{1,0:T(8,128)(2,1)S(1)}, bf16[16,8,1024]{2,1...) custom-call(s32[4]{0:T(128)S(1)} %pad_add_fusion.place, ...), custom_call_target="tpu_custom_call" | custom-call | tf_op jit(solution)/shard_map/forward_tick/pallas_call | solution.py:462
  13.3 8.0 %forward_tick.11 = (bf16[4,8,1024]{2,1,0:T(8,128)(2,1)S(1)}, bf16[1024,4096]{1,0:T(8,128)(2,1)S(1)}, bf16[1024,4096]{1,0:T(8,128)(2,1)S(1)}, bf16[16,8,1024]{2,1...) custom-call(s32[4]{0:T(128)S(1)} %pad_add_fusion.place, ...), custom_call_target="tpu_custom_call", output_to_operand_aliasing={{1}: (4, {}), {2}: (5, {}), {3}: (6, {}), {4}: (7, {}), {5}... | custom-call | tf_op jit(solution)/shard_map/forward_tick/pallas_call | solution.py:462
  22.6 8.0 %forward_tick.12 = (bf16[4,8,1024]{2,1,0:T(8,128)(2,1)S(1)}, bf16[1024,4096]{1,0:T(8,128)(2,1)S(1)}, bf16[1024,4096]{1,0:T(8,128)(2,1)S(1)}, bf16[16,8,1024]{2,1...) custom-call(s32[4]{0:T(128)S(1)} %pad_add_fusion.place, ...), custom_call_target="tpu_custom_call", output_to_operand_aliasing={{1}: (4, {}), {2}: (5, {}), {3}: (6, {}), {4}: (7, {}), {5}... | custom-call | tf_op jit(solution)/shard_map/forward_tick/pallas_call | solution.py:462
  32.0 8.0 %forward_tick.13 = (bf16[4,8,1024]{2,1,0:T(8,128)(2,1)S(1)}, bf16[1024,4096]{1,0:T(8,128)(2,1)S(1)}, bf16[1024,4096]{1,0:T(8,128)(2,1)S(1)}, bf16[16,8,1024]{2,1...) custom-call(s32[4]{0:T(128)S(1)} %pad_add_fusion.place, ...), custom_call_target="tpu_custom_call", output_to_operand_aliasing={{1}: (4, {}), {2}: (5, {}), {3}: (6, {}), {4}: (7, {}), {5}... | custom-call | tf_op jit(solution)/shard_map/forward_tick/pallas_call | solution.py:462
  46.6 7.7 %forward_tick.18 = (bf16[4,8,1024]{2,1,0:T(8,128)(2,1)}, bf16[1024,4096]{1,0:T(8,128)(2,1)S(1)}, bf16[1024,4096]{1,0:T(8,128)(2,1)S(1)}, bf16[16,8,1024]{2,1,0:T...) custom-call(s32[4]{0:T(128)S(1)} %pad_add_fusion.place, ...), custom_call_target="tpu_custom_call", output_to_operand_aliasing={{1}: (4, {}), {2}: (5, {}), {3}: (6, {}), {4}: (7, {}), {5}... | custom-call | tf_op jit(solution)/shard_map/forward_tick/pallas_call | solution.py:462
  54.4 10.5 %forward_tick.19 = (bf16[4,8,1024]{2,1,0:T(8,128)(2,1)S(1)}, bf16[1024,4096]{1,0:T(8,128)(2,1)S(1)}, bf16[1024,4096]{1,0:T(8,128)(2,1)S(1)}, bf16[16,8,1024]{2,1...) custom-call(s32[4]{0:T(128)S(1)} %pad_add_fusion.place, ...), custom_call_target="tpu_custom_call", output_to_operand_aliasing={{1}: (4, {}), {2}: (5, {}), {3}: (6, {}), {4}: (7, {}), {5}... | custom-call | tf_op jit(solution)/shard_map/forward_tick/pallas_call | solution.py:462
  64.9 3.9 %backward_tick.10 = (bf16[4,8,1024]{2,1,0:T(8,128)(2,1)S(1)}, bf16[16,8,2048]{2,1,0:T(8,128)(2,1)S(1)}, bf16[16,8,2048]{2,1,0:T(8,128)(2,1)S(1)}, f32[16,8,4096]...) custom-call(s32[4]{0:T(128)S(1)} %pad_add_fusion.place, ...), custom_call_target="tpu_custom_call", output_to_operand_aliasing={{3}: (5, {}), {4}: (6, {}), {6}: (7, {})} | custom-call | tf_op jit(solution)/shard_map/backward_tick/pallas_call | solution.py:505
  85.1 3.7 %collective-permute-start.16 = (bf16[4,4,32,128]{3,2,1,0:T(8,128)(2,1)S(1)}, bf16[4,4,32,128]{3,2,1,0:T(8,128)(2,1)S(1)}, u32[]{:S(2)}, u32[]{:S(2)}) collective-permute-start(bf16[4,4,32,128]{3,2,1,0:T(8,128)(2,1)S(1)} %get-tuple-element.382), channel_id=1, source_target_pairs={{0,8},{4,12},{8,0},{12,4},{1,9},{5,13},{9,1},{13,5},{2,10},{6,14},... | collective-permute-start | bytes 393224 | tf_op jit(solution)/shard_map/ppermute | solution.py:517
  90.1 24.2 %collective-permute-done.17.arrived = bf16[4,8,1024]{2,1,0:T(8,128)(2,1)S(1)} collective-permute-done((bf16[4,8,1024]{2,1,0:T(8,128)(2,1)S(1)}, bf16[4,8,1024]{2,1,0:T(8,128)(2,1)S(1)}, u32[]{:S(2)}, u32[]{:S(2)}) %collective-permute-start.17) | collective-permute-done | bytes 65568 | tf_op jit(solution)/shard_map/ppermute | solution.py:513
  114.3 5.4 %backward_tick.16 = (bf16[4,8,1024]{2,1,0:T(8,128)(2,1)S(1)}, bf16[16,8,2048]{2,1,0:T(8,128)(2,1)S(1)}, bf16[16,8,2048]{2,1,0:T(8,128)(2,1)S(1)}, f32[16,8,4096]...) custom-call(s32[4]{0:T(128)S(1)} %pad_add_fusion.place, ...), custom_call_target="tpu_custom_call", output_to_operand_aliasing={{1}: (4, {}), {2}: (5, {}), {3}: (6, {}), {4}: (7, {}), {5}... | custom-call | tf_op jit(solution)/shard_map/backward_tick/pallas_call | solution.py:505
  123.4 3.5 %collective-permute-done.15.arrived = bf16[4,8,1024]{2,1,0:T(8,128)(2,1)S(1)} collective-permute-done((bf16[4,8,1024]{2,1,0:T(8,128)(2,1)S(1)}, bf16[4,8,1024]{2,1,0:T(8,128)(2,1)S(1)}, u32[]{:S(2)}, u32[]{:S(2)}) %collective-permute-start.15) | collective-permute-done | bytes 65568 | tf_op jit(solution)/shard_map/ppermute | solution.py:513
  126.9 5.4 %backward_tick.17 = (bf16[4,8,1024]{2,1,0:T(8,128)(2,1)S(1)}, bf16[16,8,2048]{2,1,0:T(8,128)(2,1)S(1)}, bf16[16,8,2048]{2,1,0:T(8,128)(2,1)S(1)}, f32[16,8,4096]...) custom-call(s32[4]{0:T(128)S(1)} %pad_add_fusion.place, ...), custom_call_target="tpu_custom_call", output_to_operand_aliasing={{1}: (4, {}), {2}: (5, {}), {3}: (6, {}), {4}: (7, {}), {5}... | custom-call | tf_op jit(solution)/shard_map/backward_tick/pallas_call | solution.py:505
  136.3 6.2 %backward_tick.18 = (bf16[4,8,1024]{2,1,0:T(8,128)(2,1)}, bf16[16,8,2048]{2,1,0:T(8,128)(2,1)S(1)}, bf16[16,8,2048]{2,1,0:T(8,128)(2,1)S(1)}, f32[16,8,4096]{2,1...) custom-call(s32[4]{0:T(128)S(1)} %pad_add_fusion.place, ...), custom_call_target="tpu_custom_call", output_to_operand_aliasing={{1}: (4, {}), {2}: (5, {}), {3}: (6, {}), {4}: (7, {}), {5}... | custom-call | tf_op jit(solution)/shard_map/backward_tick/pallas_call | solution.py:505
  145.5 4.8 %backward_tick.19 = (bf16[4,8,1024]{2,1,0:T(8,128)(2,1)}, bf16[16,8,2048]{2,1,0:T(8,128)(2,1)S(1)}, bf16[16,8,2048]{2,1,0:T(8,128)(2,1)S(1)}, f32[16,8,4096]{2,1...) custom-call(s32[4]{0:T(128)S(1)} %pad_add_fusion.place, ...), custom_call_target="tpu_custom_call", output_to_operand_aliasing={{1}: (4, {}), {2}: (5, {}), {3}: (6, {}), {4}: (7, {}), {5}... | custom-call | tf_op jit(solution)/shard_map/backward_tick/pallas_call | solution.py:505
  156.0 9.2 %collective-permute-done.32.rest_7_ = bf16[16,8,2048]{2,1,0:T(8,128)(2,1)S(1)} collective-permute-done((bf16[16,8,2048]{2,1,0:T(8,128)(2,1)S(1)}, bf16[16,8,2048]{2,1,0:T(8,128)(2,1)S(1)}, u32[]{:S(2)}, u32[]{:S(2)}) %collective-permute-start.32) | collective-permute-done | bytes 524320 | tf_op jit(solution)/shard_map/ppermute | solution.py:500
  167.7 7.0 %collective-permute-done.30.rest_5_ = bf16[16,8,2048]{2,1,0:T(8,128)(2,1)S(1)} collective-permute-done((bf16[16,8,2048]{2,1,0:T(8,128)(2,1)S(1)}, bf16[16,8,2048]{2,1,0:T(8,128)(2,1)S(1)}, u32[]{:S(2)}, u32[]{:S(2)}) %collective-permute-start.30) | collective-permute-done | bytes 524320 | tf_op jit(solution)/shard_map/ppermute | solution.py:500
  174.7 3.5 %combine.3 = (f32[4,32,2048]{2,1,0:T(8,128)S(1)}, f32[1,2048]{1,0:T(1,128)S(1)}, f32[128,2048]{1,0:T(8,128)S(1)}, f32[128,2048]{1,0:T(8,128)S(1)}, bf16[64,2048]...) custom-call(s32[4]{0:T(128)S(1)} %pad_add_fusion.place, bf16[4,4,32,128]{3,2,1,0:T(8,128)(2,1)S(1)} %get-tuple-element.437.rest_0_, ...), custom_call_target="tpu_custom_call" | custom-call | tf_op jit(solution)/shard_map/combine/pallas_call | solution.py:534
  178.4 3.5 %combine.2 = (f32[4,32,2048]{2,1,0:T(8,128)S(1)}, f32[1,2048]{1,0:T(1,128)S(1)}, f32[128,2048]{1,0:T(8,128)S(1)}, f32[128,2048]{1,0:T(8,128)S(1)}, bf16[64,2048]...) custom-call(s32[4]{0:T(128)S(1)} %pad_add_fusion.place, bf16[4,4,32,128]{3,2,1,0:T(8,128)(2,1)S(1)} %get-tuple-element.323.rest_0_, ...), custom_call_target="tpu_custom_call" | custom-call | tf_op jit(solution)/shard_map/combine/pallas_call | solution.py:534
  185.9 5.5 %collective-permute-done.33.first = bf16[64,2048]{1,0:T(8,128)(2,1)S(1)} collective-permute-done((bf16[64,2048]{1,0:T(8,128)(2,1)S(1)}, bf16[64,2048]{1,0:T(8,128)(2,1)S(1)}, u32[]{:S(2)}, u32[]{:S(2)}) %collective-permute-start.33) | collective-permute-done | bytes 262176 | tf_op jit(solution)/shard_map/ppermute | solution.py:529
  200.2 6.4 %collective-permute-done.35.ahead = bf16[144,2048]{1,0:T(8,128)(2,1)S(1)} collective-permute-done((bf16[144,2048]{1,0:T(8,128)(2,1)S(1)}, bf16[144,2048]{1,0:T(8,128)(2,1)S(1)}, u32[]{:S(2)}, u32[]{:S(2)}) %collective-permute-start.35) | collective-permute-done | bytes 589856 | tf_op jit(solution)/shard_map/ppermute | solution.py:529
  207.5 3.1 %collective-permute-start.37 = (bf16[80,2048]{1,0:T(8,128)(2,1)S(1)}, bf16[80,2048]{1,0:T(8,128)(2,1)S(1)}, u32[]{:S(2)}, u32[]{:S(2)}) collective-permute-start(bf16[80,2048]{1,0:T(8,128)(2,1)S(1)} %get-tuple-element.452), channel_id=1, source_target_pairs={{0,64},{64,0},{1,65},{65,1},{2,66},{66,2},{3,67},{67,3},{4,68},{68... | collective-permute-start | bytes 983048 | tf_op jit(solution)/shard_map/ppermute | solution.py:540
  211.6 3.1 %collective-permute-start.29 = (bf16[80,2048]{1,0:T(8,128)(2,1)S(1)}, bf16[80,2048]{1,0:T(8,128)(2,1)S(1)}, u32[]{:S(2)}, u32[]{:S(2)}) collective-permute-start(bf16[80,2048]{1,0:T(8,128)(2,1)S(1)} %get-tuple-element.436), channel_id=1, source_target_pairs={{0,64},{64,0},{1,65},{65,1},{2,66},{66,2},{3,67},{67,3},{4,68},{68... | collective-permute-start | bytes 983048 | tf_op jit(solution)/shard_map/ppermute | solution.py:540
  215.8 3.3 %collective-permute-done.37.rest_5_ = bf16[80,2048]{1,0:T(8,128)(2,1)S(1)} collective-permute-done((bf16[80,2048]{1,0:T(8,128)(2,1)S(1)}, bf16[80,2048]{1,0:T(8,128)(2,1)S(1)}, u32[]{:S(2)}, u32[]{:S(2)}) %collective-permute-start.37) | collective-permute-done | bytes 327712 | tf_op jit(solution)/shard_map/ppermute | solution.py:540
  219.1 3.5 %collective-permute-done.29.rest_2_ = bf16[80,2048]{1,0:T(8,128)(2,1)S(1)} collective-permute-done((bf16[80,2048]{1,0:T(8,128)(2,1)S(1)}, bf16[80,2048]{1,0:T(8,128)(2,1)S(1)}, u32[]{:S(2)}, u32[]{:S(2)}) %collective-permute-start.29) | collective-permute-done | bytes 327712 | tf_op jit(solution)/shard_map/ppermute | solution.py:540
  (87 shorter events, 65.2 us)
Async XLA Ops:
  21.3 10.6 %collective-permute-start = (bf16[4,8,1024]{2,1,0:T(8,128)(2,1)S(1)}, bf16[4,8,1024]{2,1,0:T(8,128)(2,1)S(1)}, u32[]{:S(2)}, u32[]{:S(2)}) collective-permute-start(bf16[4,8,1024]{2,1,0:T(8,128)(2,1)S(1)} %get-tuple-element.242), channel_id=1, source_target_pairs={{0,1},{4,5},{8,9},{12,13},{16,17},{20,21},{24,25},{28,29},{32,33},... | collective-permute-start | bytes 196616 | tf_op jit(solution)/shard_map/ppermute | solution.py:467
  30.7 10.6 %collective-permute-start.3 = (bf16[4,8,1024]{2,1,0:T(8,128)(2,1)S(1)}, bf16[4,8,1024]{2,1,0:T(8,128)(2,1)S(1)}, u32[]{:S(2)}, u32[]{:S(2)}) collective-permute-start(bf16[4,8,1024]{2,1,0:T(8,128)(2,1)S(1)} %get-tuple-element.260), channel_id=1, source_target_pairs={{0,1},{1,2},{4,5},{5,6},{8,9},{9,10},{12,13},{13,14},{16,17},{17,1... | collective-permute-start | bytes 196616 | tf_op jit(solution)/shard_map/ppermute | solution.py:467
  81.2 33.0 %collective-permute-start.18 = (bf16[4,4,32,128]{3,2,1,0:T(8,128)(2,1)S(1)}, bf16[4,4,32,128]{3,2,1,0:T(8,128)(2,1)S(1)}, u32[]{:S(2)}, u32[]{:S(2)}) collective-permute-start(bf16[4,4,32,128]{3,2,1,0:T(8,128)(2,1)S(1)} %get-tuple-element.386), channel_id=1, source_target_pairs={{0,4},{4,8},{8,12},{12,0},{1,5},{5,9},{9,13},{13,1},{2,6},{6,10},{... | collective-permute-start | bytes 393224 | tf_op jit(solution)/shard_map/ppermute | solution.py:517
  83.2 31.0 %collective-permute-start.17 = (bf16[4,8,1024]{2,1,0:T(8,128)(2,1)S(1)}, bf16[4,8,1024]{2,1,0:T(8,128)(2,1)S(1)}, u32[]{:S(2)}, u32[]{:S(2)}) collective-permute-start(bf16[4,8,1024]{2,1,0:T(8,128)(2,1)S(1)} %get-tuple-element.384), channel_id=1, source_target_pairs={{1,0},{2,1},{5,4},{6,5},{9,8},{10,9},{13,12},{14,13},{17,16},{18,1... | collective-permute-start | bytes 196616 | tf_op jit(solution)/shard_map/ppermute | solution.py:513
  85.1 41.8 %collective-permute-start.16 = (bf16[4,4,32,128]{3,2,1,0:T(8,128)(2,1)S(1)}, bf16[4,4,32,128]{3,2,1,0:T(8,128)(2,1)S(1)}, u32[]{:S(2)}, u32[]{:S(2)}) collective-permute-start(bf16[4,4,32,128]{3,2,1,0:T(8,128)(2,1)S(1)} %get-tuple-element.382), channel_id=1, source_target_pairs={{0,8},{4,12},{8,0},{12,4},{1,9},{5,13},{9,1},{13,5},{2,10},{6,14},... | collective-permute-start | bytes 393224 | tf_op jit(solution)/shard_map/ppermute | solution.py:517
  88.8 38.1 %collective-permute-start.15 = (bf16[4,8,1024]{2,1,0:T(8,128)(2,1)S(1)}, bf16[4,8,1024]{2,1,0:T(8,128)(2,1)S(1)}, u32[]{:S(2)}, u32[]{:S(2)}) collective-permute-start(bf16[4,8,1024]{2,1,0:T(8,128)(2,1)S(1)} %get-tuple-element.380), channel_id=1, source_target_pairs={{1,0},{2,1},{5,4},{6,5},{9,8},{10,9},{13,12},{14,13},{17,16},{18,1... | collective-permute-start | bytes 196616 | tf_op jit(solution)/shard_map/ppermute | solution.py:513
  119.6 16.6 %collective-permute-start.21 = (bf16[4,4,32,128]{3,2,1,0:T(8,128)(2,1)S(1)}, bf16[4,4,32,128]{3,2,1,0:T(8,128)(2,1)S(1)}, u32[]{:S(2)}, u32[]{:S(2)}) collective-permute-start(bf16[4,4,32,128]{3,2,1,0:T(8,128)(2,1)S(1)} %get-tuple-element.407), channel_id=1, source_target_pairs={{0,12},{4,0},{8,4},{12,8},{1,13},{5,1},{9,5},{13,9},{2,14},{6,2},{... | collective-permute-start | bytes 393224 | tf_op jit(solution)/shard_map/ppermute | solution.py:517
  122.1 14.2 %collective-permute-start.20 = (bf16[4,8,1024]{2,1,0:T(8,128)(2,1)S(1)}, bf16[4,8,1024]{2,1,0:T(8,128)(2,1)S(1)}, u32[]{:S(2)}, u32[]{:S(2)}) collective-permute-start(bf16[4,8,1024]{2,1,0:T(8,128)(2,1)S(1)} %get-tuple-element.405), channel_id=1, source_target_pairs={{1,0},{5,4},{9,8},{13,12},{17,16},{21,20},{25,24},{29,28},{33,32},... | collective-permute-start | bytes 196616 | tf_op jit(solution)/shard_map/ppermute | solution.py:513
  132.3 13.2 %collective-permute-start.19 = (bf16[4,8,1024]{2,1,0:T(8,128)(2,1)S(1)}, bf16[4,8,1024]{2,1,0:T(8,128)(2,1)S(1)}, u32[]{:S(2)}, u32[]{:S(2)}) collective-permute-start(bf16[4,8,1024]{2,1,0:T(8,128)(2,1)S(1)} %get-tuple-element.404), channel_id=1, source_target_pairs={{1,0},{5,4},{9,8},{13,12},{17,16},{21,20},{25,24},{29,28},{33,32},... | collective-permute-start | bytes 196616 | tf_op jit(solution)/shard_map/ppermute | solution.py:513
  150.3 14.9 %collective-permute-start.32 = (bf16[16,8,2048]{2,1,0:T(8,128)(2,1)S(1)}, bf16[16,8,2048]{2,1,0:T(8,128)(2,1)S(1)}, u32[]{:S(2)}, u32[]{:S(2)}) collective-permute-start(bf16[16,8,2048]{2,1,0:T(8,128)(2,1)S(1)} %get-tuple-element.441.rest_4_), channel_id=1, source_target_pairs={{0,12},{4,0},{8,4},{12,8},{1,13},{5,1},{9,5},{13,9},{2,14},{6,2},{... | collective-permute-start | bytes 1572872 | tf_op jit(solution)/shard_map/ppermute | solution.py:500
  151.3 16.4 %collective-permute-start.31 = (bf16[16,8,2048]{2,1,0:T(8,128)(2,1)S(1)}, bf16[16,8,2048]{2,1,0:T(8,128)(2,1)S(1)}, u32[]{:S(2)}, u32[]{:S(2)}) collective-permute-start(bf16[16,8,2048]{2,1,0:T(8,128)(2,1)S(1)} %get-tuple-element.441.rest_4_), channel_id=1, source_target_pairs={{0,8},{4,12},{8,0},{12,4},{1,9},{5,13},{9,1},{13,5},{2,10},{6,14},... | collective-permute-start | bytes 1572872 | tf_op jit(solution)/shard_map/ppermute | solution.py:500
  152.9 21.8 %collective-permute-start.30 = (bf16[16,8,2048]{2,1,0:T(8,128)(2,1)S(1)}, bf16[16,8,2048]{2,1,0:T(8,128)(2,1)S(1)}, u32[]{:S(2)}, u32[]{:S(2)}) collective-permute-start(bf16[16,8,2048]{2,1,0:T(8,128)(2,1)S(1)} %get-tuple-element.441.rest_4_), channel_id=1, source_target_pairs={{0,4},{4,8},{8,12},{12,0},{1,5},{5,9},{9,13},{13,1},{2,6},{6,10},{... | collective-permute-start | bytes 1572872 | tf_op jit(solution)/shard_map/ppermute | solution.py:500
  153.3 25.1 %collective-permute-start.24 = (bf16[16,8,2048]{2,1,0:T(8,128)(2,1)S(1)}, bf16[16,8,2048]{2,1,0:T(8,128)(2,1)S(1)}, u32[]{:S(2)}, u32[]{:S(2)}) collective-permute-start(bf16[16,8,2048]{2,1,0:T(8,128)(2,1)S(1)} %get-tuple-element.425.rest_4_), channel_id=1, source_target_pairs={{0,48},{16,0},{32,16},{48,32},{1,49},{17,1},{33,17},{49,33},{2,50}... | collective-permute-start | bytes 1572872 | tf_op jit(solution)/shard_map/ppermute | solution.py:500
  154.2 24.2 %collective-permute-start.23 = (bf16[16,8,2048]{2,1,0:T(8,128)(2,1)S(1)}, bf16[16,8,2048]{2,1,0:T(8,128)(2,1)S(1)}, u32[]{:S(2)}, u32[]{:S(2)}) collective-permute-start(bf16[16,8,2048]{2,1,0:T(8,128)(2,1)S(1)} %get-tuple-element.425.rest_4_), channel_id=1, source_target_pairs={{0,32},{16,48},{32,0},{48,16},{1,33},{17,49},{33,1},{49,17},{2,34}... | collective-permute-start | bytes 1572872 | tf_op jit(solution)/shard_map/ppermute | solution.py:500
  165.2 13.2 %collective-permute-start.22 = (bf16[16,8,2048]{2,1,0:T(8,128)(2,1)S(1)}, bf16[16,8,2048]{2,1,0:T(8,128)(2,1)S(1)}, u32[]{:S(2)}, u32[]{:S(2)}) collective-permute-start(bf16[16,8,2048]{2,1,0:T(8,128)(2,1)S(1)} %get-tuple-element.425.rest_4_), channel_id=1, source_target_pairs={{0,16},{16,32},{32,48},{48,0},{1,17},{17,33},{33,49},{49,1},{2,18}... | collective-permute-start | bytes 1572872 | tf_op jit(solution)/shard_map/ppermute | solution.py:500
  178.2 13.3 %collective-permute-start.34 = (bf16[80,2048]{1,0:T(8,128)(2,1)S(1)}, bf16[80,2048]{1,0:T(8,128)(2,1)S(1)}, u32[]{:S(2)}, u32[]{:S(2)}) collective-permute-start(bf16[80,2048]{1,0:T(8,128)(2,1)S(1)} %get-tuple-element.447), channel_id=1, source_target_pairs={{0,48},{16,0},{32,16},{48,32},{1,49},{17,1},{33,17},{49,33},{2,50}... | collective-permute-start | bytes 983048 | tf_op jit(solution)/shard_map/ppermute | solution.py:529
  181.9 13.9 %collective-permute-start.26 = (bf16[80,2048]{1,0:T(8,128)(2,1)S(1)}, bf16[80,2048]{1,0:T(8,128)(2,1)S(1)}, u32[]{:S(2)}, u32[]{:S(2)}) collective-permute-start(bf16[80,2048]{1,0:T(8,128)(2,1)S(1)} %get-tuple-element.431), channel_id=1, source_target_pairs={{0,12},{4,0},{8,4},{12,8},{1,13},{5,1},{9,5},{13,9},{2,14},{6,2},{... | collective-permute-start | bytes 983048 | tf_op jit(solution)/shard_map/ppermute | solution.py:529
  184.5 11.3 %collective-permute-start.25 = (bf16[64,2048]{1,0:T(8,128)(2,1)S(1)}, bf16[64,2048]{1,0:T(8,128)(2,1)S(1)}, u32[]{:S(2)}, u32[]{:S(2)}) collective-permute-start(bf16[64,2048]{1,0:T(8,128)(2,1)S(1)} %get-tuple-element.430), channel_id=1, source_target_pairs={{0,4},{4,8},{8,12},{12,0},{1,5},{5,9},{9,13},{13,1},{2,6},{6,10},{... | collective-permute-start | bytes 786440 | tf_op jit(solution)/shard_map/ppermute | solution.py:529
  192.5 14.1 %collective-permute-start.35 = (bf16[144,2048]{1,0:T(8,128)(2,1)S(1)}, bf16[144,2048]{1,0:T(8,128)(2,1)S(1)}, u32[]{:S(2)}, u32[]{:S(2)}) collective-permute-start(bf16[144,2048]{1,0:T(8,128)(2,1)S(1)} %get-tuple-element.448), channel_id=1, source_target_pairs={{0,16},{16,32},{32,48},{48,0},{1,17},{17,33},{33,49},{49,1},{2,18}... | collective-permute-start | bytes 1769480 | tf_op jit(solution)/shard_map/ppermute | solution.py:529
  193.1 13.5 %collective-permute-start.36 = (bf16[144,2048]{1,0:T(8,128)(2,1)S(1)}, bf16[144,2048]{1,0:T(8,128)(2,1)S(1)}, u32[]{:S(2)}, u32[]{:S(2)}) collective-permute-start(bf16[144,2048]{1,0:T(8,128)(2,1)S(1)} %get-tuple-element.449), channel_id=1, source_target_pairs={{0,48},{16,0},{32,16},{48,32},{1,49},{17,1},{33,17},{49,33},{2,50}... | collective-permute-start | bytes 1769480 | tf_op jit(solution)/shard_map/ppermute | solution.py:529
  196.9 13.6 %collective-permute-start.27 = (bf16[144,2048]{1,0:T(8,128)(2,1)S(1)}, bf16[144,2048]{1,0:T(8,128)(2,1)S(1)}, u32[]{:S(2)}, u32[]{:S(2)}) collective-permute-start(bf16[144,2048]{1,0:T(8,128)(2,1)S(1)} %get-tuple-element.432), channel_id=1, source_target_pairs={{0,4},{4,8},{8,12},{12,0},{1,5},{5,9},{9,13},{13,1},{2,6},{6,10},{... | collective-permute-start | bytes 1769480 | tf_op jit(solution)/shard_map/ppermute | solution.py:529
  198.7 12.1 %collective-permute-start.28 = (bf16[144,2048]{1,0:T(8,128)(2,1)S(1)}, bf16[144,2048]{1,0:T(8,128)(2,1)S(1)}, u32[]{:S(2)}, u32[]{:S(2)}) collective-permute-start(bf16[144,2048]{1,0:T(8,128)(2,1)S(1)} %get-tuple-element.433), channel_id=1, source_target_pairs={{0,12},{4,0},{8,4},{12,8},{1,13},{5,1},{9,5},{13,9},{2,14},{6,2},{... | collective-permute-start | bytes 1769480 | tf_op jit(solution)/shard_map/ppermute | solution.py:529
  207.5 11.6 %collective-permute-start.37 = (bf16[80,2048]{1,0:T(8,128)(2,1)S(1)}, bf16[80,2048]{1,0:T(8,128)(2,1)S(1)}, u32[]{:S(2)}, u32[]{:S(2)}) collective-permute-start(bf16[80,2048]{1,0:T(8,128)(2,1)S(1)} %get-tuple-element.452), channel_id=1, source_target_pairs={{0,64},{64,0},{1,65},{65,1},{2,66},{66,2},{3,67},{67,3},{4,68},{68... | collective-permute-start | bytes 983048 | tf_op jit(solution)/shard_map/ppermute | solution.py:540
  211.6 11.0 %collective-permute-start.29 = (bf16[80,2048]{1,0:T(8,128)(2,1)S(1)}, bf16[80,2048]{1,0:T(8,128)(2,1)S(1)}, u32[]{:S(2)}, u32[]{:S(2)}) collective-permute-start(bf16[80,2048]{1,0:T(8,128)(2,1)S(1)} %get-tuple-element.436), channel_id=1, source_target_pairs={{0,64},{64,0},{1,65},{65,1},{2,66},{66,2},{3,67},{67,3},{4,68},{68... | collective-permute-start | bytes 983048 | tf_op jit(solution)/shard_map/ppermute | solution.py:540
  (16 other events, 83.8 us)

commit v5 on v4

--- a/solution.py
+++ b/solution.py
@@ -500,7 +500,7 @@
         return [near(lax.ppermute(made[n], "y" if n < 3 else "z", routes[n % 3])) for n in range(6)]
 
     group = shape((4, 4, fine, total * rows), bf16)
-    lefts, landed, lower = [], {}, emitted
+    lefts, landed, lower = {}, {}, emitted
     for tick in range(ticks):
         lower, *held = backward(tick)(place, cot, landed.get(tick, lower), lens, *held)
         if tick == 0:
@@ -512,12 +512,12 @@
         if on:
             landed[tick + LAG] = near(lax.ppermute(lower, "pipe", [(s, s - 1) for s in on]))
         if 1 <= tick <= 6:
-            axis, d = ("y", tick) if tick < 4 else ("z", tick - 3)
-            piece, _ = lax.optimization_barrier((spread[tick if tick < 4 else tick + 1], lower))
+            axis, d = (("y", 2), ("z", 2), ("y", 1), ("y", 3), ("z", 1), ("z", 3))[tick - 1]
+            piece, _ = lax.optimization_barrier((spread[d if axis == "y" else 4 + d], lower))
             piece = lax.ppermute(piece, axis, routes[d - 1])
             pair = lax.optimization_barrier((landed[tick + LAG], piece))
             landed[tick + LAG], piece = map(near, pair)
-            lefts.append(piece)
+            lefts[axis, d] = piece
     dy, dz = held[:2]
     final_hidden, final_cell = hs[total], held[3][total]
     whole, far_part = shape((4, fine, half), f32), shape((4 * fine, half), f32)
@@ -531,8 +531,9 @@
     arrivals, done = passed([dy] * 3 + [dz] * 3), []
     for side, (mine, axis) in enumerate(((dy, "z"), (dz, "y"))):
         three = slice(3 * side, 3 * side + 3)
+        near_side = [lefts["yz"[side], d] for d in range(1, 4)]
         own, bias, up, down, *pair = simple(partial(combine_kernel, side=side), "combine", (whole, bias_row) + pieces, 8, room)(
-            place, spread[4 * side], *lefts[three], mine, *arrivals[three]
+            place, spread[4 * side], *near_side, mine, *arrivals[three]
         )
         pair = simple(relay_kernel, "relay", (part,) * 2, 5)(place, bias, up, down, *ring(axis, *pair))
         outs = (shape((2, fine, half), f32), bias_row, shape((2 * fine + EXTRA, half), bf16))

time: 225 us -> 228 us (1.013)
  waiting for transfers between devices: 70.5 us -> 76.8 us
  starting transfers between devices: 53.4 us -> 50.8 us
    ppermute x6, waiting for transfers between devices: 18 us -> 23.3 us  [passed(): lax.ppermute(made[n], 'y' if n < 3 else 'z', routes[n % 3])]
    ppermute x2, waiting for transfers between devices: 6.77 us -> 4.32 us  [local(): done += [keep, bias, near(lax.ppermute(give, 'xh', [(0, 1), (1, 0)]))]]
where the time goes in v5:
time: 228 us
  Pallas kernels  97.3 us (43%)
  waiting for transfers between devices  76.8 us (34%)
  starting transfers between devices  50.8 us (22%)
    pallas_call x10, Pallas kernels, local(): emitted, *held = forward(tick)(place, *got)  55.5 us
    ppermute x8, waiting for transfers between devices, local(): lax.ppermute(lower, 'pipe', [(s, s - 1) for s in on])  33.8 us
    pallas_call x10, Pallas kernels, local(): backward(tick)(place, cot, landed.get(tick, lower), lens, *held)  28.5 us
    ppermute x6, waiting for transfers between devices, passed(): lax.ppermute(made[n], 'y' if n < 3 else 'z', routes[n % 3])  23.3 us
    ppermute x8, waiting for transfers between devices, ring(): lax.ppermute(v, axis, routes[d])  14.3 us
    ppermute x6, starting transfers between devices, local(): piece = lax.ppermute(piece, axis, routes[d - 1])  13 us
    ppermute x8, starting transfers between devices, ring(): lax.ppermute(v, axis, routes[d])  10.8 us
    ppermute x8, starting transfers between devices, local(): lax.ppermute(lower, 'pipe', [(s, s - 1) for s in on])  7.94 us
  transfers between devices with their start and end apart: 38, of which 13 were waited for; matrix products, arithmetic and copies ran while one was open for 1% of the time, Pallas kernels for 29%

profile of v5, /device:TPU:0, one launch (start us, length us, event | category | flops | bytes accessed | tf_op | source)
XLA Modules:
  0.0 227.9 jit_solution(3593453788427416157)
XLA Ops:
  1.4 10.6 %forward_tick.10 = (bf16[4,8,1024]{2,1,0:T(8,128)(2,1)S(1)}, bf16[1024,4096]{1,0:T(8,128)(2,1)S(1)}, bf16[1024,4096]{1,0:T(8,128)(2,1)S(1)}, bf16[16,8,1024]{2,1...) custom-call(s32[4]{0:T(128)S(1)} %pad_add_fusion.place, ...), custom_call_target="tpu_custom_call" | custom-call | tf_op jit(solution)/shard_map/forward_tick/pallas_call | solution.py:462
  13.3 8.0 %forward_tick.11 = (bf16[4,8,1024]{2,1,0:T(8,128)(2,1)S(1)}, bf16[1024,4096]{1,0:T(8,128)(2,1)S(1)}, bf16[1024,4096]{1,0:T(8,128)(2,1)S(1)}, bf16[16,8,1024]{2,1...) custom-call(s32[4]{0:T(128)S(1)} %pad_add_fusion.place, ...), custom_call_target="tpu_custom_call", output_to_operand_aliasing={{1}: (4, {}), {2}: (5, {}), {3}: (6, {}), {4}: (7, {}), {5}... | custom-call | tf_op jit(solution)/shard_map/forward_tick/pallas_call | solution.py:462
  22.6 8.0 %forward_tick.12 = (bf16[4,8,1024]{2,1,0:T(8,128)(2,1)S(1)}, bf16[1024,4096]{1,0:T(8,128)(2,1)S(1)}, bf16[1024,4096]{1,0:T(8,128)(2,1)S(1)}, bf16[16,8,1024]{2,1...) custom-call(s32[4]{0:T(128)S(1)} %pad_add_fusion.place, ...), custom_call_target="tpu_custom_call", output_to_operand_aliasing={{1}: (4, {}), {2}: (5, {}), {3}: (6, {}), {4}: (7, {}), {5}... | custom-call | tf_op jit(solution)/shard_map/forward_tick/pallas_call | solution.py:462
  32.0 8.0 %forward_tick.13 = (bf16[4,8,1024]{2,1,0:T(8,128)(2,1)S(1)}, bf16[1024,4096]{1,0:T(8,128)(2,1)S(1)}, bf16[1024,4096]{1,0:T(8,128)(2,1)S(1)}, bf16[16,8,1024]{2,1...) custom-call(s32[4]{0:T(128)S(1)} %pad_add_fusion.place, ...), custom_call_target="tpu_custom_call", output_to_operand_aliasing={{1}: (4, {}), {2}: (5, {}), {3}: (6, {}), {4}: (7, {}), {5}... | custom-call | tf_op jit(solution)/shard_map/forward_tick/pallas_call | solution.py:462
  46.6 7.7 %forward_tick.18 = (bf16[4,8,1024]{2,1,0:T(8,128)(2,1)}, bf16[1024,4096]{1,0:T(8,128)(2,1)S(1)}, bf16[1024,4096]{1,0:T(8,128)(2,1)S(1)}, bf16[16,8,1024]{2,1,0:T...) custom-call(s32[4]{0:T(128)S(1)} %pad_add_fusion.place, ...), custom_call_target="tpu_custom_call", output_to_operand_aliasing={{1}: (4, {}), {2}: (5, {}), {3}: (6, {}), {4}: (7, {}), {5}... | custom-call | tf_op jit(solution)/shard_map/forward_tick/pallas_call | solution.py:462
  54.4 10.5 %forward_tick.19 = (bf16[4,8,1024]{2,1,0:T(8,128)(2,1)S(1)}, bf16[1024,4096]{1,0:T(8,128)(2,1)S(1)}, bf16[1024,4096]{1,0:T(8,128)(2,1)S(1)}, bf16[16,8,1024]{2,1...) custom-call(s32[4]{0:T(128)S(1)} %pad_add_fusion.place, ...), custom_call_target="tpu_custom_call", output_to_operand_aliasing={{1}: (4, {}), {2}: (5, {}), {3}: (6, {}), {4}: (7, {}), {5}... | custom-call | tf_op jit(solution)/shard_map/forward_tick/pallas_call | solution.py:462
  64.9 3.9 %backward_tick.10 = (bf16[4,8,1024]{2,1,0:T(8,128)(2,1)S(1)}, bf16[16,8,2048]{2,1,0:T(8,128)(2,1)S(1)}, bf16[16,8,2048]{2,1,0:T(8,128)(2,1)S(1)}, f32[16,8,4096]...) custom-call(s32[4]{0:T(128)S(1)} %pad_add_fusion.place, ...), custom_call_target="tpu_custom_call", output_to_operand_aliasing={{3}: (5, {}), {4}: (6, {}), {6}: (7, {})} | custom-call | tf_op jit(solution)/shard_map/backward_tick/pallas_call | solution.py:505
  71.2 3.4 %collective-permute-start.9 = (bf16[4,4,32,128]{3,2,1,0:T(8,128)(2,1)S(1)}, bf16[4,4,32,128]{3,2,1,0:T(8,128)(2,1)S(1)}, u32[]{:S(2)}, u32[]{:S(2)}) collective-permute-start(bf16[4,4,32,128]{3,2,1,0:T(8,128)(2,1)S(1)} %get-tuple-element.335), channel_id=1, source_target_pairs={{0,32},{16,48},{32,0},{48,16},{1,33},{17,49},{33,1},{49,17},{2,34}... | collective-permute-start | bytes 393224 | tf_op jit(solution)/shard_map/ppermute | solution.py:517
  75.8 4.0 %collective-permute-start.14 = (bf16[4,4,32,128]{3,2,1,0:T(8,128)(2,1)S(1)}, bf16[4,4,32,128]{3,2,1,0:T(8,128)(2,1)S(1)}, u32[]{:S(2)}, u32[]{:S(2)}) collective-permute-start(bf16[4,4,32,128]{3,2,1,0:T(8,128)(2,1)S(1)} %get-tuple-element.360), channel_id=1, source_target_pairs={{0,8},{4,12},{8,0},{12,4},{1,9},{5,13},{9,1},{13,5},{2,10},{6,14},... | collective-permute-start | bytes 393224 | tf_op jit(solution)/shard_map/ppermute | solution.py:517
  91.4 24.6 %collective-permute-done.15.arrived = bf16[4,8,1024]{2,1,0:T(8,128)(2,1)S(1)} collective-permute-done((bf16[4,8,1024]{2,1,0:T(8,128)(2,1)S(1)}, bf16[4,8,1024]{2,1,0:T(8,128)(2,1)S(1)}, u32[]{:S(2)}, u32[]{:S(2)}) %collective-permute-start.15) | collective-permute-done | bytes 65568 | tf_op jit(solution)/shard_map/ppermute | solution.py:513
  116.0 5.4 %backward_tick.16 = (bf16[4,8,1024]{2,1,0:T(8,128)(2,1)S(1)}, bf16[16,8,2048]{2,1,0:T(8,128)(2,1)S(1)}, bf16[16,8,2048]{2,1,0:T(8,128)(2,1)S(1)}, f32[16,8,4096]...) custom-call(s32[4]{0:T(128)S(1)} %pad_add_fusion.place, ...), custom_call_target="tpu_custom_call", output_to_operand_aliasing={{1}: (4, {}), {2}: (5, {}), {3}: (6, {}), {4}: (7, {}), {5}... | custom-call | tf_op jit(solution)/shard_map/backward_tick/pallas_call | solution.py:505
  126.1 5.4 %backward_tick.17 = (bf16[4,8,1024]{2,1,0:T(8,128)(2,1)S(1)}, bf16[16,8,2048]{2,1,0:T(8,128)(2,1)S(1)}, bf16[16,8,2048]{2,1,0:T(8,128)(2,1)S(1)}, f32[16,8,4096]...) custom-call(s32[4]{0:T(128)S(1)} %pad_add_fusion.place, ...), custom_call_target="tpu_custom_call", output_to_operand_aliasing={{1}: (4, {}), {2}: (5, {}), {3}: (6, {}), {4}: (7, {}), {5}... | custom-call | tf_op jit(solution)/shard_map/backward_tick/pallas_call | solution.py:505
  132.7 3.9 %collective-permute-done.20.arrived = bf16[4,8,1024]{2,1,0:T(8,128)(2,1)S(1)} collective-permute-done((bf16[4,8,1024]{2,1,0:T(8,128)(2,1)S(1)}, bf16[4,8,1024]{2,1,0:T(8,128)(2,1)S(1)}, u32[]{:S(2)}, u32[]{:S(2)}) %collective-permute-start.20) | collective-permute-done | bytes 65568 | tf_op jit(solution)/shard_map/ppermute | solution.py:513
  136.7 6.2 %backward_tick.18 = (bf16[4,8,1024]{2,1,0:T(8,128)(2,1)}, bf16[16,8,2048]{2,1,0:T(8,128)(2,1)S(1)}, bf16[16,8,2048]{2,1,0:T(8,128)(2,1)S(1)}, f32[16,8,4096]{2,1...) custom-call(s32[4]{0:T(128)S(1)} %pad_add_fusion.place, ...), custom_call_target="tpu_custom_call", output_to_operand_aliasing={{1}: (4, {}), {2}: (5, {}), {3}: (6, {}), {4}: (7, {}), {5}... | custom-call | tf_op jit(solution)/shard_map/backward_tick/pallas_call | solution.py:505
  145.5 4.8 %backward_tick.19 = (bf16[4,8,1024]{2,1,0:T(8,128)(2,1)}, bf16[16,8,2048]{2,1,0:T(8,128)(2,1)S(1)}, bf16[16,8,2048]{2,1,0:T(8,128)(2,1)S(1)}, f32[16,8,4096]{2,1...) custom-call(s32[4]{0:T(128)S(1)} %pad_add_fusion.place, ...), custom_call_target="tpu_custom_call", output_to_operand_aliasing={{1}: (4, {}), {2}: (5, {}), {3}: (6, {}), {4}: (7, {}), {5}... | custom-call | tf_op jit(solution)/shard_map/backward_tick/pallas_call | solution.py:505
  155.4 16.9 %collective-permute-done.32.rest_7_ = bf16[16,8,2048]{2,1,0:T(8,128)(2,1)S(1)} collective-permute-done((bf16[16,8,2048]{2,1,0:T(8,128)(2,1)S(1)}, bf16[16,8,2048]{2,1,0:T(8,128)(2,1)S(1)}, u32[]{:S(2)}, u32[]{:S(2)}) %collective-permute-start.32) | collective-permute-done | bytes 524320 | tf_op jit(solution)/shard_map/ppermute | solution.py:500
  172.2 3.7 %collective-permute-done.30.rest_5_ = bf16[16,8,2048]{2,1,0:T(8,128)(2,1)S(1)} collective-permute-done((bf16[16,8,2048]{2,1,0:T(8,128)(2,1)S(1)}, bf16[16,8,2048]{2,1,0:T(8,128)(2,1)S(1)}, u32[]{:S(2)}, u32[]{:S(2)}) %collective-permute-start.30) | collective-permute-done | bytes 524320 | tf_op jit(solution)/shard_map/ppermute | solution.py:500
  175.9 3.5 %combine.3 = (f32[4,32,2048]{2,1,0:T(8,128)S(1)}, f32[1,2048]{1,0:T(1,128)S(1)}, f32[128,2048]{1,0:T(8,128)S(1)}, f32[128,2048]{1,0:T(8,128)S(1)}, bf16[64,2048]...) custom-call(s32[4]{0:T(128)S(1)} %pad_add_fusion.place, bf16[4,4,32,128]{3,2,1,0:T(8,128)(2,1)S(1)} %get-tuple-element.437.rest_0_, ...), custom_call_target="tpu_custom_call" | custom-call | tf_op jit(solution)/shard_map/combine/pallas_call | solution.py:535
  182.6 3.5 %combine.2 = (f32[4,32,2048]{2,1,0:T(8,128)S(1)}, f32[1,2048]{1,0:T(1,128)S(1)}, f32[128,2048]{1,0:T(8,128)S(1)}, f32[128,2048]{1,0:T(8,128)S(1)}, bf16[64,2048]...) custom-call(s32[4]{0:T(128)S(1)} %pad_add_fusion.place, bf16[4,4,32,128]{3,2,1,0:T(8,128)(2,1)S(1)} %get-tuple-element.323.rest_0_, ...), custom_call_target="tpu_custom_call" | custom-call | tf_op jit(solution)/shard_map/combine/pallas_call | solution.py:535
  186.1 3.7 %collective-permute-start.26 = (bf16[80,2048]{1,0:T(8,128)(2,1)S(1)}, bf16[80,2048]{1,0:T(8,128)(2,1)S(1)}, u32[]{:S(2)}, u32[]{:S(2)}) collective-permute-start(bf16[80,2048]{1,0:T(8,128)(2,1)S(1)} %get-tuple-element.431), channel_id=1, source_target_pairs={{0,12},{4,0},{8,4},{12,8},{1,13},{5,1},{9,5},{13,9},{2,14},{6,2},{... | collective-permute-start | bytes 983048 | tf_op jit(solution)/shard_map/ppermute | solution.py:529
  189.9 10.3 %collective-permute-done.33.first = bf16[64,2048]{1,0:T(8,128)(2,1)S(1)} collective-permute-done((bf16[64,2048]{1,0:T(8,128)(2,1)S(1)}, bf16[64,2048]{1,0:T(8,128)(2,1)S(1)}, u32[]{:S(2)}, u32[]{:S(2)}) %collective-permute-start.33) | collective-permute-done | bytes 262176 | tf_op jit(solution)/shard_map/ppermute | solution.py:529
  201.4 3.2 %collective-permute-start.36 = (bf16[144,2048]{1,0:T(8,128)(2,1)S(1)}, bf16[144,2048]{1,0:T(8,128)(2,1)S(1)}, u32[]{:S(2)}, u32[]{:S(2)}) collective-permute-start(bf16[144,2048]{1,0:T(8,128)(2,1)S(1)} %get-tuple-element.449), channel_id=1, source_target_pairs={{0,48},{16,0},{32,16},{48,32},{1,49},{17,1},{33,17},{49,33},{2,50}... | collective-permute-start | bytes 1769480 | tf_op jit(solution)/shard_map/ppermute | solution.py:529
  209.0 3.5 %collective-permute-done.35.ahead = bf16[144,2048]{1,0:T(8,128)(2,1)S(1)} collective-permute-done((bf16[144,2048]{1,0:T(8,128)(2,1)S(1)}, bf16[144,2048]{1,0:T(8,128)(2,1)S(1)}, u32[]{:S(2)}, u32[]{:S(2)}) %collective-permute-start.35) | collective-permute-done | bytes 589856 | tf_op jit(solution)/shard_map/ppermute | solution.py:529
  222.0 4.3 %collective-permute-done.29.rest_2_ = bf16[80,2048]{1,0:T(8,128)(2,1)S(1)} collective-permute-done((bf16[80,2048]{1,0:T(8,128)(2,1)S(1)}, bf16[80,2048]{1,0:T(8,128)(2,1)S(1)}, u32[]{:S(2)}, u32[]{:S(2)}) %collective-permute-start.29) | collective-permute-done | bytes 327712 | tf_op jit(solution)/shard_map/ppermute | solution.py:541
  (87 shorter events, 59.8 us)
Async XLA Ops:
  12.0 10.6 %collective-permute-start.1 = (bf16[4,8,1024]{2,1,0:T(8,128)(2,1)S(1)}, bf16[4,8,1024]{2,1,0:T(8,128)(2,1)S(1)}, u32[]{:S(2)}, u32[]{:S(2)}) collective-permute-start(bf16[4,8,1024]{2,1,0:T(8,128)(2,1)S(1)} %get-tuple-element.233.rest_2_), channel_id=1, source_target_pairs={{0,1},{4,5},{8,9},{12,13},{16,17},{20,21},{24,25},{28,29},{32,33},... | collective-permute-start | bytes 196616 | tf_op jit(solution)/shard_map/ppermute | solution.py:467
  21.3 10.6 %collective-permute-start = (bf16[4,8,1024]{2,1,0:T(8,128)(2,1)S(1)}, bf16[4,8,1024]{2,1,0:T(8,128)(2,1)S(1)}, u32[]{:S(2)}, u32[]{:S(2)}) collective-permute-start(bf16[4,8,1024]{2,1,0:T(8,128)(2,1)S(1)} %get-tuple-element.242), channel_id=1, source_target_pairs={{0,1},{4,5},{8,9},{12,13},{16,17},{20,21},{24,25},{28,29},{32,33},... | collective-permute-start | bytes 196616 | tf_op jit(solution)/shard_map/ppermute | solution.py:467
  30.7 10.6 %collective-permute-start.3 = (bf16[4,8,1024]{2,1,0:T(8,128)(2,1)S(1)}, bf16[4,8,1024]{2,1,0:T(8,128)(2,1)S(1)}, u32[]{:S(2)}, u32[]{:S(2)}) collective-permute-start(bf16[4,8,1024]{2,1,0:T(8,128)(2,1)S(1)} %get-tuple-element.260), channel_id=1, source_target_pairs={{0,1},{1,2},{4,5},{5,6},{8,9},{9,10},{12,13},{13,14},{16,17},{17,1... | collective-permute-start | bytes 196616 | tf_op jit(solution)/shard_map/ppermute | solution.py:467
  83.2 32.8 %collective-permute-start.16 = (bf16[4,4,32,128]{3,2,1,0:T(8,128)(2,1)S(1)}, bf16[4,4,32,128]{3,2,1,0:T(8,128)(2,1)S(1)}, u32[]{:S(2)}, u32[]{:S(2)}) collective-permute-start(bf16[4,4,32,128]{3,2,1,0:T(8,128)(2,1)S(1)} %get-tuple-element.372), channel_id=1, source_target_pairs={{0,48},{16,0},{32,16},{48,32},{1,49},{17,1},{33,17},{49,33},{2,50}... | collective-permute-start | bytes 393224 | tf_op jit(solution)/shard_map/ppermute | solution.py:517
  85.6 30.4 %collective-permute-start.15 = (bf16[4,8,1024]{2,1,0:T(8,128)(2,1)S(1)}, bf16[4,8,1024]{2,1,0:T(8,128)(2,1)S(1)}, u32[]{:S(2)}, u32[]{:S(2)}) collective-permute-start(bf16[4,8,1024]{2,1,0:T(8,128)(2,1)S(1)} %get-tuple-element.370), channel_id=1, source_target_pairs={{1,0},{2,1},{5,4},{6,5},{9,8},{10,9},{13,12},{14,13},{17,16},{18,1... | collective-permute-start | bytes 196616 | tf_op jit(solution)/shard_map/ppermute | solution.py:513
  88.3 37.7 %collective-permute-start.18 = (bf16[4,4,32,128]{3,2,1,0:T(8,128)(2,1)S(1)}, bf16[4,4,32,128]{3,2,1,0:T(8,128)(2,1)S(1)}, u32[]{:S(2)}, u32[]{:S(2)}) collective-permute-start(bf16[4,4,32,128]{3,2,1,0:T(8,128)(2,1)S(1)} %get-tuple-element.385), channel_id=1, source_target_pairs={{0,4},{4,8},{8,12},{12,0},{1,5},{5,9},{9,13},{13,1},{2,6},{6,10},{... | collective-permute-start | bytes 393224 | tf_op jit(solution)/shard_map/ppermute | solution.py:517
  90.1 35.9 %collective-permute-start.17 = (bf16[4,8,1024]{2,1,0:T(8,128)(2,1)S(1)}, bf16[4,8,1024]{2,1,0:T(8,128)(2,1)S(1)}, u32[]{:S(2)}, u32[]{:S(2)}) collective-permute-start(bf16[4,8,1024]{2,1,0:T(8,128)(2,1)S(1)} %get-tuple-element.383), channel_id=1, source_target_pairs={{1,0},{2,1},{5,4},{6,5},{9,8},{10,9},{13,12},{14,13},{17,16},{18,1... | collective-permute-start | bytes 196616 | tf_op jit(solution)/shard_map/ppermute | solution.py:513
  121.4 15.3 %collective-permute-start.21 = (bf16[4,4,32,128]{3,2,1,0:T(8,128)(2,1)S(1)}, bf16[4,4,32,128]{3,2,1,0:T(8,128)(2,1)S(1)}, u32[]{:S(2)}, u32[]{:S(2)}) collective-permute-start(bf16[4,4,32,128]{3,2,1,0:T(8,128)(2,1)S(1)} %get-tuple-element.407), channel_id=1, source_target_pairs={{0,12},{4,0},{8,4},{12,8},{1,13},{5,1},{9,5},{13,9},{2,14},{6,2},{... | collective-permute-start | bytes 393224 | tf_op jit(solution)/shard_map/ppermute | solution.py:517
  122.1 14.5 %collective-permute-start.20 = (bf16[4,8,1024]{2,1,0:T(8,128)(2,1)S(1)}, bf16[4,8,1024]{2,1,0:T(8,128)(2,1)S(1)}, u32[]{:S(2)}, u32[]{:S(2)}) collective-permute-start(bf16[4,8,1024]{2,1,0:T(8,128)(2,1)S(1)} %get-tuple-element.405), channel_id=1, source_target_pairs={{1,0},{5,4},{9,8},{13,12},{17,16},{21,20},{25,24},{29,28},{33,32},... | collective-permute-start | bytes 196616 | tf_op jit(solution)/shard_map/ppermute | solution.py:513
  131.4 14.1 %collective-permute-start.19 = (bf16[4,8,1024]{2,1,0:T(8,128)(2,1)S(1)}, bf16[4,8,1024]{2,1,0:T(8,128)(2,1)S(1)}, u32[]{:S(2)}, u32[]{:S(2)}) collective-permute-start(bf16[4,8,1024]{2,1,0:T(8,128)(2,1)S(1)} %get-tuple-element.404), channel_id=1, source_target_pairs={{1,0},{5,4},{9,8},{13,12},{17,16},{21,20},{25,24},{29,28},{33,32},... | collective-permute-start | bytes 196616 | tf_op jit(solution)/shard_map/ppermute | solution.py:513
  150.3 21.9 %collective-permute-start.32 = (bf16[16,8,2048]{2,1,0:T(8,128)(2,1)S(1)}, bf16[16,8,2048]{2,1,0:T(8,128)(2,1)S(1)}, u32[]{:S(2)}, u32[]{:S(2)}) collective-permute-start(bf16[16,8,2048]{2,1,0:T(8,128)(2,1)S(1)} %get-tuple-element.441.rest_4_), channel_id=1, source_target_pairs={{0,12},{4,0},{8,4},{12,8},{1,13},{5,1},{9,5},{13,9},{2,14},{6,2},{... | collective-permute-start | bytes 1572872 | tf_op jit(solution)/shard_map/ppermute | solution.py:500
  152.5 19.7 %collective-permute-start.31 = (bf16[16,8,2048]{2,1,0:T(8,128)(2,1)S(1)}, bf16[16,8,2048]{2,1,0:T(8,128)(2,1)S(1)}, u32[]{:S(2)}, u32[]{:S(2)}) collective-permute-start(bf16[16,8,2048]{2,1,0:T(8,128)(2,1)S(1)} %get-tuple-element.441.rest_4_), channel_id=1, source_target_pairs={{0,8},{4,12},{8,0},{12,4},{1,9},{5,13},{9,1},{13,5},{2,10},{6,14},... | collective-permute-start | bytes 1572872 | tf_op jit(solution)/shard_map/ppermute | solution.py:500
  153.2 22.7 %collective-permute-start.30 = (bf16[16,8,2048]{2,1,0:T(8,128)(2,1)S(1)}, bf16[16,8,2048]{2,1,0:T(8,128)(2,1)S(1)}, u32[]{:S(2)}, u32[]{:S(2)}) collective-permute-start(bf16[16,8,2048]{2,1,0:T(8,128)(2,1)S(1)} %get-tuple-element.441.rest_4_), channel_id=1, source_target_pairs={{0,4},{4,8},{8,12},{12,0},{1,5},{5,9},{9,13},{13,1},{2,6},{6,10},{... | collective-permute-start | bytes 1572872 | tf_op jit(solution)/shard_map/ppermute | solution.py:500
  153.6 26.3 %collective-permute-start.24 = (bf16[16,8,2048]{2,1,0:T(8,128)(2,1)S(1)}, bf16[16,8,2048]{2,1,0:T(8,128)(2,1)S(1)}, u32[]{:S(2)}, u32[]{:S(2)}) collective-permute-start(bf16[16,8,2048]{2,1,0:T(8,128)(2,1)S(1)} %get-tuple-element.425.rest_4_), channel_id=1, source_target_pairs={{0,48},{16,0},{32,16},{48,32},{1,49},{17,1},{33,17},{49,33},{2,50}... | collective-permute-start | bytes 1572872 | tf_op jit(solution)/shard_map/ppermute | solution.py:500
  154.6 25.2 %collective-permute-start.23 = (bf16[16,8,2048]{2,1,0:T(8,128)(2,1)S(1)}, bf16[16,8,2048]{2,1,0:T(8,128)(2,1)S(1)}, u32[]{:S(2)}, u32[]{:S(2)}) collective-permute-start(bf16[16,8,2048]{2,1,0:T(8,128)(2,1)S(1)} %get-tuple-element.425.rest_4_), channel_id=1, source_target_pairs={{0,32},{16,48},{32,0},{48,16},{1,33},{17,49},{33,1},{49,17},{2,34}... | collective-permute-start | bytes 1572872 | tf_op jit(solution)/shard_map/ppermute | solution.py:500
  172.2 10.4 %collective-permute-start.22 = (bf16[16,8,2048]{2,1,0:T(8,128)(2,1)S(1)}, bf16[16,8,2048]{2,1,0:T(8,128)(2,1)S(1)}, u32[]{:S(2)}, u32[]{:S(2)}) collective-permute-start(bf16[16,8,2048]{2,1,0:T(8,128)(2,1)S(1)} %get-tuple-element.425.rest_4_), channel_id=1, source_target_pairs={{0,16},{16,32},{32,48},{48,0},{1,17},{17,33},{33,49},{49,1},{2,18}... | collective-permute-start | bytes 1572872 | tf_op jit(solution)/shard_map/ppermute | solution.py:500
  179.4 20.8 %collective-permute-start.34 = (bf16[80,2048]{1,0:T(8,128)(2,1)S(1)}, bf16[80,2048]{1,0:T(8,128)(2,1)S(1)}, u32[]{:S(2)}, u32[]{:S(2)}) collective-permute-start(bf16[80,2048]{1,0:T(8,128)(2,1)S(1)} %get-tuple-element.447), channel_id=1, source_target_pairs={{0,48},{16,0},{32,16},{48,32},{1,49},{17,1},{33,17},{49,33},{2,50}... | collective-permute-start | bytes 983048 | tf_op jit(solution)/shard_map/ppermute | solution.py:529
  186.1 18.4 %collective-permute-start.26 = (bf16[80,2048]{1,0:T(8,128)(2,1)S(1)}, bf16[80,2048]{1,0:T(8,128)(2,1)S(1)}, u32[]{:S(2)}, u32[]{:S(2)}) collective-permute-start(bf16[80,2048]{1,0:T(8,128)(2,1)S(1)} %get-tuple-element.431), channel_id=1, source_target_pairs={{0,12},{4,0},{8,4},{12,8},{1,13},{5,1},{9,5},{13,9},{2,14},{6,2},{... | collective-permute-start | bytes 983048 | tf_op jit(solution)/shard_map/ppermute | solution.py:529
  189.9 10.3 %collective-permute-start.33 = (bf16[64,2048]{1,0:T(8,128)(2,1)S(1)}, bf16[64,2048]{1,0:T(8,128)(2,1)S(1)}, u32[]{:S(2)}, u32[]{:S(2)}) collective-permute-start(bf16[64,2048]{1,0:T(8,128)(2,1)S(1)} %get-tuple-element.446), channel_id=1, source_target_pairs={{0,16},{16,32},{32,48},{48,0},{1,17},{17,33},{33,49},{49,1},{2,18}... | collective-permute-start | bytes 786440 | tf_op jit(solution)/shard_map/ppermute | solution.py:529
  189.9 14.7 %collective-permute-start.25 = (bf16[64,2048]{1,0:T(8,128)(2,1)S(1)}, bf16[64,2048]{1,0:T(8,128)(2,1)S(1)}, u32[]{:S(2)}, u32[]{:S(2)}) collective-permute-start(bf16[64,2048]{1,0:T(8,128)(2,1)S(1)} %get-tuple-element.430), channel_id=1, source_target_pairs={{0,4},{4,8},{8,12},{12,0},{1,5},{5,9},{9,13},{13,1},{2,6},{6,10},{... | collective-permute-start | bytes 786440 | tf_op jit(solution)/shard_map/ppermute | solution.py:529
  201.3 11.2 %collective-permute-start.35 = (bf16[144,2048]{1,0:T(8,128)(2,1)S(1)}, bf16[144,2048]{1,0:T(8,128)(2,1)S(1)}, u32[]{:S(2)}, u32[]{:S(2)}) collective-permute-start(bf16[144,2048]{1,0:T(8,128)(2,1)S(1)} %get-tuple-element.448), channel_id=1, source_target_pairs={{0,16},{16,32},{32,48},{48,0},{1,17},{17,33},{33,49},{49,1},{2,18}... | collective-permute-start | bytes 1769480 | tf_op jit(solution)/shard_map/ppermute | solution.py:529
  201.4 11.1 %collective-permute-start.36 = (bf16[144,2048]{1,0:T(8,128)(2,1)S(1)}, bf16[144,2048]{1,0:T(8,128)(2,1)S(1)}, u32[]{:S(2)}, u32[]{:S(2)}) collective-permute-start(bf16[144,2048]{1,0:T(8,128)(2,1)S(1)} %get-tuple-element.449), channel_id=1, source_target_pairs={{0,48},{16,0},{32,16},{48,32},{1,49},{17,1},{33,17},{49,33},{2,50}... | collective-permute-start | bytes 1769480 | tf_op jit(solution)/shard_map/ppermute | solution.py:529
  205.7 11.2 %collective-permute-start.27 = (bf16[144,2048]{1,0:T(8,128)(2,1)S(1)}, bf16[144,2048]{1,0:T(8,128)(2,1)S(1)}, u32[]{:S(2)}, u32[]{:S(2)}) collective-permute-start(bf16[144,2048]{1,0:T(8,128)(2,1)S(1)} %get-tuple-element.432), channel_id=1, source_target_pairs={{0,4},{4,8},{8,12},{12,0},{1,5},{5,9},{9,13},{13,1},{2,6},{6,10},{... | collective-permute-start | bytes 1769480 | tf_op jit(solution)/shard_map/ppermute | solution.py:529
  205.7 11.1 %collective-permute-start.28 = (bf16[144,2048]{1,0:T(8,128)(2,1)S(1)}, bf16[144,2048]{1,0:T(8,128)(2,1)S(1)}, u32[]{:S(2)}, u32[]{:S(2)}) collective-permute-start(bf16[144,2048]{1,0:T(8,128)(2,1)S(1)} %get-tuple-element.433), channel_id=1, source_target_pairs={{0,12},{4,0},{8,4},{12,8},{1,13},{5,1},{9,5},{13,9},{2,14},{6,2},{... | collective-permute-start | bytes 1769480 | tf_op jit(solution)/shard_map/ppermute | solution.py:529
  (16 other events, 88.6 us)
